TPU v7x, 128 devices: a whole 4x4x4 slice. The times are simulated.
128 devices in a mesh: rep: 16 (over x, z), grp: 8 (over y, core).
Axes of the slice: x: 4, y: 4, z: 4, core: 2. Of those that a mesh axis runs over, the one named last changes fastest.
Arguments:
- inputs: bfloat16 [2, 262144, 1152], P(None, ('rep', 'grp')), may hold values from -6 to 6
- out_grads: bfloat16 [2, 262144, 1152], P(None, ('rep', 'grp')), may hold values from -6 to 6
- weights: bfloat16 [2, 1152, 1152], P(None, 'grp'), may hold values from -3 to 3
- biases: bfloat16 [2, 1152], P(None, 'grp'), may hold values from -3 to 3
- errors: float32 [16, 2, 1152, 1152], P('rep', None, 'grp'), may hold values from -6 to 6
- momenta: float32 [2, 1152, 1152], P(None, 'grp'), may hold values from -3 to 3
- bias_momenta: float32 [2, 1152], P(None, 'grp'), may hold values from -3 to 3
- q_start: float32 [2, 1152, 32], replicated, may hold values from -6 to 6
Outputs:
- new_weights: bfloat16 [2, 1152, 1152], replicated
- new_biases: bfloat16 [2, 1152], replicated
- new_errors: float32 [16, 2, 1152, 1152], P('rep', None, 'grp')
- new_momenta: float32 [2, 1152, 1152], P(None, 'grp')
- new_bias_momenta: float32 [2, 1152], P(None, 'grp')
All inputs are finite; a program needn't handle non-finite values.
Results may differ from a plain program's by a relative error of at most 0.0045.
Values may be sent and summed in bfloat16 or wider, within the bound.
No kernel may reach another device: no remote copies, remote signals or barrier semaphores. Data moves between devices by JAX's collectives and lax.ppermute only.
A program may use at most 256 MiB of HBM per device.

v0:
```python
import jax
import jax.numpy as jnp
from jax import lax
from jax.experimental import pallas as pl
from jax.experimental.pallas import tpu as pltpu
from jax.sharding import Mesh
from jax.sharding import PartitionSpec as P


NS_STEPS = 5
HIGH = lax.Precision.HIGHEST
BF = jnp.bfloat16
F32 = jnp.float32


def ring(count, step):
    return [(i, (i + step) % count) for i in range(count)]


def pick(stack, index, axis=0):
    return lax.dynamic_index_in_dim(stack, index, axis, keepdims=False)


def hi_lo(row):
    high = row.astype(BF)
    low = (row - high.astype(F32)).astype(BF)
    return jnp.concatenate([high[None], low[None], jnp.zeros((6, row.shape[0]), BF)], 0)


def from_hi_lo(rows):
    return rows[0].astype(F32) + rows[1].astype(F32)


def paired(parts):
    return (parts[0] + parts[1]) + (parts[2] + parts[3])


def split3(value):
    one = value.astype(BF)
    rest = value - one.astype(F32)
    two = rest.astype(BF)
    three = (rest - two.astype(F32)).astype(BF)
    return jnp.concatenate([one, two, three], 0)


def by_three(left, right, dims):
    rank = left.shape[0]
    out = lax.dot_general(split3(left), right, dims, preferred_element_type=F32)
    return out[:rank] + out[rank : 2 * rank] + out[2 * rank :]


def exact(left, right, dims):
    return lax.dot_general(left, right, dims, precision=HIGH, preferred_element_type=F32)


NN = (((1,), (0,)), ((), ()))
NT = (((1,), (1,)), ((), ()))
TN = (((0,), (0,)), ((), ()))


def inverse_root(gram):
    fro = jnp.sqrt(jnp.sum(gram * gram, axis=(0, 1), keepdims=True)) + 1e-06
    rank = gram.shape[0]
    spot = lambda axis: lax.broadcasted_iota(jnp.int32, (rank, rank), axis)
    eye = jnp.where(spot(0) == spot(1), 1.0, 0.0).astype(F32)

    def step(pair):
        ymat, zmat = pair
        tmat = 1.5 * eye - 0.5 * exact(zmat, ymat, NN)
        return exact(ymat, tmat, NN), exact(tmat, zmat, NN)

    pair = (gram / fro, eye)
    for _ in range(NS_STEPS):
        pair = step(pair)
    zmat = pair[1]
    return zmat, jnp.sqrt(fro)


def half_round(q, rows_of_sum):
    p = by_three(q, rows_of_sum, NT)
    return p, exact(p, p, NT), by_three(p, rows_of_sum, NN)


def store_split(ref, at, value):
    rank, wide = value.shape
    high = value.astype(BF)
    ref[:rank, at : at + wide] = high
    ref[:rank, at + wide : at + 2 * wide] = (value - high.astype(F32)).astype(BF)


def widened(gram):
    rank = gram.shape[0]
    return jnp.concatenate([gram, jnp.zeros((rank, 128 - rank), F32)], 1)


def first_kernel(xpos_ref, *refs):
    parts, (q_ref, bias_ref, sum_ref, out_ref) = refs[:4], refs[4:]
    rank, width = q_ref.shape
    piece = parts[0].shape[0]
    xpos = xpos_ref[0]
    for j in range(4):
        value = parts[j][...]
        for spot in (1, 2, 3):
            value = jnp.where(xpos == spot, parts[spot ^ j][...], value)
        sum_ref[j * piece : (j + 1) * piece] = value
    rest = sum_ref.shape[0] - 4 * piece
    sum_ref[4 * piece :] = jnp.zeros((rest, width), BF)
    _, gram, u = half_round(q_ref[...], sum_ref[...])
    out_ref[:rank, :width] = u.astype(BF)
    store_split(out_ref, width, widened(gram))
    bias = bias_ref[...]
    high = bias.astype(BF).astype(F32)
    both = jnp.concatenate([high, bias - high, jnp.zeros((6, width), F32)], 0)
    both = jnp.concatenate([both, jnp.zeros((8, 256), F32)], 1)
    out_ref[rank:] = both.astype(BF)


def summed_parts(parts, columns):
    load = lambda ref: ref[:, :columns].astype(F32)
    return (load(parts[0]) + load(parts[1])) + (load(parts[2]) + load(parts[3]))


def second_kernel(*refs):
    parts, (far_ref, out_ref, bias_ref, sum_ref, arrived) = refs[:4], refs[4:]
    fetch = pltpu.make_async_copy(far_ref, sum_ref, arrived)
    fetch.start()
    width = sum_ref.shape[1]
    rank = out_ref.shape[0]
    total = summed_parts(parts, width + 256)
    gram = total[:rank, width : width + 128] + total[:rank, width + 128 :]
    zmat, root = inverse_root(gram[:, :rank])
    q = exact(zmat, total[:rank, :width], TN) / root
    bias = total[rank : rank + 1, :width] + total[rank + 1 : rank + 2, :width]
    bias_ref[...] = jnp.concatenate([bias, jnp.zeros((7, width), F32)], 0)
    fetch.wait()
    p, gram, u = half_round(q, sum_ref[...])
    out_ref[:, :width] = u.astype(BF)
    store_split(out_ref, width, widened(gram))
    store_split(out_ref, width + 256, p)


def third_kernel(*refs):
    parts, (q_ref, z_ref) = refs[:4], refs[4:]
    rank, width = q_ref.shape
    total = summed_parts(parts, width + 256)
    gram = total[:, width : width + 128] + total[:, width + 128 :]
    zmat, root = inverse_root(gram[:, :rank])
    q_ref[...] = exact(zmat, total[:, :width], TN) / root
    z_ref[...] = zmat / root


def lineup_kernel(ypos_ref, *refs):
    parts, out_ref = refs[:4], refs[4]
    for spot in range(4):

        @pl.when(ypos_ref[0] == spot)
        def _():
            def move(i, carry):
                at = pl.ds(pl.multiple_of(8 * i, 8), 8)
                for j in range(4):
                    for layer in range(out_ref.shape[1]):
                        out_ref[j, layer, at] = parts[spot ^ j][layer, at]
                return carry

            lax.fori_loop(0, out_ref.shape[2] // 8, move, 0)


def assemble_kernel(core_ref, mine_ref, theirs_ref, out_ref):
    rows = out_ref.shape[1] // 2
    for spot in range(2):

        @pl.when(core_ref[0] == spot)
        def _():
            for side in range(2):
                ref = mine_ref if side == spot else theirs_ref
                out_ref[:, side * rows : (side + 1) * rows] = ref[0, :, :rows]


def assemble(core, mine, theirs, rows):
    ys, layers, held, width = mine.shape
    block = pl.BlockSpec((1, layers, held, width), lambda j, core: (j, 0, 0, 0))
    return pl.pallas_call(
        assemble_kernel,
        out_shape=jax.ShapeDtypeStruct((layers, width, width), BF),
        grid_spec=pltpu.PrefetchScalarGridSpec(
            num_scalar_prefetch=1,
            grid=(ys,),
            in_specs=[block, block],
            out_specs=pl.BlockSpec((layers, 2 * rows, width), lambda j, core: (0, j, 0)),
        ),
        name="assemble",
    )(core, mine, theirs)


def in_vmem(kernel, outs, scalars=0, far=0, scratch=()):
    vmem = pl.BlockSpec(memory_space=pltpu.VMEM)
    smem = pl.BlockSpec(memory_space=pltpu.SMEM)

    def call(*args):
        return pl.pallas_call(
            kernel,
            out_shape=outs,
            in_specs=[smem] * scalars
            + [vmem] * (len(args) - scalars - far)
            + [pl.BlockSpec(memory_space=pl.ANY)] * far,
            scratch_shapes=list(scratch),
            out_specs=jax.tree.map(lambda _: vmem, outs),
            compiler_params=pltpu.CompilerParams(vmem_limit_bytes=24 << 20),
        )(*args)

    return call


def products(left, right):
    l1 = left.astype(BF)
    rest = left - l1.astype(F32)
    l2 = rest.astype(BF)
    l3 = (rest - l2.astype(F32)).astype(BF)
    r1 = right.astype(BF)
    rest = right - r1.astype(F32)
    r2 = rest.astype(BF)
    r3 = (rest - r2.astype(F32)).astype(BF)
    return (
        jnp.concatenate([l1, l1, l2, l1, l2, l3], -2),
        jnp.concatenate([r1, r2, r1, r3, r2, r1], -2),
    )


def body(inputs, out_grads, weights, biases, errors, momenta, bias_momenta, q_start):
    layers, tok, width = inputs.shape
    cores = lax.axis_size("core")
    ys = lax.axis_size("y")
    xs = lax.axis_size("x")
    reps = xs * lax.axis_size("z")
    rows = width // (cores * ys)
    rank = q_start.shape[-1]
    scale = float(tok) ** (-0.5)
    core, ypos, xpos = lax.axis_index("core"), lax.axis_index("y"), lax.axis_index("x")

    def swap(value):
        return lax.ppermute(value, "core", ring(cores, 1))

    def trade(value, axis, k):
        return lax.ppermute(value, axis, [(i, i ^ k) for i in range(4)])

    def everyone(value, axis):
        return [value] + [trade(value, axis, k) for k in (1, 2, 3)]

    def natural(parts, position):
        ordered = []
        for j in range(4):
            value = parts[j]
            for spot in (1, 2, 3):
                value = jnp.where(position == spot, parts[spot ^ j], value)
            ordered.append(value)
        return ordered

    old_m = lax.optimization_barrier(momenta)
    old = (weights.astype(F32) - 0.45 * old_m).astype(BF)
    row_b, row_m = lax.optimization_barrier((biases, bias_momenta))
    two = jnp.stack([row_b, row_m.astype(BF)], 1)
    old = jnp.concatenate([old, jnp.pad(two, ((0, 0), (0, 6), (0, width - rows)))], 1)
    parts = [old]
    for k in (1, 2, 3):
        parts.append(trade(old, "y", k))
    held = rows + 8
    mine = in_vmem(
        lineup_kernel, jax.ShapeDtypeStruct((ys, layers, held, width), BF), 1
    )(ypos.astype(jnp.int32)[None], *parts)
    theirs = swap(mine)
    old = assemble(core.astype(jnp.int32)[None], mine, theirs, rows)
    tails = [stack[:, :, rows : rows + 2, :rows].astype(F32) for stack in (mine, theirs)]
    tails = [tail[:, :, 0] - 0.45 * tail[:, :, 1] for tail in tails]
    even, odd = jnp.where(core == 0, *tails), jnp.where(core == 0, *tails[::-1])
    old_b = jnp.stack([even, odd], 1).transpose(2, 0, 1, 3).reshape(layers, width)

    def chip_blocks(layer, after=None):
        x, y = inputs, out_grads
        if after is not None:
            x, y, _ = lax.optimization_barrier((x, y, after))
        part = jnp.einsum("tr,te->re", x[layer], y[layer], preferred_element_type=F32).astype(BF)
        part = lax.optimization_barrier(part).reshape(ys * cores, rows, width)
        got = swap(
            pick(part.reshape(ys, cores, rows, width), 1 - core, 1)
        )
        blocks = []
        for k in range(4):
            there = ypos ^ k
            blocks.append(pick(part, there * cores + core).astype(F32) + pick(got, there).astype(F32))
        return blocks[0], [b.astype(BF) for b in blocks[1:]]

    def merge(layer, own, blocks):
        for k in (1, 2, 3):
            block = trade(blocks[k - 1], "y", k)
            own = own + block.astype(F32)
        return own * scale + errors[0, layer]

    own0, blocks0 = chip_blocks(0)
    own1, blocks1 = chip_blocks(1, blocks0)
    merged0 = lax.optimization_barrier(merge(0, own0, blocks0))
    merged = jnp.stack([merged0, merge(1, own1, blocks1)])
    col_sums = jnp.sum(out_grads, axis=1, dtype=F32)

    got = swap(
        jnp.concatenate([pick(merged, 1 - core).astype(BF), hi_lo(pick(col_sums, 1 - core))], 0)
    )
    own, got_rows = pick(merged, core), got[:rows].astype(F32)
    both = jnp.stack([jnp.where(core == 0, own, got_rows), jnp.where(core == 0, got_rows, own)])
    both = both.reshape(4, rows // 2, width)
    bias = pick(col_sums, core) + from_hi_lo(got[rows:])
    bias_rows = hi_lo(bias)
    half = rows // 2

    def loaded(main):
        return jnp.concatenate([main.astype(BF), bias_rows], 0)

    parts = []
    for k in (1, 2, 3):
        block = loaded(pick(both, xpos ^ k))
        parts.append(trade(block, "x", k))
    main = paired([pick(both, xpos)] + [p[:half].astype(F32) for p in parts])
    bias = paired([from_hi_lo(p) for p in [bias_rows] + [p[half:] for p in parts]])
    bias_rows = hi_lo(bias)
    parts = everyone(loaded(main), "z")
    main = paired([p[:half].astype(F32) for p in parts]).astype(BF)
    bias = paired([from_hi_lo(p[half:]) for p in parts])
    parts = everyone(main, "x")
    shape = lambda *dims, of: jax.ShapeDtypeStruct(dims, of)
    q = pick(q_start, core).T
    total, packed = in_vmem(
        first_kernel, (shape(384, width, of=BF), shape(rank + 8, width + 256, of=BF)), 1
    )(xpos.astype(jnp.int32)[None], *parts, q, bias[None])
    parts = everyone(packed, "y")
    packed, bias_rows = in_vmem(
        second_kernel,
        (shape(rank, width + 1024, of=BF), shape(8, width, of=F32)),
        far=1,
        scratch=(pltpu.VMEM((384, width), BF), pltpu.SemaphoreType.DMA),
    )(*parts, total)
    parts = everyone(packed, "y")
    other = swap(bias_rows)
    bias = jnp.stack([jnp.where(core == l, bias_rows[0], other[0]) for l in range(layers)])
    bias_grad = bias * (scale / reps)
    grp = ypos * cores + core
    bias_own = lax.dynamic_slice_in_dim(bias_grad, grp * rows, rows, 1)
    new_bias_momenta = 0.9 * bias_momenta + bias_own
    new_biases = (old_b - 0.5 * bias_grad).astype(BF)
    q, zmat = in_vmem(third_kernel, (shape(rank, width, of=F32), shape(rank, rank, of=F32)))(*parts)
    at = width + 256
    p_all = [
        part[:, at : at + 2 * rows].astype(F32) + part[:, at + 384 : at + 384 + 2 * rows].astype(F32)
        for part in parts
    ]
    p_all = jnp.concatenate(natural(p_all, ypos), 1)
    phat = exact(zmat, p_all, TN)

    packed = jnp.concatenate([q, phat], 1)
    other = swap(packed)
    pair = [jnp.where(core == layer, packed, other) for layer in range(layers)]
    q = jnp.stack([p[:, :width] for p in pair])
    phat = jnp.stack([p[:, width:] for p in pair])
    left, right = products(phat, q)
    own = lax.dynamic_slice_in_dim(left, grp * rows, rows, 2)
    spec = "lkr,lke->lre"
    approx = jnp.einsum(spec, own, right, preferred_element_type=F32) * (1.0 / reps)
    new_errors = merged - approx
    new_momenta = 0.9 * momenta + approx
    whole = jnp.einsum(spec, left, right, preferred_element_type=F32) * (1.0 / reps)
    new_weights = (old.astype(F32) - 0.5 * whole).astype(BF)

    return (new_weights, new_biases, new_errors[None], new_momenta, new_bias_momenta)


def solution(mesh):
    split = Mesh(mesh.devices.reshape(4, 4, 4, 2), ("x", "z", "y", "core"))
    rep, grp = ("x", "z"), ("y", "core")
    placed = (
        P(None, rep + grp, None),
        P(None, rep + grp, None),
        P(None, grp, None),
        P(None, grp),
        P(rep, None, grp, None),
        P(None, grp, None),
        P(None, grp),
        P(),
    )

    return jax.shard_map(
        body,
        mesh=split,
        in_specs=placed,
        out_specs=(P(), P(), P(rep, None, grp, None), P(None, grp, None), P(None, grp)),
        check_vma=False,
    )
```

profile of v0, /device:TPU:1, one launch (start us, length us, event | category | flops | bytes accessed | tf_op | source)
XLA Modules:
  0.0 194.8 jit_solution(8960728616716444060)
XLA Ops:
  0.7 10.2 %convolution_convert_fusion.1 = bf16[1152,1152]{1,0:T(8,128)(2,1)S(1)} fusion(bf16[2,2048,1152]{2,1,0:T(8,128)(2,1)} %param.9, bf16[2,2048,1152]{2,1,0:T(8,128)(2,1)} %param.8), kind=kOutput, calls=%fused_computation.4 | convolution fusion | flops 5437145088 | bytes 12091392 | tf_op jit(solution)/shard_map/tr,te->re/dot_general | solution.py:281
  10.9 1.3 dynamic-slice_bitcast_fusion.1
  12.1 1.4 collective-permute-start.4
  13.6 2.9 %collective-permute-done.4 = bf16[4,144,1152]{2,1,0:T(8,128)(2,1)} collective-permute-done((bf16[4,144,1152]{2,1,0:T(8,128)(2,1)}, bf16[4,144,1152]{2,1,0:T(8,128)(2,1)}, u32[]{:S(2)}, u32[]{:S(2)}) %collective-permute-start.4) | collective-permute-done | bytes 1327136 | tf_op jit(solution)/shard_map/ppermute | solution.py:241
  16.5 2.3 %fusion.25 = (bf16[144,1152]{1,0:T(8,128)(2,1)}, bf16[144,1152]{1,0:T(8,128)(2,1)}, bf16[144,1152]{1,0:T(8,128)(2,1)}) fusion(bf16[4,144,1152]{2,1,0:T(8,128)(2,1)} %collective-permute-done.4, s32[]{:T(128)S(6)} %select_n.206, bf16[8,144,1152]{2,1,0:T(8,128)(2,1)S(1)} %bitcast.131, s32[]{:T(128)S(6)} %select_n.205, s32[]{:T(128)S(6)} %select_n.204, ...), kind=kLoop, calls=%fused_computation.59 | loop fusion | flops 1990656 | bytes 2986008 | tf_op jit(solution)/shard_map/convert_element_type | solution.py:290
  18.9 10.3 %convolution_convert_fusion = bf16[1152,1152]{1,0:T(8,128)(2,1)S(1)} fusion(bf16[2,2048,1152]{2,1,0:T(8,128)(2,1)} %param.9, bf16[2,2048,1152]{2,1,0:T(8,128)(2,1)} %param.8), kind=kOutput, calls=%fused_computation.3 | convolution fusion | flops 5437145088 | bytes 12091392 | tf_op jit(solution)/shard_map/tr,te->re/dot_general | solution.py:281
  29.7 1.7 copy-done.16
  31.8 1.3 convert_reduce_fusion
  33.1 1.5 collective-permute-start.5
  34.6 2.7 %collective-permute-start.6 = (bf16[144,1152]{1,0:T(8,128)(2,1)S(1)}, bf16[144,1152]{1,0:T(8,128)(2,1)}, u32[]{:S(2)}, u32[]{:S(2)}) collective-permute-start(bf16[144,1152]{1,0:T(8,128)(2,1)S(1)} %copy-done.24), channel_id=1, source_target_pairs={{0,4},{2,6},{4,0},{6,2},{1,5},{3,7},{5,1},{7,3},{8,12},{10,14},{12... | collective-permute-start | bytes 995336 | tf_op jit(solution)/shard_map/ppermute | solution.py:244
  37.4 1.2 fusion.26
  38.6 1.7 collective-permute-start.10
  42.2 1.5 collective-permute-start.9
  43.8 8.2 %collective-permute-done.6 = bf16[144,1152]{1,0:T(8,128)(2,1)} collective-permute-done((bf16[144,1152]{1,0:T(8,128)(2,1)S(1)}, bf16[144,1152]{1,0:T(8,128)(2,1)}, u32[]{:S(2)}, u32[]{:S(2)}) %collective-permute-start.6) | collective-permute-done | bytes 331808 | tf_op jit(solution)/shard_map/ppermute | solution.py:244
  52.0 9.3 %collective-permute-done.7 = bf16[144,1152]{1,0:T(8,128)(2,1)} collective-permute-done((bf16[144,1152]{1,0:T(8,128)(2,1)S(1)}, bf16[144,1152]{1,0:T(8,128)(2,1)}, u32[]{:S(2)}, u32[]{:S(2)}) %collective-permute-start.7) | collective-permute-done | bytes 331808 | tf_op jit(solution)/shard_map/ppermute | solution.py:244
  61.7 6.7 %collective-permute-done.11 = bf16[144,1152]{1,0:T(8,128)(2,1)} collective-permute-done((bf16[144,1152]{1,0:T(8,128)(2,1)}, bf16[144,1152]{1,0:T(8,128)(2,1)}, u32[]{:S(2)}, u32[]{:S(2)}) %collective-permute-start.11) | collective-permute-done | bytes 331808 | tf_op jit(solution)/shard_map/ppermute | solution.py:244
  68.4 2.6 %bitcast_add_fusion.2 = (f32[144,1152]{1,0:T(8,128)S(1)}, f32[1,144,1152]{2,1,0:T(8,128)S(1)}) fusion(f32[1,2,144,1152]{3,2,1,0:T(8,128)} %param.12, bf16[144,1152]{1,0:T(8,128)(2,1)} %collective-permute-done.7, bf16[144,1152]{1,0:T(8,128)(2,1)} %collective-permute-done.6, bf16[144,1152]{1,0:T(8,128)(2,1)S(1)} %collective-permute-done.5, ...), kind=kLoop, calls=%fused_computation.41 | loop fusion | flops 3649536 | bytes 5971976 | tf_op jit(solution)/shard_map/add | solution.py:296
  72.2 3.2 %collective-permute-start.12 = (bf16[152,1152]{1,0:T(8,128)(2,1)S(1)}, bf16[152,1152]{1,0:T(8,128)(2,1)}, u32[]{:S(2)}, u32[]{:S(2)}) collective-permute-start(bf16[152,1152]{1,0:T(8,128)(2,1)S(1)} %pad_maximum_fusion.7), channel_id=1, source_target_pairs={{0,1},{1,0},{2,3},{3,2},{4,5},{5,4},{6,7},{7,6},{8,9},{9,8},{10,11... | collective-permute-start | bytes 1050632 | tf_op jit(solution)/shard_map/ppermute | solution.py:241
  75.4 3.2 %collective-permute-done.refs_1_ = bf16[2,152,1152]{2,1,0:T(8,128)(2,1)S(1)} collective-permute-done((bf16[2,152,1152]{2,1,0:T(8,128)(2,1)S(1)}, bf16[2,152,1152]{2,1,0:T(8,128)(2,1)S(1)}, u32[]{:S(2)}, u32[]{:S(2)}) %collective-permute-start) | collective-permute-done | bytes 700448 | tf_op jit(solution)/shard_map/ppermute | solution.py:244
  79.4 16.8 %collective-permute-done.1.refs_2_ = bf16[2,152,1152]{2,1,0:T(8,128)(2,1)S(1)} collective-permute-done((bf16[2,152,1152]{2,1,0:T(8,128)(2,1)S(1)}, bf16[2,152,1152]{2,1,0:T(8,128)(2,1)S(1)}, u32[]{:S(2)}, u32[]{:S(2)}) %collective-permute-start.1) | collective-permute-done | bytes 700448 | tf_op jit(solution)/shard_map/ppermute | solution.py:244
  97.0 1.3 collective-permute-done.2.refs_3_
  103.9 1.9 collective-permute-start.3
  108.0 1.3 collective-permute-start.13
  109.3 2.4 %collective-permute-start.14 = (bf16[80,1152]{1,0:T(8,128)(2,1)S(1)}, bf16[80,1152]{1,0:T(8,128)(2,1)S(1)}, u32[]{:S(2)}, u32[]{:S(2)}) collective-permute-start(bf16[80,1152]{1,0:T(8,128)(2,1)S(1)} %get-tuple-element.59), channel_id=1, source_target_pairs={{0,64},{32,96},{64,0},{96,32},{1,65},{33,97},{65,1},{97,33},{2,66}... | collective-permute-start | bytes 552968 | tf_op jit(solution)/shard_map/ppermute | solution.py:244
  112.0 2.1 %collective-permute-done.13 = bf16[80,1152]{1,0:T(8,128)(2,1)S(1)} collective-permute-done((bf16[80,1152]{1,0:T(8,128)(2,1)S(1)}, bf16[80,1152]{1,0:T(8,128)(2,1)S(1)}, u32[]{:S(2)}, u32[]{:S(2)}) %collective-permute-start.13) | collective-permute-done | bytes 184352 | tf_op jit(solution)/shard_map/ppermute | solution.py:244
  114.0 6.2 %collective-permute-done.14 = bf16[80,1152]{1,0:T(8,128)(2,1)S(1)} collective-permute-done((bf16[80,1152]{1,0:T(8,128)(2,1)S(1)}, bf16[80,1152]{1,0:T(8,128)(2,1)S(1)}, u32[]{:S(2)}, u32[]{:S(2)}) %collective-permute-start.14) | collective-permute-done | bytes 184352 | tf_op jit(solution)/shard_map/ppermute | solution.py:244
  120.2 2.4 %collective-permute-done.15 = bf16[80,1152]{1,0:T(8,128)(2,1)S(1)} collective-permute-done((bf16[80,1152]{1,0:T(8,128)(2,1)S(1)}, bf16[80,1152]{1,0:T(8,128)(2,1)S(1)}, u32[]{:S(2)}, u32[]{:S(2)}) %collective-permute-start.15) | collective-permute-done | bytes 184352 | tf_op jit(solution)/shard_map/ppermute | solution.py:244
  122.8 1.7 collective-permute-start.16
  124.6 3.3 %collective-permute-start.17 = (bf16[80,1152]{1,0:T(8,128)(2,1)S(1)}, bf16[80,1152]{1,0:T(8,128)(2,1)S(1)}, u32[]{:S(2)}, u32[]{:S(2)}) collective-permute-start(bf16[80,1152]{1,0:T(8,128)(2,1)S(1)} %pad_maximum_fusion.3), channel_id=1, source_target_pairs={{0,16},{8,24},{16,0},{24,8},{1,17},{9,25},{17,1},{25,9},{2,18},{10... | collective-permute-start | bytes 552968 | tf_op jit(solution)/shard_map/ppermute | solution.py:244
  128.2 7.1 %collective-permute-done.17 = bf16[80,1152]{1,0:T(8,128)(2,1)S(1)} collective-permute-done((bf16[80,1152]{1,0:T(8,128)(2,1)S(1)}, bf16[80,1152]{1,0:T(8,128)(2,1)S(1)}, u32[]{:S(2)}, u32[]{:S(2)}) %collective-permute-start.17) | collective-permute-done | bytes 184352 | tf_op jit(solution)/shard_map/ppermute | solution.py:244
  135.2 3.0 %collective-permute-done.18 = bf16[80,1152]{1,0:T(8,128)(2,1)S(1)} collective-permute-done((bf16[80,1152]{1,0:T(8,128)(2,1)S(1)}, bf16[80,1152]{1,0:T(8,128)(2,1)S(1)}, u32[]{:S(2)}, u32[]{:S(2)}) %collective-permute-start.18) | collective-permute-done | bytes 184352 | tf_op jit(solution)/shard_map/ppermute | solution.py:244
  138.5 1.4 collective-permute-start.20
  139.8 2.5 %collective-permute-start.21 = (bf16[72,1152]{1,0:T(8,128)(2,1)S(1)}, bf16[72,1152]{1,0:T(8,128)(2,1)S(1)}, u32[]{:S(2)}, u32[]{:S(2)}) collective-permute-start(bf16[72,1152]{1,0:T(8,128)(2,1)S(1)} %add_convert_fusion.6.refs_0_), channel_id=1, source_target_pairs={{0,96},{32,64},{64,32},{96,0},{1,97},{33,65},{65,33},{97,1},{2,98}... | collective-permute-start | bytes 497672 | tf_op jit(solution)/shard_map/ppermute | solution.py:244
  142.6 3.2 %collective-permute-done.20.refs_2_ = bf16[72,1152]{1,0:T(8,128)(2,1)S(1)} collective-permute-done((bf16[72,1152]{1,0:T(8,128)(2,1)S(1)}, bf16[72,1152]{1,0:T(8,128)(2,1)S(1)}, u32[]{:S(2)}, u32[]{:S(2)}) %collective-permute-start.20) | collective-permute-done | bytes 165920 | tf_op jit(solution)/shard_map/ppermute | solution.py:244
  145.9 3.0 %collective-permute-done.21.refs_3_ = bf16[72,1152]{1,0:T(8,128)(2,1)S(1)} collective-permute-done((bf16[72,1152]{1,0:T(8,128)(2,1)S(1)}, bf16[72,1152]{1,0:T(8,128)(2,1)S(1)}, u32[]{:S(2)}, u32[]{:S(2)}) %collective-permute-start.21) | collective-permute-done | bytes 165920 | tf_op jit(solution)/shard_map/ppermute | solution.py:244
  151.0 2.7 %collective-permute-start.24 = (bf16[40,1408]{1,0:T(8,128)(2,1)S(1)}, bf16[40,1408]{1,0:T(8,128)(2,1)S(1)}, u32[]{:S(2)}, u32[]{:S(2)}) collective-permute-start(bf16[40,1408]{1,0:T(8,128)(2,1)S(1)} %get-tuple-element.19.refs_0_), channel_id=1, source_target_pairs={{0,6},{2,4},{4,2},{6,0},{1,7},{3,5},{5,3},{7,1},{8,14},{10,12},{12... | collective-permute-start | bytes 337928 | tf_op jit(solution)/shard_map/ppermute | solution.py:244
  153.8 2.2 %collective-permute-done.23.refs_2_ = bf16[40,1408]{1,0:T(8,128)(2,1)S(1)} collective-permute-done((bf16[40,1408]{1,0:T(8,128)(2,1)S(1)}, bf16[40,1408]{1,0:T(8,128)(2,1)S(1)}, u32[]{:S(2)}, u32[]{:S(2)}) %collective-permute-start.23) | collective-permute-done | bytes 112672 | tf_op jit(solution)/shard_map/ppermute | solution.py:244
  156.0 2.2 %collective-permute-done.24.refs_3_ = bf16[40,1408]{1,0:T(8,128)(2,1)S(1)} collective-permute-done((bf16[40,1408]{1,0:T(8,128)(2,1)S(1)}, bf16[40,1408]{1,0:T(8,128)(2,1)S(1)}, u32[]{:S(2)}, u32[]{:S(2)}) %collective-permute-start.24) | collective-permute-done | bytes 112672 | tf_op jit(solution)/shard_map/ppermute | solution.py:244
  158.2 3.2 %shard_map.121 = (bf16[32,2176]{1,0:T(8,128)(2,1)S(1)}, f32[8,1152]{1,0:T(8,128)S(1)}) custom-call(bf16[40,1408]{1,0:T(8,128)(2,1)S(1)} %get-tuple-element.19.refs_0_, bf16[40,1408]{1,0:T(8,128)(2,1)S(1)} %collective-permute-done.22.refs_1_, bf16[40,1408]{1,0:T(8,128)(2,1)S(1)} %collective-permute-done.23.refs_2_, ...), custom_call_target="tpu_custom_call" | custom-call | tf_op jit(solution)/shard_map/pallas_call | solution.py:200
  161.4 1.5 collective-permute-start.29
  163.1 5.4 %assemble.1 = bf16[2,1152,1152]{2,1,0:T(8,128)(2,1)} custom-call(s32[1]{0:T(128)} %bitcast.core_ref, bf16[4,2,152,1152]{3,2,1,0:T(8,128)(2,1)} %copy-done.1, bf16[4,2,152,1152]{3,2,1,0:T(8,128)(2,1)} %copy-done.18), custom_call_target="tpu_custom_call" | custom-call | tf_op jit(solution)/shard_map/assemble/pallas_call | solution.py:182
  168.5 3.6 %collective-permute-start.26 = (bf16[32,2176]{1,0:T(8,128)(2,1)S(1)}, bf16[32,2176]{1,0:T(8,128)(2,1)S(1)}, u32[]{:S(2)}, u32[]{:S(2)}) collective-permute-start(bf16[32,2176]{1,0:T(8,128)(2,1)S(1)} %get-tuple-element.21.refs_0_), channel_id=1, source_target_pairs={{0,4},{2,6},{4,0},{6,2},{1,5},{3,7},{5,1},{7,3},{8,12},{10,14},{12... | collective-permute-start | bytes 417800 | tf_op jit(solution)/shard_map/ppermute | solution.py:244
  172.3 1.3 collective-permute-done.25.refs_1_
  173.6 5.1 %collective-permute-done.26.refs_2_ = bf16[32,2176]{1,0:T(8,128)(2,1)S(1)} collective-permute-done((bf16[32,2176]{1,0:T(8,128)(2,1)S(1)}, bf16[32,2176]{1,0:T(8,128)(2,1)S(1)}, u32[]{:S(2)}, u32[]{:S(2)}) %collective-permute-start.26) | collective-permute-done | bytes 139296 | tf_op jit(solution)/shard_map/ppermute | solution.py:244
  178.8 2.5 %collective-permute-done.27.refs_3_ = bf16[32,2176]{1,0:T(8,128)(2,1)S(1)} collective-permute-done((bf16[32,2176]{1,0:T(8,128)(2,1)S(1)}, bf16[32,2176]{1,0:T(8,128)(2,1)S(1)}, u32[]{:S(2)}, u32[]{:S(2)}) %collective-permute-start.27) | collective-permute-done | bytes 139296 | tf_op jit(solution)/shard_map/ppermute | solution.py:244
  181.5 2.1 %shard_map.122 = (f32[32,1152]{1,0:T(8,128)S(1)}, f32[32,32]{1,0:T(8,128)S(1)}) custom-call(bf16[32,2176]{1,0:T(8,128)(2,1)S(1)} %get-tuple-element.21.refs_0_, bf16[32,2176]{1,0:T(8,128)(2,1)S(1)} %collective-permute-done.25.refs_1_, bf16[32,2176]{1,0:T(8,128)(2,1)S(1)} %collective-permute-done.26.refs_2_, bf16[32,2176]{1,0:T(8,128)(2,1)S(1)} %collective-permute-done.27.refs_3_), custom_call_target="tpu_custom_call" | custom-call | tf_op jit(solution)/shard_map/pallas_call | solution.py:200
  188.4 2.2 %multiply_add_fusion = (f32[2,144,1152]{2,1,0:T(8,128)}, f32[1,2,144,1152]{3,2,1,0:T(8,128)}) fusion(f32[2,144,1152]{2,1,0:T(8,128)S(1)} %copy-done.17, f32[1,144,1152]{2,1,0:T(8,128)S(1)} %copy-done.15, f32[1,144,1152]{2,1,0:T(8,128)S(1)} %bitcast.125, bf16[2,192,1152]{2,1,0:T(8,128)(2,1)S(1)} %constant_dynamic-update-slice_fusion.5, ...), kind=kOutput, calls=%fused_computation.22 | convolution fusion | flops 129060864 | bytes 6389764 | tf_op jit(solution)/shard_map/lkr,lke->lre/dot_general | solution.py:365
  190.6 4.2 %subtract_convert_fusion = bf16[2,1152,1152]{2,1,0:T(8,128)(2,1)} fusion(bf16[2,1152,1152]{2,1,0:T(8,128)(2,1)S(1)} %bitcast.122, bf16[2,192,1152]{2,1,0:T(8,128)(2,1)S(1)} %fusion.40, bf16[2,192,1152]{2,1,0:T(8,128)(2,1)S(1)} %constant_dynamic-update-slice_fusion.5), kind=kOutput, calls=%fused_computation.2 | convolution fusion | flops 1029832704 | bytes 12386304 | tf_op jit(solution)/shard_map/lkr,lke->lre/dot_general | solution.py:368
  (147 shorter events, 22.5 us)
Async XLA Ops:
  0.6 74.8 %copy-start = (f32[2,1152,32]{1,2,0:T(8,128)S(1)}, f32[2,1152,32]{1,2,0:T(8,128)}, u32[]{:S(2)}) copy-start(f32[2,1152,32]{1,2,0:T(8,128)} %param.15) | copy-start | bytes 884740
  10.8 8.0 %copy-start.19 = (bf16[1152,1152]{1,0:T(8,128)(2,1)}, bf16[1152,1152]{1,0:T(8,128)(2,1)S(1)}, u32[]{:S(2)}) copy-start(bf16[1152,1152]{1,0:T(8,128)(2,1)S(1)} %convolution_convert_fusion.1) | copy-start | bytes 7962628
  10.8 2.7 %copy-start.26 = (f32[2,144]{1,0:T(2,128)S(1)}, f32[2,144]{1,0:T(2,128)}, u32[]{:S(2)}) copy-start(f32[2,144]{1,0:T(2,128)} %param.14) | copy-start | bytes 3460
  10.8 2.7 %copy-start.27 = (bf16[2,144]{1,0:T(2,128)(2,1)S(1)}, bf16[2,144]{1,0:T(2,128)(2,1)}, u32[]{:S(2)}) copy-start(bf16[2,144]{1,0:T(2,128)(2,1)} %param.11) | copy-start | bytes 1732
  12.1 4.4 %collective-permute-start.4 = (bf16[4,144,1152]{2,1,0:T(8,128)(2,1)}, bf16[4,144,1152]{2,1,0:T(8,128)(2,1)}, u32[]{:S(2)}, u32[]{:S(2)}) collective-permute-start(bf16[4,144,1152]{2,1,0:T(8,128)(2,1)} %dynamic-slice_bitcast_fusion.1), channel_id=1, source_target_pairs={{0,1},{1,0},{2,3},{3,2},{4,5},{5,4},{6,7},{7,6},{8,9},{9,8},{10,11... | collective-permute-start | bytes 3981320 | tf_op jit(solution)/shard_map/ppermute | solution.py:241
  18.8 12.9 %slice-start.2 = ((s8[9437184]{0:T(1024)(128)(4,1)}), s8[4194304]{0:T(1024)(128)(4,1)S(1)}, s32[]{:S(2)}) async-start(s8[9437184]{0:T(1024)(128)(4,1)} %bitcast.126), calls=%async_computation.2 | async-start | bytes 8388608
  18.8 12.9 %slice-start.3 = ((s8[9437184]{0:T(1024)(128)(4,1)}), s8[4194304]{0:T(1024)(128)(4,1)S(1)}, s32[]{:S(2)}) async-start(s8[9437184]{0:T(1024)(128)(4,1)} %bitcast.126), calls=%async_computation.3 | async-start | bytes 8388608
  18.8 12.9 %slice-start.4 = ((s8[9437184]{0:T(1024)(128)(4,1)}), s8[1048576]{0:T(1024)(128)(4,1)S(1)}, s32[]{:S(2)}) async-start(s8[9437184]{0:T(1024)(128)(4,1)} %bitcast.126), calls=%async_computation.4 | async-start | bytes 2097152
  29.1 8.2 %copy-start.20 = (bf16[1152,1152]{1,0:T(8,128)(2,1)}, bf16[1152,1152]{1,0:T(8,128)(2,1)S(1)}, u32[]{:S(2)}) copy-start(bf16[1152,1152]{1,0:T(8,128)(2,1)S(1)} %convolution_convert_fusion) | copy-start | bytes 7962628
  29.1 2.4 %copy-start.22 = (bf16[2,144,1152]{2,1,0:T(8,128)(2,1)S(1)}, bf16[2,144,1152]{2,1,0:T(8,128)(2,1)}, u32[]{:S(2)}) copy-start(bf16[2,144,1152]{2,1,0:T(8,128)(2,1)} %param.10) | copy-start | bytes 1990660
  29.3 8.1 %collective-permute-start.8 = (bf16[4,144,1152]{2,1,0:T(8,128)(2,1)S(1)}, bf16[4,144,1152]{2,1,0:T(8,128)(2,1)S(1)}, u32[]{:S(2)}, u32[]{:S(2)}) collective-permute-start(bf16[4,144,1152]{2,1,0:T(8,128)(2,1)S(1)} %dynamic-slice_bitcast_fusion), channel_id=1, source_target_pairs={{0,1},{1,0},{2,3},{3,2},{4,5},{5,4},{6,7},{7,6},{8,9},{9,8},{10,11... | collective-permute-start | bytes 3981320 | tf_op jit(solution)/shard_map/ppermute | solution.py:241
  31.8 2.8 %copy-start.24 = (bf16[144,1152]{1,0:T(8,128)(2,1)S(1)}, bf16[144,1152]{1,0:T(8,128)(2,1)}, u32[]{:S(2)}) copy-start(bf16[144,1152]{1,0:T(8,128)(2,1)} %get-tuple-element.33) | copy-start | bytes 995332
  31.8 5.5 %copy-start.23 = (bf16[144,1152]{1,0:T(8,128)(2,1)S(1)}, bf16[144,1152]{1,0:T(8,128)(2,1)}, u32[]{:S(2)}) copy-start(bf16[144,1152]{1,0:T(8,128)(2,1)} %get-tuple-element.32) | copy-start | bytes 995332
  33.1 9.1 %collective-permute-start.5 = (bf16[144,1152]{1,0:T(8,128)(2,1)S(1)}, bf16[144,1152]{1,0:T(8,128)(2,1)S(1)}, u32[]{:S(2)}, u32[]{:S(2)}) collective-permute-start(bf16[144,1152]{1,0:T(8,128)(2,1)S(1)} %copy-done.25), channel_id=1, source_target_pairs={{0,2},{2,0},{4,6},{6,4},{1,3},{3,1},{5,7},{7,5},{8,10},{10,8},{12,... | collective-permute-start | bytes 995336 | tf_op jit(solution)/shard_map/ppermute | solution.py:244
  34.6 17.4 %collective-permute-start.6 = (bf16[144,1152]{1,0:T(8,128)(2,1)S(1)}, bf16[144,1152]{1,0:T(8,128)(2,1)}, u32[]{:S(2)}, u32[]{:S(2)}) collective-permute-start(bf16[144,1152]{1,0:T(8,128)(2,1)S(1)} %copy-done.24), channel_id=1, source_target_pairs={{0,4},{2,6},{4,0},{6,2},{1,5},{3,7},{5,1},{7,3},{8,12},{10,14},{12... | collective-permute-start | bytes 995336 | tf_op jit(solution)/shard_map/ppermute | solution.py:244
  37.3 24.0 %collective-permute-start.7 = (bf16[144,1152]{1,0:T(8,128)(2,1)S(1)}, bf16[144,1152]{1,0:T(8,128)(2,1)}, u32[]{:S(2)}, u32[]{:S(2)}) collective-permute-start(bf16[144,1152]{1,0:T(8,128)(2,1)S(1)} %copy-done.23), channel_id=1, source_target_pairs={{0,6},{2,4},{4,2},{6,0},{1,7},{3,5},{5,3},{7,1},{8,14},{10,12},{12... | collective-permute-start | bytes 995336 | tf_op jit(solution)/shard_map/ppermute | solution.py:244
  38.6 22.7 %collective-permute-start.10 = (bf16[144,1152]{1,0:T(8,128)(2,1)S(1)}, bf16[144,1152]{1,0:T(8,128)(2,1)}, u32[]{:S(2)}, u32[]{:S(2)}) collective-permute-start(bf16[144,1152]{1,0:T(8,128)(2,1)S(1)} %get-tuple-element.31), channel_id=1, source_target_pairs={{0,4},{2,6},{4,0},{6,2},{1,5},{3,7},{5,1},{7,3},{8,12},{10,14},{12... | collective-permute-start | bytes 995336 | tf_op jit(solution)/shard_map/ppermute | solution.py:244
  40.3 28.1 %collective-permute-start.11 = (bf16[144,1152]{1,0:T(8,128)(2,1)}, bf16[144,1152]{1,0:T(8,128)(2,1)}, u32[]{:S(2)}, u32[]{:S(2)}) collective-permute-start(bf16[144,1152]{1,0:T(8,128)(2,1)} %get-tuple-element.30), channel_id=1, source_target_pairs={{0,6},{2,4},{4,2},{6,0},{1,7},{3,5},{5,3},{7,1},{8,14},{10,12},{12... | collective-permute-start | bytes 995336 | tf_op jit(solution)/shard_map/ppermute | solution.py:244
  42.2 26.2 %collective-permute-start.9 = (bf16[144,1152]{1,0:T(8,128)(2,1)}, bf16[144,1152]{1,0:T(8,128)(2,1)}, u32[]{:S(2)}, u32[]{:S(2)}) collective-permute-start(bf16[144,1152]{1,0:T(8,128)(2,1)} %get-tuple-element.29), channel_id=1, source_target_pairs={{0,2},{2,0},{4,6},{6,4},{1,3},{3,1},{5,7},{7,5},{8,10},{10,8},{12,... | collective-permute-start | bytes 995336 | tf_op jit(solution)/shard_map/ppermute | solution.py:244
  43.8 27.3 %copy-start.2 = (bf16[2,152,1152]{2,1,0:T(8,128)(2,1)}, bf16[2,152,1152]{2,1,0:T(8,128)(2,1)S(1)}, u32[]{:S(2)}) copy-start(bf16[2,152,1152]{2,1,0:T(8,128)(2,1)S(1)} %pad_maximum_fusion.2.refs_0_) | copy-start | bytes 2101252
  52.0 26.6 %collective-permute-start = (bf16[2,152,1152]{2,1,0:T(8,128)(2,1)S(1)}, bf16[2,152,1152]{2,1,0:T(8,128)(2,1)S(1)}, u32[]{:S(2)}, u32[]{:S(2)}) collective-permute-start(bf16[2,152,1152]{2,1,0:T(8,128)(2,1)S(1)} %pad_maximum_fusion.2.refs_0_), channel_id=1, source_target_pairs={{0,2},{2,0},{4,6},{6,4},{1,3},{3,1},{5,7},{7,5},{8,10},{10,8},{12,... | collective-permute-start | bytes 2101256 | tf_op jit(solution)/shard_map/ppermute | solution.py:244
  61.3 34.9 %collective-permute-start.1 = (bf16[2,152,1152]{2,1,0:T(8,128)(2,1)S(1)}, bf16[2,152,1152]{2,1,0:T(8,128)(2,1)S(1)}, u32[]{:S(2)}, u32[]{:S(2)}) collective-permute-start(bf16[2,152,1152]{2,1,0:T(8,128)(2,1)S(1)} %pad_maximum_fusion.2.refs_0_), channel_id=1, source_target_pairs={{0,4},{2,6},{4,0},{6,2},{1,5},{3,7},{5,1},{7,3},{8,12},{10,14},{12... | collective-permute-start | bytes 2101256 | tf_op jit(solution)/shard_map/ppermute | solution.py:244
  61.3 37.0 %collective-permute-start.2 = (bf16[2,152,1152]{2,1,0:T(8,128)(2,1)S(1)}, bf16[2,152,1152]{2,1,0:T(8,128)(2,1)S(1)}, u32[]{:S(2)}, u32[]{:S(2)}) collective-permute-start(bf16[2,152,1152]{2,1,0:T(8,128)(2,1)S(1)} %pad_maximum_fusion.2.refs_0_), channel_id=1, source_target_pairs={{0,6},{2,4},{4,2},{6,0},{1,7},{3,5},{5,3},{7,1},{8,14},{10,12},{12... | collective-permute-start | bytes 2101256 | tf_op jit(solution)/shard_map/ppermute | solution.py:244
  72.2 33.6 %collective-permute-start.12 = (bf16[152,1152]{1,0:T(8,128)(2,1)S(1)}, bf16[152,1152]{1,0:T(8,128)(2,1)}, u32[]{:S(2)}, u32[]{:S(2)}) collective-permute-start(bf16[152,1152]{1,0:T(8,128)(2,1)S(1)} %pad_maximum_fusion.7), channel_id=1, source_target_pairs={{0,1},{1,0},{2,3},{3,2},{4,5},{5,4},{6,7},{7,6},{8,9},{9,8},{10,11... | collective-permute-start | bytes 1050632 | tf_op jit(solution)/shard_map/ppermute | solution.py:241
  103.6 3.0 %copy-start.11 = (f32[144,1152]{1,0:T(8,128)S(1)}, f32[144,1152]{1,0:T(8,128)}, u32[]{:S(2)}) copy-start(f32[144,1152]{1,0:T(8,128)} %copy-done.10) | copy-start | bytes 1990660
  103.6 3.0 %copy-start.14 = (f32[1,144,1152]{2,1,0:T(8,128)S(1)}, f32[1,144,1152]{2,1,0:T(8,128)}, u32[]{:S(2)}) copy-start(f32[1,144,1152]{2,1,0:T(8,128)} %copy-done.13) | copy-start | bytes 1990660
  103.9 8.0 %copy-start.1 = (bf16[4,2,152,1152]{3,2,1,0:T(8,128)(2,1)}, bf16[4,2,152,1152]{3,2,1,0:T(8,128)(2,1)S(1)}, u32[]{:S(2)}) copy-start(bf16[4,2,152,1152]{3,2,1,0:T(8,128)(2,1)S(1)} %shard_map.119.mine_ref) | copy-start | bytes 8404996
  103.9 23.9 %collective-permute-start.3 = (bf16[4,2,152,1152]{3,2,1,0:T(8,128)(2,1)S(1)}, bf16[4,2,152,1152]{3,2,1,0:T(8,128)(2,1)S(1)}, u32[]{:S(2)}, u32[]{:S(2)}) collective-permute-start(bf16[4,2,152,1152]{3,2,1,0:T(8,128)(2,1)S(1)} %shard_map.119.mine_ref), channel_id=1, source_target_pairs={{0,1},{1,0},{2,3},{3,2},{4,5},{5,4},{6,7},{7,6},{8,9},{9,8},{10,11... | collective-permute-start | bytes 8405000 | tf_op jit(solution)/shard_map/ppermute | solution.py:241
  108.0 6.0 %collective-permute-start.13 = (bf16[80,1152]{1,0:T(8,128)(2,1)S(1)}, bf16[80,1152]{1,0:T(8,128)(2,1)S(1)}, u32[]{:S(2)}, u32[]{:S(2)}) collective-permute-start(bf16[80,1152]{1,0:T(8,128)(2,1)S(1)} %get-tuple-element.58), channel_id=1, source_target_pairs={{0,32},{32,0},{64,96},{96,64},{1,33},{33,1},{65,97},{97,65},{2,34}... | collective-permute-start | bytes 552968 | tf_op jit(solution)/shard_map/ppermute | solution.py:244
  109.3 10.9 %collective-permute-start.14 = (bf16[80,1152]{1,0:T(8,128)(2,1)S(1)}, bf16[80,1152]{1,0:T(8,128)(2,1)S(1)}, u32[]{:S(2)}, u32[]{:S(2)}) collective-permute-start(bf16[80,1152]{1,0:T(8,128)(2,1)S(1)} %get-tuple-element.59), channel_id=1, source_target_pairs={{0,64},{32,96},{64,0},{96,32},{1,65},{33,97},{65,1},{97,33},{2,66}... | collective-permute-start | bytes 552968 | tf_op jit(solution)/shard_map/ppermute | solution.py:244
  111.8 10.9 %collective-permute-start.15 = (bf16[80,1152]{1,0:T(8,128)(2,1)S(1)}, bf16[80,1152]{1,0:T(8,128)(2,1)S(1)}, u32[]{:S(2)}, u32[]{:S(2)}) collective-permute-start(bf16[80,1152]{1,0:T(8,128)(2,1)S(1)} %get-tuple-element.60), channel_id=1, source_target_pairs={{0,96},{32,64},{64,32},{96,0},{1,97},{33,65},{65,33},{97,1},{2,98}... | collective-permute-start | bytes 552968 | tf_op jit(solution)/shard_map/ppermute | solution.py:244
  122.8 5.3 %collective-permute-start.16 = (bf16[80,1152]{1,0:T(8,128)(2,1)S(1)}, bf16[80,1152]{1,0:T(8,128)(2,1)S(1)}, u32[]{:S(2)}, u32[]{:S(2)}) collective-permute-start(bf16[80,1152]{1,0:T(8,128)(2,1)S(1)} %pad_maximum_fusion.3), channel_id=1, source_target_pairs={{0,8},{8,0},{16,24},{24,16},{1,9},{9,1},{17,25},{25,17},{2,10},{10... | collective-permute-start | bytes 552968 | tf_op jit(solution)/shard_map/ppermute | solution.py:244
  124.6 10.7 %collective-permute-start.17 = (bf16[80,1152]{1,0:T(8,128)(2,1)S(1)}, bf16[80,1152]{1,0:T(8,128)(2,1)S(1)}, u32[]{:S(2)}, u32[]{:S(2)}) collective-permute-start(bf16[80,1152]{1,0:T(8,128)(2,1)S(1)} %pad_maximum_fusion.3), channel_id=1, source_target_pairs={{0,16},{8,24},{16,0},{24,8},{1,17},{9,25},{17,1},{25,9},{2,18},{10... | collective-permute-start | bytes 552968 | tf_op jit(solution)/shard_map/ppermute | solution.py:244
  127.9 10.4 %collective-permute-start.18 = (bf16[80,1152]{1,0:T(8,128)(2,1)S(1)}, bf16[80,1152]{1,0:T(8,128)(2,1)S(1)}, u32[]{:S(2)}, u32[]{:S(2)}) collective-permute-start(bf16[80,1152]{1,0:T(8,128)(2,1)S(1)} %pad_maximum_fusion.3), channel_id=1, source_target_pairs={{0,24},{8,16},{16,8},{24,0},{1,25},{9,17},{17,9},{25,1},{2,26},{10... | collective-permute-start | bytes 552968 | tf_op jit(solution)/shard_map/ppermute | solution.py:244
  127.9 35.2 %copy-start.18 = (bf16[4,2,152,1152]{3,2,1,0:T(8,128)(2,1)}, bf16[4,2,152,1152]{3,2,1,0:T(8,128)(2,1)S(1)}, u32[]{:S(2)}) copy-start(bf16[4,2,152,1152]{3,2,1,0:T(8,128)(2,1)S(1)} %collective-permute-done.3.theirs_ref) | copy-start | bytes 8404996
  138.4 4.3 %collective-permute-start.19 = (bf16[72,1152]{1,0:T(8,128)(2,1)S(1)}, bf16[72,1152]{1,0:T(8,128)(2,1)S(1)}, u32[]{:S(2)}, u32[]{:S(2)}) collective-permute-start(bf16[72,1152]{1,0:T(8,128)(2,1)S(1)} %add_convert_fusion.6.refs_0_), channel_id=1, source_target_pairs={{0,32},{32,0},{64,96},{96,64},{1,33},{33,1},{65,97},{97,65},{2,34}... | collective-permute-start | bytes 497672 | tf_op jit(solution)/shard_map/ppermute | solution.py:244
  138.5 7.4 %collective-permute-start.20 = (bf16[72,1152]{1,0:T(8,128)(2,1)S(1)}, bf16[72,1152]{1,0:T(8,128)(2,1)S(1)}, u32[]{:S(2)}, u32[]{:S(2)}) collective-permute-start(bf16[72,1152]{1,0:T(8,128)(2,1)S(1)} %add_convert_fusion.6.refs_0_), channel_id=1, source_target_pairs={{0,64},{32,96},{64,0},{96,32},{1,65},{33,97},{65,1},{97,33},{2,66}... | collective-permute-start | bytes 497672 | tf_op jit(solution)/shard_map/ppermute | solution.py:244
  139.8 9.1 %collective-permute-start.21 = (bf16[72,1152]{1,0:T(8,128)(2,1)S(1)}, bf16[72,1152]{1,0:T(8,128)(2,1)S(1)}, u32[]{:S(2)}, u32[]{:S(2)}) collective-permute-start(bf16[72,1152]{1,0:T(8,128)(2,1)S(1)} %add_convert_fusion.6.refs_0_), channel_id=1, source_target_pairs={{0,96},{32,64},{64,32},{96,0},{1,97},{33,65},{65,33},{97,1},{2,98}... | collective-permute-start | bytes 497672 | tf_op jit(solution)/shard_map/ppermute | solution.py:244
  149.8 4.0 %collective-permute-start.22 = (bf16[40,1408]{1,0:T(8,128)(2,1)S(1)}, bf16[40,1408]{1,0:T(8,128)(2,1)S(1)}, u32[]{:S(2)}, u32[]{:S(2)}) collective-permute-start(bf16[40,1408]{1,0:T(8,128)(2,1)S(1)} %get-tuple-element.19.refs_0_), channel_id=1, source_target_pairs={{0,2},{2,0},{4,6},{6,4},{1,3},{3,1},{5,7},{7,5},{8,10},{10,8},{12,... | collective-permute-start | bytes 337928 | tf_op jit(solution)/shard_map/ppermute | solution.py:244
  149.9 6.1 %collective-permute-start.23 = (bf16[40,1408]{1,0:T(8,128)(2,1)S(1)}, bf16[40,1408]{1,0:T(8,128)(2,1)S(1)}, u32[]{:S(2)}, u32[]{:S(2)}) collective-permute-start(bf16[40,1408]{1,0:T(8,128)(2,1)S(1)} %get-tuple-element.19.refs_0_), channel_id=1, source_target_pairs={{0,4},{2,6},{4,0},{6,2},{1,5},{3,7},{5,1},{7,3},{8,12},{10,14},{12... | collective-permute-start | bytes 337928 | tf_op jit(solution)/shard_map/ppermute | solution.py:244
  151.0 7.1 %collective-permute-start.24 = (bf16[40,1408]{1,0:T(8,128)(2,1)S(1)}, bf16[40,1408]{1,0:T(8,128)(2,1)S(1)}, u32[]{:S(2)}, u32[]{:S(2)}) collective-permute-start(bf16[40,1408]{1,0:T(8,128)(2,1)S(1)} %get-tuple-element.19.refs_0_), channel_id=1, source_target_pairs={{0,6},{2,4},{4,2},{6,0},{1,7},{3,5},{5,3},{7,1},{8,14},{10,12},{12... | collective-permute-start | bytes 337928 | tf_op jit(solution)/shard_map/ppermute | solution.py:244
  161.4 10.9 %collective-permute-start.29 = (f32[8,1152]{1,0:T(8,128)S(1)}, f32[8,1152]{1,0:T(8,128)S(1)}, u32[]{:S(2)}, u32[]{:S(2)}) collective-permute-start(f32[8,1152]{1,0:T(8,128)S(1)} %get-tuple-element.24), channel_id=1, source_target_pairs={{0,1},{1,0},{2,3},{3,2},{4,5},{5,4},{6,7},{7,6},{8,9},{9,8},{10,11... | collective-permute-start | bytes 110600 | tf_op jit(solution)/shard_map/ppermute | solution.py:241
  168.4 5.2 %collective-permute-start.25 = (bf16[32,2176]{1,0:T(8,128)(2,1)S(1)}, bf16[32,2176]{1,0:T(8,128)(2,1)S(1)}, u32[]{:S(2)}, u32[]{:S(2)}) collective-permute-start(bf16[32,2176]{1,0:T(8,128)(2,1)S(1)} %get-tuple-element.21.refs_0_), channel_id=1, source_target_pairs={{0,2},{2,0},{4,6},{6,4},{1,3},{3,1},{5,7},{7,5},{8,10},{10,8},{12,... | collective-permute-start | bytes 417800 | tf_op jit(solution)/shard_map/ppermute | solution.py:244
  168.5 10.3 %collective-permute-start.26 = (bf16[32,2176]{1,0:T(8,128)(2,1)S(1)}, bf16[32,2176]{1,0:T(8,128)(2,1)S(1)}, u32[]{:S(2)}, u32[]{:S(2)}) collective-permute-start(bf16[32,2176]{1,0:T(8,128)(2,1)S(1)} %get-tuple-element.21.refs_0_), channel_id=1, source_target_pairs={{0,4},{2,6},{4,0},{6,2},{1,5},{3,7},{5,1},{7,3},{8,12},{10,14},{12... | collective-permute-start | bytes 417800 | tf_op jit(solution)/shard_map/ppermute | solution.py:244
  172.0 9.3 %collective-permute-start.27 = (bf16[32,2176]{1,0:T(8,128)(2,1)S(1)}, bf16[32,2176]{1,0:T(8,128)(2,1)S(1)}, u32[]{:S(2)}, u32[]{:S(2)}) collective-permute-start(bf16[32,2176]{1,0:T(8,128)(2,1)S(1)} %get-tuple-element.21.refs_0_), channel_id=1, source_target_pairs={{0,6},{2,4},{4,2},{6,0},{1,7},{3,5},{5,3},{7,1},{8,14},{10,12},{12... | collective-permute-start | bytes 417800 | tf_op jit(solution)/shard_map/ppermute | solution.py:244
  184.0 6.6 %slice-start = ((s8[5308416]{0:T(1024)(128)(4,1)}), s8[4194304]{0:T(1024)(128)(4,1)S(1)}, s32[]{:S(2)}) async-start(s8[5308416]{0:T(1024)(128)(4,1)} %bitcast.121), calls=%async_computation | async-start | bytes 8388608
  184.0 2.5 %collective-permute-start.28 = (f32[32,2304]{1,0:T(8,128)S(1)}, f32[32,2304]{1,0:T(8,128)S(1)}, u32[]{:S(2)}, u32[]{:S(2)}) collective-permute-start(f32[32,2304]{1,0:T(8,128)S(1)} %pad_maximum_fusion.14), channel_id=1, source_target_pairs={{0,1},{1,0},{2,3},{3,2},{4,5},{5,4},{6,7},{7,6},{8,9},{9,8},{10,11... | collective-permute-start | bytes 884744 | tf_op jit(solution)/shard_map/ppermute | solution.py:241
  186.9 3.6 %slice-start.1 = ((s8[5308416]{0:T(1024)(128)(4,1)}), s8[1114112]{0:T(1024)(128)(4,1)S(1)}, s32[]{:S(2)}) async-start(s8[5308416]{0:T(1024)(128)(4,1)} %bitcast.121), calls=%async_computation.1 | async-start | bytes 2228224
  (15 other events, 17.9 us)
where the time goes:
time: 195 us
  waiting for transfers between devices  90.3 us (46%)
  starting transfers between devices  39.1 us (20%)
  matrix products  27.2 us (14%)
  local copies, waits for them, and re-layouts  13 us (7%)
  other arithmetic  12.1 us (6%)
  Pallas kernels  11.9 us (6%)
    ppermute x24, waiting for transfers between devices, trade(): return lax.ppermute(value, axis, [(i, i ^ k) for i in range(4)])  87.4 us
    ppermute x24, starting transfers between devices, trade(): return lax.ppermute(value, axis, [(i, i ^ k) for i in range(4)])  29.4 us
    dot_general x2, matrix products, chip_blocks(): jnp.einsum('tr,te->re', x[layer], y[layer], preferred_element_type=F32)  20.4 us
    unnamed x66, local copies, waits for them, and re-layouts  11.2 us
    ppermute x6, starting transfers between devices, swap(): return lax.ppermute(value, 'core', ring(cores, 1))  9.69 us
    pallas_call x4, Pallas kernels, call(): pl.pallas_call(kernel, out_shape=outs, in_specs=[smem] * scalars + [vmem]...  6.47 us
    pallas_call x1, Pallas kernels, assemble(): pl.pallas_call(assemble_kernel, out_shape=jax.ShapeDtypeStruct((layers, w...  5.38 us
    dot_general x1, matrix products, body(): jnp.einsum(spec, left, right, preferred_element_type=F32) * (1.0 / reps)  4.19 us
  transfers between devices with their start and end apart: 30, of which 22 were waited for; matrix products, arithmetic and copies ran while one was open for 5% of the time, Pallas kernels for 3%

commit v1 on v0

--- a/solution.py
+++ b/solution.py
@@ -155,14 +155,24 @@
 
         @pl.when(ypos_ref[0] == spot)
         def _():
-            def move(i, carry):
-                at = pl.ds(pl.multiple_of(8 * i, 8), 8)
-                for j in range(4):
-                    for layer in range(out_ref.shape[1]):
-                        out_ref[j, layer, at] = parts[spot ^ j][layer, at]
-                return carry
-
-            lax.fori_loop(0, out_ref.shape[2] // 8, move, 0)
+            for j in range(4):
+                out_ref[j] = parts[spot ^ j][...]
+
+
+def lineup(ypos, parts):
+    layers, held, width = parts[0].shape
+    block = pl.BlockSpec((1, held, width), lambda i, ypos: (i, 0, 0))
+    return pl.pallas_call(
+        lineup_kernel,
+        out_shape=jax.ShapeDtypeStruct((4, layers, held, width), BF),
+        grid_spec=pltpu.PrefetchScalarGridSpec(
+            num_scalar_prefetch=1,
+            grid=(layers,),
+            in_specs=[block] * 4,
+            out_specs=pl.BlockSpec((4, 1, held, width), lambda i, ypos: (0, i, 0, 0)),
+        ),
+        name="lineup",
+    )(ypos, *parts)
 
 
 def assemble_kernel(core_ref, mine_ref, theirs_ref, out_ref):
@@ -263,10 +273,7 @@
     parts = [old]
     for k in (1, 2, 3):
         parts.append(trade(old, "y", k))
-    held = rows + 8
-    mine = in_vmem(
-        lineup_kernel, jax.ShapeDtypeStruct((ys, layers, held, width), BF), 1
-    )(ypos.astype(jnp.int32)[None], *parts)
+    mine = lineup(ypos.astype(jnp.int32)[None], parts)
     theirs = swap(mine)
     old = assemble(core.astype(jnp.int32)[None], mine, theirs, rows)
     tails = [stack[:, :, rows : rows + 2, :rows].astype(F32) for stack in (mine, theirs)]
@@ -293,7 +300,8 @@
         for k in (1, 2, 3):
             block = trade(blocks[k - 1], "y", k)
             own = own + block.astype(F32)
-        return own * scale + errors[0, layer]
+        held = errors if layer else lax.optimization_barrier(errors)
+        return own * scale + held[0, layer]
 
     own0, blocks0 = chip_blocks(0)
     own1, blocks1 = chip_blocks(1, blocks0)

time: 195 us -> 212 us (1.087)
  waiting for transfers between devices: 90.3 us -> 103 us
  other arithmetic: 12.1 us -> 18.1 us
  local copies, waits for them, and re-layouts: 13 us -> 8.55 us
  starting transfers between devices: 39.1 us -> 36.2 us
  Pallas kernels: 11.9 us -> 14.5 us
  matrix products: 27.2 us -> 29.5 us
    ppermute x24, waiting for transfers between devices: 87.4 us -> 100 us  [trade(): return lax.ppermute(value, axis, [(i, i ^ k) for i in range(4)])]
    unnamed x66 -> x30, local copies, waits for them, and re-layouts: 11.2 us -> 2.27 us
    ppermute x6, starting transfers between devices: 9.69 us -> 5.66 us  [swap(): return lax.ppermute(value, 'core', ring(cores, 1))]
    pallas_call x0 -> x1, Pallas kernels: none -> 2.96 us  [lineup(): pl.pallas_call(lineup_kernel, out_shape=jax.ShapeDtypeStruct((4, layers,...]
    squeeze x2, local copies, waits for them, and re-layouts: 1.4 us -> 3.8 us  [pick(): return lax.dynamic_index_in_dim(stack, index, axis, keepdims=False)]
    pallas_call x4 -> x3, Pallas kernels: 6.47 us -> 6.18 us  [call(): pl.pallas_call(kernel, out_shape=outs, in_specs=[smem] * scalars + [vmem]...]
  transfers between devices with their start and end apart: 30 -> 30, of which waited for: 22 -> 19; matrix products, arithmetic and copies ran while one was open for 5% -> 7% of each run, Pallas kernels for 3% -> 4%
where the time goes in v1:
time: 212 us; the launch traced here: 211 us
  waiting for transfers between devices  103 us (49%)
  starting transfers between devices  36.2 us (17%)
  matrix products  29.5 us (14%)
  other arithmetic  18.1 us (9%)
  Pallas kernels  14.5 us (7%)
  local copies, waits for them, and re-layouts  8.55 us (4%)
    ppermute x24, waiting for transfers between devices, trade(): return lax.ppermute(value, axis, [(i, i ^ k) for i in range(4)])  100 us
    ppermute x24, starting transfers between devices, trade(): return lax.ppermute(value, axis, [(i, i ^ k) for i in range(4)])  30.5 us
    dot_general x2, matrix products, chip_blocks(): jnp.einsum('tr,te->re', x[layer], y[layer], preferred_element_type=F32)  21.9 us
    pallas_call x3, Pallas kernels, call(): pl.pallas_call(kernel, out_shape=outs, in_specs=[smem] * scalars + [vmem]...  6.18 us
    ppermute x6, starting transfers between devices, swap(): return lax.ppermute(value, 'core', ring(cores, 1))  5.66 us
    pallas_call x1, Pallas kernels, assemble(): pl.pallas_call(assemble_kernel, out_shape=jax.ShapeDtypeStruct((layers, w...  5.37 us
  transfers between devices with their start and end apart: 30, of which 19 were waited for; matrix products, arithmetic and copies ran while one was open for 7% of the time, Pallas kernels for 4%

profile of v1, /device:TPU:1, one launch (start us, length us, event | category | flops | bytes accessed | tf_op | source)
XLA Modules:
  0.0 211.0 jit_solution(14934100676447299267)
XLA Ops:
  0.7 11.6 %convolution_convert_fusion.1 = bf16[1152,1152]{1,0:T(8,128)(2,1)} fusion(bf16[2,2048,1152]{2,1,0:T(8,128)(2,1)} %param.9, bf16[2,2048,1152]{2,1,0:T(8,128)(2,1)} %param.8), kind=kOutput, calls=%fused_computation.4 | convolution fusion | flops 5437145088 | bytes 12091392 | tf_op jit(solution)/shard_map/tr,te->re/dot_general | solution.py:288
  12.3 2.6 %dynamic-slice_bitcast_fusion.1 = bf16[4,144,1152]{2,1,0:T(8,128)(2,1)} fusion(bf16[4,2,144,1152]{3,2,1,0:T(8,128)(2,1)} %bitcast.132, s32[]{:T(128)S(6)} %select_n.199), kind=kLoop, calls=%fused_computation.24 | loop fusion | bytes 2654212 | tf_op jit(solution)/shard_map/jit(dynamic_index_in_dim)/squeeze | solution.py:21
  14.9 1.4 collective-permute-start.4
  16.6 2.8 %collective-permute-done.4 = bf16[4,144,1152]{2,1,0:T(8,128)(2,1)} collective-permute-done((bf16[4,144,1152]{2,1,0:T(8,128)(2,1)}, bf16[4,144,1152]{2,1,0:T(8,128)(2,1)}, u32[]{:S(2)}, u32[]{:S(2)}) %collective-permute-start.4) | collective-permute-done | bytes 1327136 | tf_op jit(solution)/shard_map/ppermute | solution.py:251
  19.4 1.7 fusion.26
  21.1 10.3 %convolution_convert_fusion = bf16[1152,1152]{1,0:T(8,128)(2,1)S(1)} fusion(bf16[2,2048,1152]{2,1,0:T(8,128)(2,1)} %param.9, bf16[2,2048,1152]{2,1,0:T(8,128)(2,1)} %param.8), kind=kOutput, calls=%fused_computation.3 | convolution fusion | flops 5437145088 | bytes 12091392 | tf_op jit(solution)/shard_map/tr,te->re/dot_general | solution.py:288
  31.4 1.5 copy-done.3
  35.3 1.4 collective-permute-start
  38.2 3.0 %collective-permute-start.6 = (bf16[144,1152]{1,0:T(8,128)(2,1)S(1)}, bf16[144,1152]{1,0:T(8,128)(2,1)S(1)}, u32[]{:S(2)}, u32[]{:S(2)}) collective-permute-start(bf16[144,1152]{1,0:T(8,128)(2,1)S(1)} %get-tuple-element.33), channel_id=1, source_target_pairs={{0,4},{2,6},{4,0},{6,2},{1,5},{3,7},{5,1},{7,3},{8,12},{10,14},{12... | collective-permute-start | bytes 995336 | tf_op jit(solution)/shard_map/ppermute | solution.py:254
  42.0 1.5 collective-permute-start.1
  43.5 1.8 fusion.27
  45.3 14.4 %collective-permute-done.5 = bf16[144,1152]{1,0:T(8,128)(2,1)S(1)} collective-permute-done((bf16[144,1152]{1,0:T(8,128)(2,1)S(1)}, bf16[144,1152]{1,0:T(8,128)(2,1)S(1)}, u32[]{:S(2)}, u32[]{:S(2)}) %collective-permute-start.5) | collective-permute-done | bytes 331808 | tf_op jit(solution)/shard_map/ppermute | solution.py:254
  59.8 3.0 %collective-permute-start.10 = (bf16[144,1152]{1,0:T(8,128)(2,1)S(1)}, bf16[144,1152]{1,0:T(8,128)(2,1)S(1)}, u32[]{:S(2)}, u32[]{:S(2)}) collective-permute-start(bf16[144,1152]{1,0:T(8,128)(2,1)S(1)} %get-tuple-element.31), channel_id=1, source_target_pairs={{0,4},{2,6},{4,0},{6,2},{1,5},{3,7},{5,1},{7,3},{8,12},{10,14},{12... | collective-permute-start | bytes 995336 | tf_op jit(solution)/shard_map/ppermute | solution.py:254
  62.8 6.6 %collective-permute-done.6 = bf16[144,1152]{1,0:T(8,128)(2,1)S(1)} collective-permute-done((bf16[144,1152]{1,0:T(8,128)(2,1)S(1)}, bf16[144,1152]{1,0:T(8,128)(2,1)S(1)}, u32[]{:S(2)}, u32[]{:S(2)}) %collective-permute-start.6) | collective-permute-done | bytes 331808 | tf_op jit(solution)/shard_map/ppermute | solution.py:254
  70.2 1.8 fusion.16
  72.0 19.6 %collective-permute-done.10 = bf16[144,1152]{1,0:T(8,128)(2,1)S(1)} collective-permute-done((bf16[144,1152]{1,0:T(8,128)(2,1)S(1)}, bf16[144,1152]{1,0:T(8,128)(2,1)S(1)}, u32[]{:S(2)}, u32[]{:S(2)}) %collective-permute-start.10) | collective-permute-done | bytes 331808 | tf_op jit(solution)/shard_map/ppermute | solution.py:254
  91.6 7.6 %collective-permute-done.11 = bf16[144,1152]{1,0:T(8,128)(2,1)S(1)} collective-permute-done((bf16[144,1152]{1,0:T(8,128)(2,1)S(1)}, bf16[144,1152]{1,0:T(8,128)(2,1)S(1)}, u32[]{:S(2)}, u32[]{:S(2)}) %collective-permute-start.11) | collective-permute-done | bytes 331808 | tf_op jit(solution)/shard_map/ppermute | solution.py:254
  99.2 1.3 fusion.17
  101.4 12.9 %collective-permute-done.2.refs_3_ = bf16[2,152,1152]{2,1,0:T(8,128)(2,1)} collective-permute-done((bf16[2,152,1152]{2,1,0:T(8,128)(2,1)}, bf16[2,152,1152]{2,1,0:T(8,128)(2,1)}, u32[]{:S(2)}, u32[]{:S(2)}) %collective-permute-start.2) | collective-permute-done | bytes 700448 | tf_op jit(solution)/shard_map/ppermute | solution.py:254
  114.3 3.0 %lineup.1.mine_ref = bf16[4,2,152,1152]{3,2,1,0:T(8,128)(2,1)} custom-call(s32[1]{0:T(128)} %bitcast.1.ypos_ref, bf16[2,152,1152]{2,1,0:T(8,128)(2,1)} %pad_maximum_fusion.2.refs_0_, bf16[2,152,1152]{2,1,0:T(8,128)(2,1)} %collective-permute-done.refs_1_, bf16[2,152,1152]{2,1,0:T(8,128)(2,1)} %collective-permute-done.1.refs_2_, ...), custom_call_target="tpu_custom_call" | custom-call | tf_op jit(solution)/shard_map/lineup/pallas_call | solution.py:165
  121.2 2.5 %collective-permute-start.14 = (bf16[80,1152]{1,0:T(8,128)(2,1)S(1)}, bf16[80,1152]{1,0:T(8,128)(2,1)S(1)}, u32[]{:S(2)}, u32[]{:S(2)}) collective-permute-start(bf16[80,1152]{1,0:T(8,128)(2,1)S(1)} %get-tuple-element.57), channel_id=1, source_target_pairs={{0,64},{32,96},{64,0},{96,32},{1,65},{33,97},{65,1},{97,33},{2,66}... | collective-permute-start | bytes 552968 | tf_op jit(solution)/shard_map/ppermute | solution.py:254
  124.6 1.6 collective-permute-done.13
  126.2 6.2 %collective-permute-done.14 = bf16[80,1152]{1,0:T(8,128)(2,1)S(1)} collective-permute-done((bf16[80,1152]{1,0:T(8,128)(2,1)S(1)}, bf16[80,1152]{1,0:T(8,128)(2,1)S(1)}, u32[]{:S(2)}, u32[]{:S(2)}) %collective-permute-start.14) | collective-permute-done | bytes 184352 | tf_op jit(solution)/shard_map/ppermute | solution.py:254
  132.4 2.2 %collective-permute-done.15 = bf16[80,1152]{1,0:T(8,128)(2,1)S(1)} collective-permute-done((bf16[80,1152]{1,0:T(8,128)(2,1)S(1)}, bf16[80,1152]{1,0:T(8,128)(2,1)S(1)}, u32[]{:S(2)}, u32[]{:S(2)}) %collective-permute-start.15) | collective-permute-done | bytes 184352 | tf_op jit(solution)/shard_map/ppermute | solution.py:254
  134.8 1.7 collective-permute-start.16
  136.5 3.3 %collective-permute-start.17 = (bf16[80,1152]{1,0:T(8,128)(2,1)S(1)}, bf16[80,1152]{1,0:T(8,128)(2,1)S(1)}, u32[]{:S(2)}, u32[]{:S(2)}) collective-permute-start(bf16[80,1152]{1,0:T(8,128)(2,1)S(1)} %pad_maximum_fusion.3), channel_id=1, source_target_pairs={{0,16},{8,24},{16,0},{24,8},{1,17},{9,25},{17,1},{25,9},{2,18},{10... | collective-permute-start | bytes 552968 | tf_op jit(solution)/shard_map/ppermute | solution.py:254
  140.1 7.1 %collective-permute-done.17 = bf16[80,1152]{1,0:T(8,128)(2,1)S(1)} collective-permute-done((bf16[80,1152]{1,0:T(8,128)(2,1)S(1)}, bf16[80,1152]{1,0:T(8,128)(2,1)S(1)}, u32[]{:S(2)}, u32[]{:S(2)}) %collective-permute-start.17) | collective-permute-done | bytes 184352 | tf_op jit(solution)/shard_map/ppermute | solution.py:254
  147.2 3.0 %collective-permute-done.18 = bf16[80,1152]{1,0:T(8,128)(2,1)S(1)} collective-permute-done((bf16[80,1152]{1,0:T(8,128)(2,1)S(1)}, bf16[80,1152]{1,0:T(8,128)(2,1)S(1)}, u32[]{:S(2)}, u32[]{:S(2)}) %collective-permute-start.18) | collective-permute-done | bytes 184352 | tf_op jit(solution)/shard_map/ppermute | solution.py:254
  150.4 1.4 collective-permute-start.20
  151.7 2.5 %collective-permute-start.21 = (bf16[72,1152]{1,0:T(8,128)(2,1)S(1)}, bf16[72,1152]{1,0:T(8,128)(2,1)S(1)}, u32[]{:S(2)}, u32[]{:S(2)}) collective-permute-start(bf16[72,1152]{1,0:T(8,128)(2,1)S(1)} %add_convert_fusion.6.refs_0_), channel_id=1, source_target_pairs={{0,96},{32,64},{64,32},{96,0},{1,97},{33,65},{65,33},{97,1},{2,98}... | collective-permute-start | bytes 497672 | tf_op jit(solution)/shard_map/ppermute | solution.py:254
  154.6 3.2 %collective-permute-done.20.refs_2_ = bf16[72,1152]{1,0:T(8,128)(2,1)S(1)} collective-permute-done((bf16[72,1152]{1,0:T(8,128)(2,1)S(1)}, bf16[72,1152]{1,0:T(8,128)(2,1)S(1)}, u32[]{:S(2)}, u32[]{:S(2)}) %collective-permute-start.20) | collective-permute-done | bytes 165920 | tf_op jit(solution)/shard_map/ppermute | solution.py:254
  157.8 3.0 %collective-permute-done.21.refs_3_ = bf16[72,1152]{1,0:T(8,128)(2,1)S(1)} collective-permute-done((bf16[72,1152]{1,0:T(8,128)(2,1)S(1)}, bf16[72,1152]{1,0:T(8,128)(2,1)S(1)}, u32[]{:S(2)}, u32[]{:S(2)}) %collective-permute-start.21) | collective-permute-done | bytes 165920 | tf_op jit(solution)/shard_map/ppermute | solution.py:254
  162.9 2.8 %collective-permute-start.24 = (bf16[40,1408]{1,0:T(8,128)(2,1)S(1)}, bf16[40,1408]{1,0:T(8,128)(2,1)S(1)}, u32[]{:S(2)}, u32[]{:S(2)}) collective-permute-start(bf16[40,1408]{1,0:T(8,128)(2,1)S(1)} %get-tuple-element.19.refs_0_), channel_id=1, source_target_pairs={{0,6},{2,4},{4,2},{6,0},{1,7},{3,5},{5,3},{7,1},{8,14},{10,12},{12... | collective-permute-start | bytes 337928 | tf_op jit(solution)/shard_map/ppermute | solution.py:254
  165.7 2.3 %collective-permute-done.23.refs_2_ = bf16[40,1408]{1,0:T(8,128)(2,1)S(1)} collective-permute-done((bf16[40,1408]{1,0:T(8,128)(2,1)S(1)}, bf16[40,1408]{1,0:T(8,128)(2,1)S(1)}, u32[]{:S(2)}, u32[]{:S(2)}) %collective-permute-start.23) | collective-permute-done | bytes 112672 | tf_op jit(solution)/shard_map/ppermute | solution.py:254
  168.0 2.2 %collective-permute-done.24.refs_3_ = bf16[40,1408]{1,0:T(8,128)(2,1)S(1)} collective-permute-done((bf16[40,1408]{1,0:T(8,128)(2,1)S(1)}, bf16[40,1408]{1,0:T(8,128)(2,1)S(1)}, u32[]{:S(2)}, u32[]{:S(2)}) %collective-permute-start.24) | collective-permute-done | bytes 112672 | tf_op jit(solution)/shard_map/ppermute | solution.py:254
  170.2 3.2 %shard_map.120 = (bf16[32,2176]{1,0:T(8,128)(2,1)S(1)}, f32[8,1152]{1,0:T(8,128)S(1)}) custom-call(bf16[40,1408]{1,0:T(8,128)(2,1)S(1)} %get-tuple-element.19.refs_0_, bf16[40,1408]{1,0:T(8,128)(2,1)S(1)} %collective-permute-done.22.refs_1_, bf16[40,1408]{1,0:T(8,128)(2,1)S(1)} %collective-permute-done.23.refs_2_, ...), custom_call_target="tpu_custom_call" | custom-call | tf_op jit(solution)/shard_map/pallas_call | solution.py:210
  173.4 1.5 collective-permute-start.29
  175.6 5.4 %assemble.1 = bf16[2,1152,1152]{2,1,0:T(8,128)(2,1)} custom-call(s32[1]{0:T(128)} %bitcast.core_ref, bf16[4,2,152,1152]{3,2,1,0:T(8,128)(2,1)} %lineup.1.mine_ref, bf16[4,2,152,1152]{3,2,1,0:T(8,128)(2,1)} %copy-done.2), custom_call_target="tpu_custom_call" | custom-call | tf_op jit(solution)/shard_map/assemble/pallas_call | solution.py:192
  181.1 3.5 %collective-permute-start.26 = (bf16[32,2176]{1,0:T(8,128)(2,1)S(1)}, bf16[32,2176]{1,0:T(8,128)(2,1)S(1)}, u32[]{:S(2)}, u32[]{:S(2)}) collective-permute-start(bf16[32,2176]{1,0:T(8,128)(2,1)S(1)} %get-tuple-element.21.refs_0_), channel_id=1, source_target_pairs={{0,4},{2,6},{4,0},{6,2},{1,5},{3,7},{5,1},{7,3},{8,12},{10,14},{12... | collective-permute-start | bytes 417800 | tf_op jit(solution)/shard_map/ppermute | solution.py:254
  184.8 1.4 broadcast_select_fusion.5
  186.2 5.1 %collective-permute-done.26.refs_2_ = bf16[32,2176]{1,0:T(8,128)(2,1)S(1)} collective-permute-done((bf16[32,2176]{1,0:T(8,128)(2,1)S(1)}, bf16[32,2176]{1,0:T(8,128)(2,1)S(1)}, u32[]{:S(2)}, u32[]{:S(2)}) %collective-permute-start.26) | collective-permute-done | bytes 139296 | tf_op jit(solution)/shard_map/ppermute | solution.py:254
  191.3 2.5 %collective-permute-done.27.refs_3_ = bf16[32,2176]{1,0:T(8,128)(2,1)S(1)} collective-permute-done((bf16[32,2176]{1,0:T(8,128)(2,1)S(1)}, bf16[32,2176]{1,0:T(8,128)(2,1)S(1)}, u32[]{:S(2)}, u32[]{:S(2)}) %collective-permute-start.27) | collective-permute-done | bytes 139296 | tf_op jit(solution)/shard_map/ppermute | solution.py:254
  195.2 1.6 concatenate.40
  196.8 2.1 %shard_map.121 = (f32[32,1152]{1,0:T(8,128)S(1)}, f32[32,32]{1,0:T(8,128)S(1)}) custom-call(bf16[32,2176]{1,0:T(8,128)(2,1)S(1)} %get-tuple-element.21.refs_0_, bf16[32,2176]{1,0:T(8,128)(2,1)S(1)} %collective-permute-done.25.refs_1_, bf16[32,2176]{1,0:T(8,128)(2,1)S(1)} %collective-permute-done.26.refs_2_, bf16[32,2176]{1,0:T(8,128)(2,1)S(1)} %collective-permute-done.27.refs_3_), custom_call_target="tpu_custom_call" | custom-call | tf_op jit(solution)/shard_map/pallas_call | solution.py:210
  201.4 1.3 fusion.51
  202.7 1.3 multiply_add_fusion.1
  204.6 2.2 %multiply_add_fusion = (f32[2,144,1152]{2,1,0:T(8,128)}, f32[1,2,144,1152]{3,2,1,0:T(8,128)}) fusion(f32[2,144,1152]{2,1,0:T(8,128)S(1)} %copy-done.1, f32[1,144,1152]{2,1,0:T(8,128)S(1)} %fusion.17, f32[1,144,1152]{2,1,0:T(8,128)S(1)} %bitcast.127, bf16[2,192,1152]{2,1,0:T(8,128)(2,1)S(1)} %constant_dynamic-update-slice_fusion.5, ...), kind=kOutput, calls=%fused_computation.22 | convolution fusion | flops 129060864 | bytes 6389764 | tf_op jit(solution)/shard_map/lkr,lke->lre/dot_general | solution.py:373
  206.8 4.2 %subtract_convert_fusion = bf16[2,1152,1152]{2,1,0:T(8,128)(2,1)} fusion(bf16[2,1152,1152]{2,1,0:T(8,128)(2,1)S(1)} %bitcast.124, bf16[2,192,1152]{2,1,0:T(8,128)(2,1)S(1)} %fusion.41, bf16[2,192,1152]{2,1,0:T(8,128)(2,1)S(1)} %constant_dynamic-update-slice_fusion.5), kind=kOutput, calls=%fused_computation.2 | convolution fusion | flops 1029832704 | bytes 12386304 | tf_op jit(solution)/shard_map/lkr,lke->lre/dot_general | solution.py:376
  (112 shorter events, 19.9 us)
Async XLA Ops:
  0.6 100.7 %copy-start = (f32[2,1152,32]{1,2,0:T(8,128)S(1)}, f32[2,1152,32]{1,2,0:T(8,128)}, u32[]{:S(2)}) copy-start(f32[2,1152,32]{1,2,0:T(8,128)} %param.15) | copy-start | bytes 884740
  12.3 4.0 %copy-start.8 = (f32[2,144]{1,0:T(2,128)S(1)}, f32[2,144]{1,0:T(2,128)}, u32[]{:S(2)}) copy-start(f32[2,144]{1,0:T(2,128)} %param.14) | copy-start | bytes 3460
  12.3 4.0 %copy-start.9 = (bf16[2,144]{1,0:T(2,128)(2,1)S(1)}, bf16[2,144]{1,0:T(2,128)(2,1)}, u32[]{:S(2)}) copy-start(bf16[2,144]{1,0:T(2,128)(2,1)} %param.11) | copy-start | bytes 1732
  12.3 4.1 %copy-start.1 = (f32[2,144,1152]{2,1,0:T(8,128)S(1)}, f32[2,144,1152]{2,1,0:T(8,128)}, u32[]{:S(2)}) copy-start(f32[2,144,1152]{2,1,0:T(8,128)} %param.13) | copy-start | bytes 3981316
  12.3 4.1 %copy-start.5 = (bf16[2,144,1152]{2,1,0:T(8,128)(2,1)S(1)}, bf16[2,144,1152]{2,1,0:T(8,128)(2,1)}, u32[]{:S(2)}) copy-start(bf16[2,144,1152]{2,1,0:T(8,128)(2,1)} %param.10) | copy-start | bytes 1990660
  14.9 4.4 %collective-permute-start.4 = (bf16[4,144,1152]{2,1,0:T(8,128)(2,1)}, bf16[4,144,1152]{2,1,0:T(8,128)(2,1)}, u32[]{:S(2)}, u32[]{:S(2)}) collective-permute-start(bf16[4,144,1152]{2,1,0:T(8,128)(2,1)} %dynamic-slice_bitcast_fusion.1), channel_id=1, source_target_pairs={{0,1},{1,0},{2,3},{3,2},{4,5},{5,4},{6,7},{7,6},{8,9},{9,8},{10,11... | collective-permute-start | bytes 3981320 | tf_op jit(solution)/shard_map/ppermute | solution.py:251
  21.1 15.7 %slice-start.2 = ((s8[9437184]{0:T(1024)(128)(4,1)}), s8[4194304]{0:T(1024)(128)(4,1)S(1)}, s32[]{:S(2)}) async-start(s8[9437184]{0:T(1024)(128)(4,1)} %bitcast.128), calls=%async_computation.2 | async-start | bytes 8388608
  21.1 15.7 %slice-start.3 = ((s8[9437184]{0:T(1024)(128)(4,1)}), s8[4194304]{0:T(1024)(128)(4,1)S(1)}, s32[]{:S(2)}) async-start(s8[9437184]{0:T(1024)(128)(4,1)} %bitcast.128), calls=%async_computation.3 | async-start | bytes 8388608
  21.1 15.7 %slice-start.4 = ((s8[9437184]{0:T(1024)(128)(4,1)}), s8[1048576]{0:T(1024)(128)(4,1)S(1)}, s32[]{:S(2)}) async-start(s8[9437184]{0:T(1024)(128)(4,1)} %bitcast.128), calls=%async_computation.4 | async-start | bytes 2097152
  31.4 1.5 copy-start.3
  34.0 8.0 %collective-permute-start.8 = (bf16[4,144,1152]{2,1,0:T(8,128)(2,1)}, bf16[4,144,1152]{2,1,0:T(8,128)(2,1)}, u32[]{:S(2)}, u32[]{:S(2)}) collective-permute-start(bf16[4,144,1152]{2,1,0:T(8,128)(2,1)} %dynamic-slice_bitcast_fusion), channel_id=1, source_target_pairs={{0,1},{1,0},{2,3},{3,2},{4,5},{5,4},{6,7},{7,6},{8,9},{9,8},{10,11... | collective-permute-start | bytes 3981320 | tf_op jit(solution)/shard_map/ppermute | solution.py:251
  35.3 66.1 %collective-permute-start = (bf16[2,152,1152]{2,1,0:T(8,128)(2,1)}, bf16[2,152,1152]{2,1,0:T(8,128)(2,1)}, u32[]{:S(2)}, u32[]{:S(2)}) collective-permute-start(bf16[2,152,1152]{2,1,0:T(8,128)(2,1)} %pad_maximum_fusion.2.refs_0_), channel_id=1, source_target_pairs={{0,2},{2,0},{4,6},{6,4},{1,3},{3,1},{5,7},{7,5},{8,10},{10,8},{12,... | collective-permute-start | bytes 2101256 | tf_op jit(solution)/shard_map/ppermute | solution.py:254
  38.1 21.7 %collective-permute-start.5 = (bf16[144,1152]{1,0:T(8,128)(2,1)S(1)}, bf16[144,1152]{1,0:T(8,128)(2,1)S(1)}, u32[]{:S(2)}, u32[]{:S(2)}) collective-permute-start(bf16[144,1152]{1,0:T(8,128)(2,1)S(1)} %get-tuple-element.34), channel_id=1, source_target_pairs={{0,2},{2,0},{4,6},{6,4},{1,3},{3,1},{5,7},{7,5},{8,10},{10,8},{12,... | collective-permute-start | bytes 995336 | tf_op jit(solution)/shard_map/ppermute | solution.py:254
  38.2 31.3 %collective-permute-start.6 = (bf16[144,1152]{1,0:T(8,128)(2,1)S(1)}, bf16[144,1152]{1,0:T(8,128)(2,1)S(1)}, u32[]{:S(2)}, u32[]{:S(2)}) collective-permute-start(bf16[144,1152]{1,0:T(8,128)(2,1)S(1)} %get-tuple-element.33), channel_id=1, source_target_pairs={{0,4},{2,6},{4,0},{6,2},{1,5},{3,7},{5,1},{7,3},{8,12},{10,14},{12... | collective-permute-start | bytes 995336 | tf_op jit(solution)/shard_map/ppermute | solution.py:254
  41.2 28.2 %collective-permute-start.7 = (bf16[144,1152]{1,0:T(8,128)(2,1)S(1)}, bf16[144,1152]{1,0:T(8,128)(2,1)}, u32[]{:S(2)}, u32[]{:S(2)}) collective-permute-start(bf16[144,1152]{1,0:T(8,128)(2,1)S(1)} %get-tuple-element.32), channel_id=1, source_target_pairs={{0,6},{2,4},{4,2},{6,0},{1,7},{3,5},{5,3},{7,1},{8,14},{10,12},{12... | collective-permute-start | bytes 995336 | tf_op jit(solution)/shard_map/ppermute | solution.py:254
  42.0 59.4 %collective-permute-start.1 = (bf16[2,152,1152]{2,1,0:T(8,128)(2,1)}, bf16[2,152,1152]{2,1,0:T(8,128)(2,1)}, u32[]{:S(2)}, u32[]{:S(2)}) collective-permute-start(bf16[2,152,1152]{2,1,0:T(8,128)(2,1)} %pad_maximum_fusion.2.refs_0_), channel_id=1, source_target_pairs={{0,4},{2,6},{4,0},{6,2},{1,5},{3,7},{5,1},{7,3},{8,12},{10,14},{12... | collective-permute-start | bytes 2101256 | tf_op jit(solution)/shard_map/ppermute | solution.py:254
  43.5 55.7 %copy-start.4 = (f32[1,2,144,1152]{3,2,1,0:T(8,128)S(1)}, f32[1,2,144,1152]{3,2,1,0:T(8,128)}, u32[]{:S(2)}) copy-start(f32[1,2,144,1152]{3,2,1,0:T(8,128)} %param.12) | copy-start | bytes 3981316
  59.8 9.7 %copy-start.6 = (bf16[144,1152]{1,0:T(8,128)(2,1)}, bf16[144,1152]{1,0:T(8,128)(2,1)S(1)}, u32[]{:S(2)}) copy-start(bf16[144,1152]{1,0:T(8,128)(2,1)S(1)} %collective-permute-done.5) | copy-start | bytes 995332
  59.8 31.8 %collective-permute-start.10 = (bf16[144,1152]{1,0:T(8,128)(2,1)S(1)}, bf16[144,1152]{1,0:T(8,128)(2,1)S(1)}, u32[]{:S(2)}, u32[]{:S(2)}) collective-permute-start(bf16[144,1152]{1,0:T(8,128)(2,1)S(1)} %get-tuple-element.31), channel_id=1, source_target_pairs={{0,4},{2,6},{4,0},{6,2},{1,5},{3,7},{5,1},{7,3},{8,12},{10,14},{12... | collective-permute-start | bytes 995336 | tf_op jit(solution)/shard_map/ppermute | solution.py:254
  69.4 0.7 copy-start.7
  69.4 29.7 %collective-permute-start.11 = (bf16[144,1152]{1,0:T(8,128)(2,1)S(1)}, bf16[144,1152]{1,0:T(8,128)(2,1)S(1)}, u32[]{:S(2)}, u32[]{:S(2)}) collective-permute-start(bf16[144,1152]{1,0:T(8,128)(2,1)S(1)} %get-tuple-element.30), channel_id=1, source_target_pairs={{0,6},{2,4},{4,2},{6,0},{1,7},{3,5},{5,3},{7,1},{8,14},{10,12},{12... | collective-permute-start | bytes 995336 | tf_op jit(solution)/shard_map/ppermute | solution.py:254
  70.2 29.0 %collective-permute-start.9 = (bf16[144,1152]{1,0:T(8,128)(2,1)S(1)}, bf16[144,1152]{1,0:T(8,128)(2,1)S(1)}, u32[]{:S(2)}, u32[]{:S(2)}) collective-permute-start(bf16[144,1152]{1,0:T(8,128)(2,1)S(1)} %get-tuple-element.29), channel_id=1, source_target_pairs={{0,2},{2,0},{4,6},{6,4},{1,3},{3,1},{5,7},{7,5},{8,10},{10,8},{12,... | collective-permute-start | bytes 995336 | tf_op jit(solution)/shard_map/ppermute | solution.py:254
  91.6 22.7 %collective-permute-start.2 = (bf16[2,152,1152]{2,1,0:T(8,128)(2,1)}, bf16[2,152,1152]{2,1,0:T(8,128)(2,1)}, u32[]{:S(2)}, u32[]{:S(2)}) collective-permute-start(bf16[2,152,1152]{2,1,0:T(8,128)(2,1)} %pad_maximum_fusion.2.refs_0_), channel_id=1, source_target_pairs={{0,6},{2,4},{4,2},{6,0},{1,7},{3,5},{5,3},{7,1},{8,14},{10,12},{12... | collective-permute-start | bytes 2101256 | tf_op jit(solution)/shard_map/ppermute | solution.py:254
  100.7 17.0 %collective-permute-start.12 = (bf16[152,1152]{1,0:T(8,128)(2,1)S(1)}, bf16[152,1152]{1,0:T(8,128)(2,1)}, u32[]{:S(2)}, u32[]{:S(2)}) collective-permute-start(bf16[152,1152]{1,0:T(8,128)(2,1)S(1)} %pad_maximum_fusion.7), channel_id=1, source_target_pairs={{0,1},{1,0},{2,3},{3,2},{4,5},{5,4},{6,7},{7,6},{8,9},{9,8},{10,11... | collective-permute-start | bytes 1050632 | tf_op jit(solution)/shard_map/ppermute | solution.py:251
  117.2 22.5 %collective-permute-start.3 = (bf16[4,2,152,1152]{3,2,1,0:T(8,128)(2,1)}, bf16[4,2,152,1152]{3,2,1,0:T(8,128)(2,1)S(1)}, u32[]{:S(2)}, u32[]{:S(2)}) collective-permute-start(bf16[4,2,152,1152]{3,2,1,0:T(8,128)(2,1)} %lineup.1.mine_ref), channel_id=1, source_target_pairs={{0,1},{1,0},{2,3},{3,2},{4,5},{5,4},{6,7},{7,6},{8,9},{9,8},{10,11... | collective-permute-start | bytes 8405000 | tf_op jit(solution)/shard_map/ppermute | solution.py:251
  119.9 6.3 %collective-permute-start.13 = (bf16[80,1152]{1,0:T(8,128)(2,1)S(1)}, bf16[80,1152]{1,0:T(8,128)(2,1)S(1)}, u32[]{:S(2)}, u32[]{:S(2)}) collective-permute-start(bf16[80,1152]{1,0:T(8,128)(2,1)S(1)} %get-tuple-element.56), channel_id=1, source_target_pairs={{0,32},{32,0},{64,96},{96,64},{1,33},{33,1},{65,97},{97,65},{2,34}... | collective-permute-start | bytes 552968 | tf_op jit(solution)/shard_map/ppermute | solution.py:254
  121.2 11.2 %collective-permute-start.14 = (bf16[80,1152]{1,0:T(8,128)(2,1)S(1)}, bf16[80,1152]{1,0:T(8,128)(2,1)S(1)}, u32[]{:S(2)}, u32[]{:S(2)}) collective-permute-start(bf16[80,1152]{1,0:T(8,128)(2,1)S(1)} %get-tuple-element.57), channel_id=1, source_target_pairs={{0,64},{32,96},{64,0},{96,32},{1,65},{33,97},{65,1},{97,33},{2,66}... | collective-permute-start | bytes 552968 | tf_op jit(solution)/shard_map/ppermute | solution.py:254
  123.7 10.9 %collective-permute-start.15 = (bf16[80,1152]{1,0:T(8,128)(2,1)S(1)}, bf16[80,1152]{1,0:T(8,128)(2,1)S(1)}, u32[]{:S(2)}, u32[]{:S(2)}) collective-permute-start(bf16[80,1152]{1,0:T(8,128)(2,1)S(1)} %get-tuple-element.58), channel_id=1, source_target_pairs={{0,96},{32,64},{64,32},{96,0},{1,97},{33,65},{65,33},{97,1},{2,98}... | collective-permute-start | bytes 552968 | tf_op jit(solution)/shard_map/ppermute | solution.py:254
  134.8 5.3 %collective-permute-start.16 = (bf16[80,1152]{1,0:T(8,128)(2,1)S(1)}, bf16[80,1152]{1,0:T(8,128)(2,1)S(1)}, u32[]{:S(2)}, u32[]{:S(2)}) collective-permute-start(bf16[80,1152]{1,0:T(8,128)(2,1)S(1)} %pad_maximum_fusion.3), channel_id=1, source_target_pairs={{0,8},{8,0},{16,24},{24,16},{1,9},{9,1},{17,25},{25,17},{2,10},{10... | collective-permute-start | bytes 552968 | tf_op jit(solution)/shard_map/ppermute | solution.py:254
  136.5 10.7 %collective-permute-start.17 = (bf16[80,1152]{1,0:T(8,128)(2,1)S(1)}, bf16[80,1152]{1,0:T(8,128)(2,1)S(1)}, u32[]{:S(2)}, u32[]{:S(2)}) collective-permute-start(bf16[80,1152]{1,0:T(8,128)(2,1)S(1)} %pad_maximum_fusion.3), channel_id=1, source_target_pairs={{0,16},{8,24},{16,0},{24,8},{1,17},{9,25},{17,1},{25,9},{2,18},{10... | collective-permute-start | bytes 552968 | tf_op jit(solution)/shard_map/ppermute | solution.py:254
  139.8 10.4 %collective-permute-start.18 = (bf16[80,1152]{1,0:T(8,128)(2,1)S(1)}, bf16[80,1152]{1,0:T(8,128)(2,1)S(1)}, u32[]{:S(2)}, u32[]{:S(2)}) collective-permute-start(bf16[80,1152]{1,0:T(8,128)(2,1)S(1)} %pad_maximum_fusion.3), channel_id=1, source_target_pairs={{0,24},{8,16},{16,8},{24,0},{1,25},{9,17},{17,9},{25,1},{2,26},{10... | collective-permute-start | bytes 552968 | tf_op jit(solution)/shard_map/ppermute | solution.py:254
  139.8 21.0 %copy-start.2 = (bf16[4,2,152,1152]{3,2,1,0:T(8,128)(2,1)}, bf16[4,2,152,1152]{3,2,1,0:T(8,128)(2,1)S(1)}, u32[]{:S(2)}) copy-start(bf16[4,2,152,1152]{3,2,1,0:T(8,128)(2,1)S(1)} %collective-permute-done.3.theirs_ref) | copy-start | bytes 8404996
  150.3 4.3 %collective-permute-start.19 = (bf16[72,1152]{1,0:T(8,128)(2,1)S(1)}, bf16[72,1152]{1,0:T(8,128)(2,1)S(1)}, u32[]{:S(2)}, u32[]{:S(2)}) collective-permute-start(bf16[72,1152]{1,0:T(8,128)(2,1)S(1)} %add_convert_fusion.6.refs_0_), channel_id=1, source_target_pairs={{0,32},{32,0},{64,96},{96,64},{1,33},{33,1},{65,97},{97,65},{2,34}... | collective-permute-start | bytes 497672 | tf_op jit(solution)/shard_map/ppermute | solution.py:254
  150.4 7.4 %collective-permute-start.20 = (bf16[72,1152]{1,0:T(8,128)(2,1)S(1)}, bf16[72,1152]{1,0:T(8,128)(2,1)S(1)}, u32[]{:S(2)}, u32[]{:S(2)}) collective-permute-start(bf16[72,1152]{1,0:T(8,128)(2,1)S(1)} %add_convert_fusion.6.refs_0_), channel_id=1, source_target_pairs={{0,64},{32,96},{64,0},{96,32},{1,65},{33,97},{65,1},{97,33},{2,66}... | collective-permute-start | bytes 497672 | tf_op jit(solution)/shard_map/ppermute | solution.py:254
  151.7 9.1 %collective-permute-start.21 = (bf16[72,1152]{1,0:T(8,128)(2,1)S(1)}, bf16[72,1152]{1,0:T(8,128)(2,1)S(1)}, u32[]{:S(2)}, u32[]{:S(2)}) collective-permute-start(bf16[72,1152]{1,0:T(8,128)(2,1)S(1)} %add_convert_fusion.6.refs_0_), channel_id=1, source_target_pairs={{0,96},{32,64},{64,32},{96,0},{1,97},{33,65},{65,33},{97,1},{2,98}... | collective-permute-start | bytes 497672 | tf_op jit(solution)/shard_map/ppermute | solution.py:254
  161.7 4.0 %collective-permute-start.22 = (bf16[40,1408]{1,0:T(8,128)(2,1)S(1)}, bf16[40,1408]{1,0:T(8,128)(2,1)S(1)}, u32[]{:S(2)}, u32[]{:S(2)}) collective-permute-start(bf16[40,1408]{1,0:T(8,128)(2,1)S(1)} %get-tuple-element.19.refs_0_), channel_id=1, source_target_pairs={{0,2},{2,0},{4,6},{6,4},{1,3},{3,1},{5,7},{7,5},{8,10},{10,8},{12,... | collective-permute-start | bytes 337928 | tf_op jit(solution)/shard_map/ppermute | solution.py:254
  161.8 6.1 %collective-permute-start.23 = (bf16[40,1408]{1,0:T(8,128)(2,1)S(1)}, bf16[40,1408]{1,0:T(8,128)(2,1)S(1)}, u32[]{:S(2)}, u32[]{:S(2)}) collective-permute-start(bf16[40,1408]{1,0:T(8,128)(2,1)S(1)} %get-tuple-element.19.refs_0_), channel_id=1, source_target_pairs={{0,4},{2,6},{4,0},{6,2},{1,5},{3,7},{5,1},{7,3},{8,12},{10,14},{12... | collective-permute-start | bytes 337928 | tf_op jit(solution)/shard_map/ppermute | solution.py:254
  162.9 7.3 %collective-permute-start.24 = (bf16[40,1408]{1,0:T(8,128)(2,1)S(1)}, bf16[40,1408]{1,0:T(8,128)(2,1)S(1)}, u32[]{:S(2)}, u32[]{:S(2)}) collective-permute-start(bf16[40,1408]{1,0:T(8,128)(2,1)S(1)} %get-tuple-element.19.refs_0_), channel_id=1, source_target_pairs={{0,6},{2,4},{4,2},{6,0},{1,7},{3,5},{5,3},{7,1},{8,14},{10,12},{12... | collective-permute-start | bytes 337928 | tf_op jit(solution)/shard_map/ppermute | solution.py:254
  173.4 11.5 %collective-permute-start.29 = (f32[8,1152]{1,0:T(8,128)S(1)}, f32[8,1152]{1,0:T(8,128)}, u32[]{:S(2)}, u32[]{:S(2)}) collective-permute-start(f32[8,1152]{1,0:T(8,128)S(1)} %get-tuple-element.24), channel_id=1, source_target_pairs={{0,1},{1,0},{2,3},{3,2},{4,5},{5,4},{6,7},{7,6},{8,9},{9,8},{10,11... | collective-permute-start | bytes 110600 | tf_op jit(solution)/shard_map/ppermute | solution.py:251
  181.0 5.2 %collective-permute-start.25 = (bf16[32,2176]{1,0:T(8,128)(2,1)S(1)}, bf16[32,2176]{1,0:T(8,128)(2,1)S(1)}, u32[]{:S(2)}, u32[]{:S(2)}) collective-permute-start(bf16[32,2176]{1,0:T(8,128)(2,1)S(1)} %get-tuple-element.21.refs_0_), channel_id=1, source_target_pairs={{0,2},{2,0},{4,6},{6,4},{1,3},{3,1},{5,7},{7,5},{8,10},{10,8},{12,... | collective-permute-start | bytes 417800 | tf_op jit(solution)/shard_map/ppermute | solution.py:254
  181.1 10.2 %collective-permute-start.26 = (bf16[32,2176]{1,0:T(8,128)(2,1)S(1)}, bf16[32,2176]{1,0:T(8,128)(2,1)S(1)}, u32[]{:S(2)}, u32[]{:S(2)}) collective-permute-start(bf16[32,2176]{1,0:T(8,128)(2,1)S(1)} %get-tuple-element.21.refs_0_), channel_id=1, source_target_pairs={{0,4},{2,6},{4,0},{6,2},{1,5},{3,7},{5,1},{7,3},{8,12},{10,14},{12... | collective-permute-start | bytes 417800 | tf_op jit(solution)/shard_map/ppermute | solution.py:254
  184.5 9.3 %collective-permute-start.27 = (bf16[32,2176]{1,0:T(8,128)(2,1)S(1)}, bf16[32,2176]{1,0:T(8,128)(2,1)S(1)}, u32[]{:S(2)}, u32[]{:S(2)}) collective-permute-start(bf16[32,2176]{1,0:T(8,128)(2,1)S(1)} %get-tuple-element.21.refs_0_), channel_id=1, source_target_pairs={{0,6},{2,4},{4,2},{6,0},{1,7},{3,5},{5,3},{7,1},{8,14},{10,12},{12... | collective-permute-start | bytes 417800 | tf_op jit(solution)/shard_map/ppermute | solution.py:254
  200.2 6.6 %slice-start = ((s8[5308416]{0:T(1024)(128)(4,1)}), s8[4194304]{0:T(1024)(128)(4,1)S(1)}, s32[]{:S(2)}) async-start(s8[5308416]{0:T(1024)(128)(4,1)} %bitcast.123), calls=%async_computation | async-start | bytes 8388608
  200.2 3.9 %collective-permute-start.28 = (f32[32,2304]{1,0:T(8,128)S(1)}, f32[32,2304]{1,0:T(8,128)S(1)}, u32[]{:S(2)}, u32[]{:S(2)}) collective-permute-start(f32[32,2304]{1,0:T(8,128)S(1)} %pad_maximum_fusion.14), channel_id=1, source_target_pairs={{0,1},{1,0},{2,3},{3,2},{4,5},{5,4},{6,7},{7,6},{8,9},{9,8},{10,11... | collective-permute-start | bytes 884744 | tf_op jit(solution)/shard_map/ppermute | solution.py:251
  204.4 2.3 %slice-start.1 = ((s8[5308416]{0:T(1024)(128)(4,1)}), s8[1114112]{0:T(1024)(128)(4,1)S(1)}, s32[]{:S(2)}) async-start(s8[5308416]{0:T(1024)(128)(4,1)} %bitcast.123), calls=%async_computation.1 | async-start | bytes 2228224

commit v2 on v1

--- a/solution.py
+++ b/solution.py
@@ -32,7 +32,7 @@
 
 
 def paired(parts):
-    return (parts[0] + parts[1]) + (parts[2] + parts[3])
+    return (parts[0] + parts[2]) + (parts[1] + parts[3])
 
 
 def split3(value):
@@ -253,6 +253,9 @@
     def trade(value, axis, k):
         return lax.ppermute(value, axis, [(i, i ^ k) for i in range(4)])
 
+    def from_back(value, axis, k):
+        return lax.ppermute(value, axis, ring(4, k))
+
     def everyone(value, axis):
         return [value] + [trade(value, axis, k) for k in (1, 2, 3)]
 
@@ -276,10 +279,11 @@
     mine = lineup(ypos.astype(jnp.int32)[None], parts)
     theirs = swap(mine)
     old = assemble(core.astype(jnp.int32)[None], mine, theirs, rows)
-    tails = [stack[:, :, rows : rows + 2, :rows].astype(F32) for stack in (mine, theirs)]
-    tails = [tail[:, :, 0] - 0.45 * tail[:, :, 1] for tail in tails]
-    even, odd = jnp.where(core == 0, *tails), jnp.where(core == 0, *tails[::-1])
-    old_b = jnp.stack([even, odd], 1).transpose(2, 0, 1, 3).reshape(layers, width)
+    tail = mine[:, :, rows : rows + 2, :rows].astype(F32)
+    tail = tail[:, :, 0] - 0.45 * tail[:, :, 1]
+    even, odd = jnp.where(core == 0, tail, 0.0), jnp.where(core == 0, 0.0, tail)
+    pieces = [side[j] for j in range(ys) for side in (even, odd)]
+    half_b = jnp.concatenate(pieces, -1)
 
     def chip_blocks(layer, after=None):
         x, y = inputs, out_grads
@@ -290,10 +294,11 @@
         got = swap(
             pick(part.reshape(ys, cores, rows, width), 1 - core, 1)
         )
+        keep = lax.optimization_barrier(pick(part.reshape(ys, cores, rows, width), core, 1))
         blocks = []
         for k in range(4):
             there = ypos ^ k
-            blocks.append(pick(part, there * cores + core).astype(F32) + pick(got, there).astype(F32))
+            blocks.append(pick(keep, there).astype(F32) + pick(got, there).astype(F32))
         return blocks[0], [b.astype(BF) for b in blocks[1:]]
 
     def merge(layer, own, blocks):
@@ -324,12 +329,13 @@
 
     parts = []
     for k in (1, 2, 3):
-        block = loaded(pick(both, xpos ^ k))
-        parts.append(trade(block, "x", k))
+        block = loaded(pick(both, (xpos + k) % 4))
+        parts.append(from_back(block, "x", k))
     main = paired([pick(both, xpos)] + [p[:half].astype(F32) for p in parts])
     bias = paired([from_hi_lo(p) for p in [bias_rows] + [p[half:] for p in parts]])
     bias_rows = hi_lo(bias)
-    parts = everyone(loaded(main), "z")
+    block = loaded(main)
+    parts = [block] + [from_back(block, "z", k) for k in (1, 2, 3)]
     main = paired([p[:half].astype(F32) for p in parts]).astype(BF)
     bias = paired([from_hi_lo(p[half:]) for p in parts])
     parts = everyone(main, "x")
@@ -346,12 +352,14 @@
         scratch=(pltpu.VMEM((384, width), BF), pltpu.SemaphoreType.DMA),
     )(*parts, total)
     parts = everyone(packed, "y")
+    bias_rows = jnp.concatenate([bias_rows[:1], half_b, bias_rows[3:]], 0)
     other = swap(bias_rows)
     bias = jnp.stack([jnp.where(core == l, bias_rows[0], other[0]) for l in range(layers)])
     bias_grad = bias * (scale / reps)
     grp = ypos * cores + core
     bias_own = lax.dynamic_slice_in_dim(bias_grad, grp * rows, rows, 1)
     new_bias_momenta = 0.9 * bias_momenta + bias_own
+    old_b = bias_rows[1:3] + other[1:3]
     new_biases = (old_b - 0.5 * bias_grad).astype(BF)
     q, zmat = in_vmem(third_kernel, (shape(rank, width, of=F32), shape(rank, rank, of=F32)))(*parts)
     at = width + 256

time: 212 us -> 202 us (0.953)
  waiting for transfers between devices: 103 us -> 91.6 us
  starting transfers between devices: 36.2 us -> 45.5 us
  other arithmetic: 18.1 us -> 12.7 us
    ppermute x24 -> x18, waiting for transfers between devices: 100 us -> 75.3 us  [trade(): return lax.ppermute(value, axis, [(i, i ^ k) for i in range(4)])]
    ppermute x0 -> x6, waiting for transfers between devices: none -> 14.6 us  [from_back(): return lax.ppermute(value, axis, ring(4, k))]
    ppermute x0 -> x6, starting transfers between devices: none -> 10.4 us  [from_back(): return lax.ppermute(value, axis, ring(4, k))]
    ppermute x24 -> x18, starting transfers between devices: 30.5 us -> 21.8 us  [trade(): return lax.ppermute(value, axis, [(i, i ^ k) for i in range(4)])]
    ppermute x6, starting transfers between devices: 5.66 us -> 13.4 us  [swap(): return lax.ppermute(value, 'core', ring(cores, 1))]
  transfers between devices with their start and end apart: 30 -> 30, of which waited for: 19 -> 16; matrix products, arithmetic and copies ran while one was open for 7% -> 5% of each run, Pallas kernels for 4% -> 6%
where the time goes in v2:
time: 202 us
  waiting for transfers between devices  91.6 us (45%)
  starting transfers between devices  45.5 us (23%)
  matrix products  28.6 us (14%)
  Pallas kernels  14.6 us (7%)
  other arithmetic  12.7 us (6%)
  local copies, waits for them, and re-layouts  7.59 us (4%)
    ppermute x18, waiting for transfers between devices, trade(): return lax.ppermute(value, axis, [(i, i ^ k) for i in range(4)])  75.3 us
    dot_general x2, matrix products, chip_blocks(): jnp.einsum('tr,te->re', x[layer], y[layer], preferred_element_type=F32)  21.9 us
    ppermute x18, starting transfers between devices, trade(): return lax.ppermute(value, axis, [(i, i ^ k) for i in range(4)])  21.8 us
    ppermute x6, waiting for transfers between devices, from_back(): return lax.ppermute(value, axis, ring(4, k))  14.6 us
    ppermute x6, starting transfers between devices, swap(): return lax.ppermute(value, 'core', ring(cores, 1))  13.4 us
    ppermute x6, starting transfers between devices, from_back(): return lax.ppermute(value, axis, ring(4, k))  10.4 us
    pallas_call x3, Pallas kernels, call(): pl.pallas_call(kernel, out_shape=outs, in_specs=[smem] * scalars + [vmem]...  6.19 us
    pallas_call x1, Pallas kernels, assemble(): pl.pallas_call(assemble_kernel, out_shape=jax.ShapeDtypeStruct((layers, w...  5.37 us
  transfers between devices with their start and end apart: 30, of which 16 were waited for; matrix products, arithmetic and copies ran while one was open for 5% of the time, Pallas kernels for 6%

profile of v2, /device:TPU:1, one launch (start us, length us, event | category | flops | bytes accessed | tf_op | source)
XLA Modules:
  0.0 201.7 jit_solution(10822106483826218399)
XLA Ops:
  0.7 11.7 %convolution_convert_fusion.1 = bf16[1152,1152]{1,0:T(8,128)(2,1)} fusion(bf16[2,2048,1152]{2,1,0:T(8,128)(2,1)} %param.9, bf16[2,2048,1152]{2,1,0:T(8,128)(2,1)} %param.8), kind=kOutput, calls=%fused_computation.4 | convolution fusion | flops 5437145088 | bytes 12091392 | tf_op jit(solution)/shard_map/tr,te->re/dot_general | solution.py:292
  12.3 3.1 %dynamic-slice_bitcast_fusion.3 = (bf16[4,144,1152]{2,1,0:T(8,128)(2,1)S(1)}, bf16[4,144,1152]{2,1,0:T(8,128)(2,1)}) fusion(bf16[4,2,144,1152]{3,2,1,0:T(8,128)(2,1)} %bitcast.148, s32[]{:T(128)S(6)} %select_n.190, s32[]{:T(128)S(6)} %select_n.192), kind=kLoop, calls=%fused_computation.26 | loop fusion | bytes 5308424 | tf_op jit(solution)/shard_map/jit(dynamic_index_in_dim)/squeeze | solution.py:21
  15.4 1.4 collective-permute-start.4
  16.9 1.2 subtract_convert_fusion.1
  18.1 1.7 collective-permute-done.4
  19.8 2.3 %fusion.26 = (bf16[144,1152]{1,0:T(8,128)(2,1)}, bf16[144,1152]{1,0:T(8,128)(2,1)}, bf16[144,1152]{1,0:T(8,128)(2,1)S(1)}) fusion(bf16[4,144,1152]{2,1,0:T(8,128)(2,1)} %collective-permute-done.4, s32[]{:T(128)S(6)} %select_n.195, bf16[4,144,1152]{2,1,0:T(8,128)(2,1)S(1)} %get-tuple-element.37, s32[]{:T(128)S(6)} %select_n.194, s32[]{:T(128)S(6)} %select_n.193), kind=kLoop, calls=%fused_computation.62 | loop fusion | flops 1990656 | bytes 2985996 | tf_op jit(solution)/shard_map/convert_element_type | solution.py:302
  22.1 10.3 %convolution_convert_fusion = bf16[1152,1152]{1,0:T(8,128)(2,1)S(1)} fusion(bf16[2,2048,1152]{2,1,0:T(8,128)(2,1)} %param.9, bf16[2,2048,1152]{2,1,0:T(8,128)(2,1)} %param.8), kind=kOutput, calls=%fused_computation.3 | convolution fusion | flops 5437145088 | bytes 12091392 | tf_op jit(solution)/shard_map/tr,te->re/dot_general | solution.py:292
  32.4 1.3 dynamic-slice_bitcast_fusion.1
  35.0 2.9 %collective-permute-start.2 = (bf16[2,152,1152]{2,1,0:T(8,128)(2,1)}, bf16[2,152,1152]{2,1,0:T(8,128)(2,1)}, u32[]{:S(2)}, u32[]{:S(2)}) collective-permute-start(bf16[2,152,1152]{2,1,0:T(8,128)(2,1)} %pad_maximum_fusion.2.refs_0_), channel_id=1, source_target_pairs={{0,6},{2,4},{4,2},{6,0},{1,7},{3,5},{5,3},{7,1},{8,14},{10,12},{12... | collective-permute-start | bytes 2101256 | tf_op jit(solution)/shard_map/ppermute | solution.py:254
  37.9 1.3 convert_reduce_fusion
  39.3 1.6 collective-permute-start.6
  40.9 1.6 collective-permute-start.5
  43.2 1.4 fusion.27
  44.7 38.4 %collective-permute-done.7 = bf16[144,1152]{1,0:T(8,128)(2,1)} collective-permute-done((bf16[144,1152]{1,0:T(8,128)(2,1)}, bf16[144,1152]{1,0:T(8,128)(2,1)}, u32[]{:S(2)}, u32[]{:S(2)}) %collective-permute-start.7) | collective-permute-done | bytes 331808 | tf_op jit(solution)/shard_map/ppermute | solution.py:254
  83.0 2.5 %collective-permute-start.11 = (bf16[144,1152]{1,0:T(8,128)(2,1)S(1)}, bf16[144,1152]{1,0:T(8,128)(2,1)S(1)}, u32[]{:S(2)}, u32[]{:S(2)}) collective-permute-start(bf16[144,1152]{1,0:T(8,128)(2,1)S(1)} %get-tuple-element.30), channel_id=1, source_target_pairs={{0,6},{2,4},{4,2},{6,0},{1,7},{3,5},{5,3},{7,1},{8,14},{10,12},{12... | collective-permute-start | bytes 995336 | tf_op jit(solution)/shard_map/ppermute | solution.py:254
  85.5 1.3 collective-permute-start.10
  86.8 1.5 fusion.16
  88.3 3.0 %collective-permute-done.9 = bf16[144,1152]{1,0:T(8,128)(2,1)S(1)} collective-permute-done((bf16[144,1152]{1,0:T(8,128)(2,1)S(1)}, bf16[144,1152]{1,0:T(8,128)(2,1)S(1)}, u32[]{:S(2)}, u32[]{:S(2)}) %collective-permute-start.9) | collective-permute-done | bytes 331808 | tf_op jit(solution)/shard_map/ppermute | solution.py:254
  92.3 8.2 %collective-permute-done.10 = bf16[144,1152]{1,0:T(8,128)(2,1)S(1)} collective-permute-done((bf16[144,1152]{1,0:T(8,128)(2,1)S(1)}, bf16[144,1152]{1,0:T(8,128)(2,1)S(1)}, u32[]{:S(2)}, u32[]{:S(2)}) %collective-permute-start.10) | collective-permute-done | bytes 331808 | tf_op jit(solution)/shard_map/ppermute | solution.py:254
  100.5 1.4 fusion.17
  102.0 3.8 %collective-permute-start.12 = (bf16[152,1152]{1,0:T(8,128)(2,1)S(1)}, bf16[152,1152]{1,0:T(8,128)(2,1)S(1)}, u32[]{:S(2)}, u32[]{:S(2)}) collective-permute-start(bf16[152,1152]{1,0:T(8,128)(2,1)S(1)} %pad_maximum_fusion.7), channel_id=1, source_target_pairs={{0,1},{1,0},{2,3},{3,2},{4,5},{5,4},{6,7},{7,6},{8,9},{9,8},{10,11... | collective-permute-start | bytes 1050632 | tf_op jit(solution)/shard_map/ppermute | solution.py:251
  105.9 7.7 %collective-permute-done.refs_1_ = bf16[2,152,1152]{2,1,0:T(8,128)(2,1)S(1)} collective-permute-done((bf16[2,152,1152]{2,1,0:T(8,128)(2,1)}, bf16[2,152,1152]{2,1,0:T(8,128)(2,1)S(1)}, u32[]{:S(2)}, u32[]{:S(2)}) %collective-permute-start) | collective-permute-done | bytes 700448 | tf_op jit(solution)/shard_map/ppermute | solution.py:254
  114.4 3.0 %lineup.1.mine_ref = bf16[4,2,152,1152]{3,2,1,0:T(8,128)(2,1)} custom-call(s32[1]{0:T(128)} %bitcast.1.ypos_ref, bf16[2,152,1152]{2,1,0:T(8,128)(2,1)} %pad_maximum_fusion.2.refs_0_, bf16[2,152,1152]{2,1,0:T(8,128)(2,1)} %copy-done.5, bf16[2,152,1152]{2,1,0:T(8,128)(2,1)} %collective-permute-done.1.refs_2_, bf16[2,152,1152]{2,1,0:T(8,128)(2,1)} %collective-permute-done.2.refs_3_), custom_call_target="tpu_custom_call" | custom-call | tf_op jit(solution)/shard_map/lineup/pallas_call | solution.py:165
  118.2 1.9 collective-permute-start.3
  120.5 2.7 %collective-permute-start.13 = (bf16[80,1152]{1,0:T(8,128)(2,1)S(1)}, bf16[80,1152]{1,0:T(8,128)(2,1)S(1)}, u32[]{:S(2)}, u32[]{:S(2)}) collective-permute-start(bf16[80,1152]{1,0:T(8,128)(2,1)S(1)} %get-tuple-element.58), channel_id=1, source_target_pairs={{0,64},{32,96},{64,0},{96,32},{1,65},{33,97},{65,1},{97,33},{2,66}... | collective-permute-start | bytes 552968 | tf_op jit(solution)/shard_map/ppermute | solution.py:257
  123.5 2.4 %collective-permute-start.15 = (bf16[80,1152]{1,0:T(8,128)(2,1)S(1)}, bf16[80,1152]{1,0:T(8,128)(2,1)S(1)}, u32[]{:S(2)}, u32[]{:S(2)}) collective-permute-start(bf16[80,1152]{1,0:T(8,128)(2,1)S(1)} %get-tuple-element.60), channel_id=1, source_target_pairs={{0,96},{32,0},{64,32},{96,64},{1,97},{33,1},{65,33},{97,65},{2,98}... | collective-permute-start | bytes 552968 | tf_op jit(solution)/shard_map/ppermute | solution.py:257
  125.9 2.4 %collective-permute-done.13 = bf16[80,1152]{1,0:T(8,128)(2,1)S(1)} collective-permute-done((bf16[80,1152]{1,0:T(8,128)(2,1)S(1)}, bf16[80,1152]{1,0:T(8,128)(2,1)S(1)}, u32[]{:S(2)}, u32[]{:S(2)}) %collective-permute-start.13) | collective-permute-done | bytes 184352 | tf_op jit(solution)/shard_map/ppermute | solution.py:257
  128.2 4.4 %collective-permute-done.14 = bf16[80,1152]{1,0:T(8,128)(2,1)S(1)} collective-permute-done((bf16[80,1152]{1,0:T(8,128)(2,1)S(1)}, bf16[80,1152]{1,0:T(8,128)(2,1)S(1)}, u32[]{:S(2)}, u32[]{:S(2)}) %collective-permute-start.14) | collective-permute-done | bytes 184352 | tf_op jit(solution)/shard_map/ppermute | solution.py:257
  132.8 3.7 %collective-permute-start.18 = (bf16[80,1152]{1,0:T(8,128)(2,1)S(1)}, bf16[80,1152]{1,0:T(8,128)(2,1)S(1)}, u32[]{:S(2)}, u32[]{:S(2)}) collective-permute-start(bf16[80,1152]{1,0:T(8,128)(2,1)S(1)} %pad_maximum_fusion.3), channel_id=1, source_target_pairs={{0,24},{8,0},{16,8},{24,16},{1,25},{9,1},{17,9},{25,17},{2,26},{10... | collective-permute-start | bytes 552968 | tf_op jit(solution)/shard_map/ppermute | solution.py:257
  136.5 1.3 collective-permute-start.16
  137.8 2.1 %collective-permute-done.18 = bf16[80,1152]{1,0:T(8,128)(2,1)S(1)} collective-permute-done((bf16[80,1152]{1,0:T(8,128)(2,1)S(1)}, bf16[80,1152]{1,0:T(8,128)(2,1)S(1)}, u32[]{:S(2)}, u32[]{:S(2)}) %collective-permute-start.18) | collective-permute-done | bytes 184352 | tf_op jit(solution)/shard_map/ppermute | solution.py:257
  139.9 4.4 %collective-permute-done.17 = bf16[80,1152]{1,0:T(8,128)(2,1)S(1)} collective-permute-done((bf16[80,1152]{1,0:T(8,128)(2,1)S(1)}, bf16[80,1152]{1,0:T(8,128)(2,1)S(1)}, u32[]{:S(2)}, u32[]{:S(2)}) %collective-permute-start.17) | collective-permute-done | bytes 184352 | tf_op jit(solution)/shard_map/ppermute | solution.py:257
  144.4 1.3 collective-permute-done.16
  145.8 3.9 %collective-permute-start.21 = (bf16[72,1152]{1,0:T(8,128)(2,1)S(1)}, bf16[72,1152]{1,0:T(8,128)(2,1)S(1)}, u32[]{:S(2)}, u32[]{:S(2)}) collective-permute-start(bf16[72,1152]{1,0:T(8,128)(2,1)S(1)} %add_convert_fusion.6.refs_0_), channel_id=1, source_target_pairs={{0,96},{32,64},{64,32},{96,0},{1,97},{33,65},{65,33},{97,1},{2,98}... | collective-permute-start | bytes 497672 | tf_op jit(solution)/shard_map/ppermute | solution.py:254
  150.4 6.3 %collective-permute-done.21.refs_3_ = bf16[72,1152]{1,0:T(8,128)(2,1)S(1)} collective-permute-done((bf16[72,1152]{1,0:T(8,128)(2,1)S(1)}, bf16[72,1152]{1,0:T(8,128)(2,1)S(1)}, u32[]{:S(2)}, u32[]{:S(2)}) %collective-permute-start.21) | collective-permute-done | bytes 165920 | tf_op jit(solution)/shard_map/ppermute | solution.py:254
  157.5 2.6 %collective-permute-start.24 = (bf16[40,1408]{1,0:T(8,128)(2,1)S(1)}, bf16[40,1408]{1,0:T(8,128)(2,1)S(1)}, u32[]{:S(2)}, u32[]{:S(2)}) collective-permute-start(bf16[40,1408]{1,0:T(8,128)(2,1)S(1)} %get-tuple-element.19.refs_0_), channel_id=1, source_target_pairs={{0,6},{2,4},{4,2},{6,0},{1,7},{3,5},{5,3},{7,1},{8,14},{10,12},{12... | collective-permute-start | bytes 337928 | tf_op jit(solution)/shard_map/ppermute | solution.py:254
  161.0 2.1 %collective-permute-done.24.refs_3_ = bf16[40,1408]{1,0:T(8,128)(2,1)S(1)} collective-permute-done((bf16[40,1408]{1,0:T(8,128)(2,1)S(1)}, bf16[40,1408]{1,0:T(8,128)(2,1)S(1)}, u32[]{:S(2)}, u32[]{:S(2)}) %collective-permute-start.24) | collective-permute-done | bytes 112672 | tf_op jit(solution)/shard_map/ppermute | solution.py:254
  163.1 2.3 %collective-permute-done.23.refs_2_ = bf16[40,1408]{1,0:T(8,128)(2,1)S(1)} collective-permute-done((bf16[40,1408]{1,0:T(8,128)(2,1)S(1)}, bf16[40,1408]{1,0:T(8,128)(2,1)S(1)}, u32[]{:S(2)}, u32[]{:S(2)}) %collective-permute-start.23) | collective-permute-done | bytes 112672 | tf_op jit(solution)/shard_map/ppermute | solution.py:254
  165.3 3.2 %shard_map.120 = (bf16[32,2176]{1,0:T(8,128)(2,1)S(1)}, f32[8,1152]{1,0:T(8,128)S(1)}) custom-call(bf16[40,1408]{1,0:T(8,128)(2,1)S(1)} %get-tuple-element.19.refs_0_, bf16[40,1408]{1,0:T(8,128)(2,1)S(1)} %collective-permute-done.22.refs_1_, bf16[40,1408]{1,0:T(8,128)(2,1)S(1)} %collective-permute-done.23.refs_2_, ...), custom_call_target="tpu_custom_call" | custom-call | tf_op jit(solution)/shard_map/pallas_call | solution.py:210
  168.6 4.4 %collective-permute-start.29 = (f32[8,1152]{1,0:T(8,128)S(1)}, f32[8,1152]{1,0:T(8,128)S(1)}, u32[]{:S(2)}, u32[]{:S(2)}) collective-permute-start(f32[8,1152]{1,0:T(8,128)S(1)} %pad_maximum_fusion.17), channel_id=1, source_target_pairs={{0,1},{1,0},{2,3},{3,2},{4,5},{5,4},{6,7},{7,6},{8,9},{9,8},{10,11... | collective-permute-start | bytes 110600 | tf_op jit(solution)/shard_map/ppermute | solution.py:251
  173.0 5.4 %assemble.1 = bf16[2,1152,1152]{2,1,0:T(8,128)(2,1)} custom-call(s32[1]{0:T(128)} %bitcast.core_ref, bf16[4,2,152,1152]{3,2,1,0:T(8,128)(2,1)} %lineup.1.mine_ref, bf16[4,2,152,1152]{3,2,1,0:T(8,128)(2,1)} %collective-permute-done.3.theirs_ref), custom_call_target="tpu_custom_call" | custom-call | tf_op jit(solution)/shard_map/assemble/pallas_call | solution.py:192
  178.4 1.5 collective-permute-start.27
  180.2 1.5 collective-permute-start.25
  181.7 5.9 %collective-permute-done.27.refs_3_ = bf16[32,2176]{1,0:T(8,128)(2,1)S(1)} collective-permute-done((bf16[32,2176]{1,0:T(8,128)(2,1)S(1)}, bf16[32,2176]{1,0:T(8,128)(2,1)S(1)}, u32[]{:S(2)}, u32[]{:S(2)}) %collective-permute-start.27) | collective-permute-done | bytes 139296 | tf_op jit(solution)/shard_map/ppermute | solution.py:254
  188.3 2.1 %shard_map.121 = (f32[32,1152]{1,0:T(8,128)S(1)}, f32[32,32]{1,0:T(8,128)S(1)}) custom-call(bf16[32,2176]{1,0:T(8,128)(2,1)S(1)} %get-tuple-element.21.refs_0_, bf16[32,2176]{1,0:T(8,128)(2,1)S(1)} %collective-permute-done.25.refs_1_, bf16[32,2176]{1,0:T(8,128)(2,1)S(1)} %collective-permute-done.26.refs_2_, bf16[32,2176]{1,0:T(8,128)(2,1)S(1)} %collective-permute-done.27.refs_3_), custom_call_target="tpu_custom_call" | custom-call | tf_op jit(solution)/shard_map/pallas_call | solution.py:210
  190.8 1.5 collective-permute-start.28
  195.3 2.2 %multiply_add_fusion = (f32[2,144,1152]{2,1,0:T(8,128)}, f32[1,2,144,1152]{3,2,1,0:T(8,128)}) fusion(f32[2,144,1152]{2,1,0:T(8,128)S(1)} %copy-done.2, f32[1,144,1152]{2,1,0:T(8,128)S(1)} %fusion.17, f32[1,144,1152]{2,1,0:T(8,128)S(1)} %bitcast.143, bf16[2,192,1152]{2,1,0:T(8,128)(2,1)S(1)} %constant_dynamic-update-slice_fusion.5, ...), kind=kOutput, calls=%fused_computation.22 | convolution fusion | flops 129060864 | bytes 6389764 | tf_op jit(solution)/shard_map/lkr,lke->lre/dot_general | solution.py:381
  197.5 4.2 %subtract_convert_fusion = bf16[2,1152,1152]{2,1,0:T(8,128)(2,1)} fusion(bf16[2,1152,1152]{2,1,0:T(8,128)(2,1)S(1)} %bitcast.140, bf16[2,192,1152]{2,1,0:T(8,128)(2,1)S(1)} %fusion.41, bf16[2,192,1152]{2,1,0:T(8,128)(2,1)S(1)} %constant_dynamic-update-slice_fusion.5), kind=kOutput, calls=%fused_computation.2 | convolution fusion | flops 1029832704 | bytes 12386304 | tf_op jit(solution)/shard_map/lkr,lke->lre/dot_general | solution.py:384
  (110 shorter events, 12.5 us)
Async XLA Ops:
  0.6 105.2 %copy-start = (f32[2,1152,32]{1,2,0:T(8,128)S(1)}, f32[2,1152,32]{1,2,0:T(8,128)}, u32[]{:S(2)}) copy-start(f32[2,1152,32]{1,2,0:T(8,128)} %param.15) | copy-start | bytes 884740
  12.3 4.5 %copy-start.6 = (f32[2,144]{1,0:T(2,128)S(1)}, f32[2,144]{1,0:T(2,128)}, u32[]{:S(2)}) copy-start(f32[2,144]{1,0:T(2,128)} %param.14) | copy-start | bytes 3460
  12.3 4.5 %copy-start.7 = (bf16[2,144]{1,0:T(2,128)(2,1)S(1)}, bf16[2,144]{1,0:T(2,128)(2,1)}, u32[]{:S(2)}) copy-start(bf16[2,144]{1,0:T(2,128)(2,1)} %param.11) | copy-start | bytes 1732
  12.3 4.5 %copy-start.1 = (f32[2,144,1152]{2,1,0:T(8,128)S(1)}, f32[2,144,1152]{2,1,0:T(8,128)}, u32[]{:S(2)}) copy-start(f32[2,144,1152]{2,1,0:T(8,128)} %param.13) | copy-start | bytes 3981316
  15.4 4.4 %collective-permute-start.4 = (bf16[4,144,1152]{2,1,0:T(8,128)(2,1)}, bf16[4,144,1152]{2,1,0:T(8,128)(2,1)}, u32[]{:S(2)}, u32[]{:S(2)}) collective-permute-start(bf16[4,144,1152]{2,1,0:T(8,128)(2,1)} %get-tuple-element.38), channel_id=1, source_target_pairs={{0,1},{1,0},{2,3},{3,2},{4,5},{5,4},{6,7},{7,6},{8,9},{9,8},{10,11... | collective-permute-start | bytes 3981320 | tf_op jit(solution)/shard_map/ppermute | solution.py:251
  22.1 15.7 %slice-start.2 = ((s8[9437184]{0:T(1024)(128)(4,1)}), s8[4194304]{0:T(1024)(128)(4,1)S(1)}, s32[]{:S(2)}) async-start(s8[9437184]{0:T(1024)(128)(4,1)} %bitcast.144), calls=%async_computation.2 | async-start | bytes 8388608
  22.1 15.7 %slice-start.3 = ((s8[9437184]{0:T(1024)(128)(4,1)}), s8[4194304]{0:T(1024)(128)(4,1)S(1)}, s32[]{:S(2)}) async-start(s8[9437184]{0:T(1024)(128)(4,1)} %bitcast.144), calls=%async_computation.3 | async-start | bytes 8388608
  22.1 15.7 %slice-start.4 = ((s8[9437184]{0:T(1024)(128)(4,1)}), s8[1048576]{0:T(1024)(128)(4,1)S(1)}, s32[]{:S(2)}) async-start(s8[9437184]{0:T(1024)(128)(4,1)} %bitcast.144), calls=%async_computation.4 | async-start | bytes 2097152
  33.7 9.5 %copy-start.3 = (bf16[4,144,1152]{2,1,0:T(8,128)(2,1)}, bf16[4,144,1152]{2,1,0:T(8,128)(2,1)S(1)}, u32[]{:S(2)}) copy-start(bf16[4,144,1152]{2,1,0:T(8,128)(2,1)S(1)} %get-tuple-element.32) | copy-start | bytes 3981316
  33.7 8.8 %collective-permute-start.8 = (bf16[4,144,1152]{2,1,0:T(8,128)(2,1)}, bf16[4,144,1152]{2,1,0:T(8,128)(2,1)}, u32[]{:S(2)}, u32[]{:S(2)}) collective-permute-start(bf16[4,144,1152]{2,1,0:T(8,128)(2,1)} %get-tuple-element.33), channel_id=1, source_target_pairs={{0,1},{1,0},{2,3},{3,2},{4,5},{5,4},{6,7},{7,6},{8,9},{9,8},{10,11... | collective-permute-start | bytes 3981320 | tf_op jit(solution)/shard_map/ppermute | solution.py:251
  35.0 70.9 %collective-permute-start.2 = (bf16[2,152,1152]{2,1,0:T(8,128)(2,1)}, bf16[2,152,1152]{2,1,0:T(8,128)(2,1)}, u32[]{:S(2)}, u32[]{:S(2)}) collective-permute-start(bf16[2,152,1152]{2,1,0:T(8,128)(2,1)} %pad_maximum_fusion.2.refs_0_), channel_id=1, source_target_pairs={{0,6},{2,4},{4,2},{6,0},{1,7},{3,5},{5,3},{7,1},{8,14},{10,12},{12... | collective-permute-start | bytes 2101256 | tf_op jit(solution)/shard_map/ppermute | solution.py:254
  39.2 43.9 %collective-permute-start.7 = (bf16[144,1152]{1,0:T(8,128)(2,1)}, bf16[144,1152]{1,0:T(8,128)(2,1)}, u32[]{:S(2)}, u32[]{:S(2)}) collective-permute-start(bf16[144,1152]{1,0:T(8,128)(2,1)} %get-tuple-element.34), channel_id=1, source_target_pairs={{0,6},{2,4},{4,2},{6,0},{1,7},{3,5},{5,3},{7,1},{8,14},{10,12},{12... | collective-permute-start | bytes 995336 | tf_op jit(solution)/shard_map/ppermute | solution.py:254
  39.3 43.8 %collective-permute-start.6 = (bf16[144,1152]{1,0:T(8,128)(2,1)}, bf16[144,1152]{1,0:T(8,128)(2,1)}, u32[]{:S(2)}, u32[]{:S(2)}) collective-permute-start(bf16[144,1152]{1,0:T(8,128)(2,1)} %get-tuple-element.35), channel_id=1, source_target_pairs={{0,4},{2,6},{4,0},{6,2},{1,5},{3,7},{5,1},{7,3},{8,12},{10,14},{12... | collective-permute-start | bytes 995336 | tf_op jit(solution)/shard_map/ppermute | solution.py:254
  40.9 44.7 %collective-permute-start.5 = (bf16[144,1152]{1,0:T(8,128)(2,1)S(1)}, bf16[144,1152]{1,0:T(8,128)(2,1)}, u32[]{:S(2)}, u32[]{:S(2)}) collective-permute-start(bf16[144,1152]{1,0:T(8,128)(2,1)S(1)} %get-tuple-element.36), channel_id=1, source_target_pairs={{0,2},{2,0},{4,6},{6,4},{1,3},{3,1},{5,7},{7,5},{8,10},{10,8},{12,... | collective-permute-start | bytes 995336 | tf_op jit(solution)/shard_map/ppermute | solution.py:254
  42.5 44.3 %copy-start.4 = (f32[1,2,144,1152]{3,2,1,0:T(8,128)S(1)}, f32[1,2,144,1152]{3,2,1,0:T(8,128)}, u32[]{:S(2)}) copy-start(f32[1,2,144,1152]{3,2,1,0:T(8,128)} %param.12) | copy-start | bytes 3981316
  42.5 63.3 %collective-permute-start.1 = (bf16[2,152,1152]{2,1,0:T(8,128)(2,1)}, bf16[2,152,1152]{2,1,0:T(8,128)(2,1)}, u32[]{:S(2)}, u32[]{:S(2)}) collective-permute-start(bf16[2,152,1152]{2,1,0:T(8,128)(2,1)} %pad_maximum_fusion.2.refs_0_), channel_id=1, source_target_pairs={{0,4},{2,6},{4,0},{6,2},{1,5},{3,7},{5,1},{7,3},{8,12},{10,14},{12... | collective-permute-start | bytes 2101256 | tf_op jit(solution)/shard_map/ppermute | solution.py:254
  83.0 8.3 %collective-permute-start.9 = (bf16[144,1152]{1,0:T(8,128)(2,1)S(1)}, bf16[144,1152]{1,0:T(8,128)(2,1)S(1)}, u32[]{:S(2)}, u32[]{:S(2)}) collective-permute-start(bf16[144,1152]{1,0:T(8,128)(2,1)S(1)} %get-tuple-element.29), channel_id=1, source_target_pairs={{0,2},{2,0},{4,6},{6,4},{1,3},{3,1},{5,7},{7,5},{8,10},{10,8},{12,... | collective-permute-start | bytes 995336 | tf_op jit(solution)/shard_map/ppermute | solution.py:254
  83.0 9.3 %collective-permute-start.11 = (bf16[144,1152]{1,0:T(8,128)(2,1)S(1)}, bf16[144,1152]{1,0:T(8,128)(2,1)S(1)}, u32[]{:S(2)}, u32[]{:S(2)}) collective-permute-start(bf16[144,1152]{1,0:T(8,128)(2,1)S(1)} %get-tuple-element.30), channel_id=1, source_target_pairs={{0,6},{2,4},{4,2},{6,0},{1,7},{3,5},{5,3},{7,1},{8,14},{10,12},{12... | collective-permute-start | bytes 995336 | tf_op jit(solution)/shard_map/ppermute | solution.py:254
  85.5 15.0 %collective-permute-start.10 = (bf16[144,1152]{1,0:T(8,128)(2,1)S(1)}, bf16[144,1152]{1,0:T(8,128)(2,1)S(1)}, u32[]{:S(2)}, u32[]{:S(2)}) collective-permute-start(bf16[144,1152]{1,0:T(8,128)(2,1)S(1)} %get-tuple-element.31), channel_id=1, source_target_pairs={{0,4},{2,6},{4,0},{6,2},{1,5},{3,7},{5,1},{7,3},{8,12},{10,14},{12... | collective-permute-start | bytes 995336 | tf_op jit(solution)/shard_map/ppermute | solution.py:254
  91.4 22.2 %collective-permute-start = (bf16[2,152,1152]{2,1,0:T(8,128)(2,1)}, bf16[2,152,1152]{2,1,0:T(8,128)(2,1)S(1)}, u32[]{:S(2)}, u32[]{:S(2)}) collective-permute-start(bf16[2,152,1152]{2,1,0:T(8,128)(2,1)} %pad_maximum_fusion.2.refs_0_), channel_id=1, source_target_pairs={{0,2},{2,0},{4,6},{6,4},{1,3},{3,1},{5,7},{7,5},{8,10},{10,8},{12,... | collective-permute-start | bytes 2101256 | tf_op jit(solution)/shard_map/ppermute | solution.py:254
  102.0 18.0 %collective-permute-start.12 = (bf16[152,1152]{1,0:T(8,128)(2,1)S(1)}, bf16[152,1152]{1,0:T(8,128)(2,1)S(1)}, u32[]{:S(2)}, u32[]{:S(2)}) collective-permute-start(bf16[152,1152]{1,0:T(8,128)(2,1)S(1)} %pad_maximum_fusion.7), channel_id=1, source_target_pairs={{0,1},{1,0},{2,3},{3,2},{4,5},{5,4},{6,7},{7,6},{8,9},{9,8},{10,11... | collective-permute-start | bytes 1050632 | tf_op jit(solution)/shard_map/ppermute | solution.py:251
  113.5 0.9 copy-start.5
  118.2 54.9 %collective-permute-start.3 = (bf16[4,2,152,1152]{3,2,1,0:T(8,128)(2,1)}, bf16[4,2,152,1152]{3,2,1,0:T(8,128)(2,1)}, u32[]{:S(2)}, u32[]{:S(2)}) collective-permute-start(bf16[4,2,152,1152]{3,2,1,0:T(8,128)(2,1)} %lineup.1.mine_ref), channel_id=1, source_target_pairs={{0,1},{1,0},{2,3},{3,2},{4,5},{5,4},{6,7},{7,6},{8,9},{9,8},{10,11... | collective-permute-start | bytes 8405000 | tf_op jit(solution)/shard_map/ppermute | solution.py:251
  120.5 7.8 %collective-permute-start.13 = (bf16[80,1152]{1,0:T(8,128)(2,1)S(1)}, bf16[80,1152]{1,0:T(8,128)(2,1)S(1)}, u32[]{:S(2)}, u32[]{:S(2)}) collective-permute-start(bf16[80,1152]{1,0:T(8,128)(2,1)S(1)} %get-tuple-element.58), channel_id=1, source_target_pairs={{0,64},{32,96},{64,0},{96,32},{1,65},{33,97},{65,1},{97,33},{2,66}... | collective-permute-start | bytes 552968 | tf_op jit(solution)/shard_map/ppermute | solution.py:257
  123.2 9.4 %collective-permute-start.14 = (bf16[80,1152]{1,0:T(8,128)(2,1)S(1)}, bf16[80,1152]{1,0:T(8,128)(2,1)S(1)}, u32[]{:S(2)}, u32[]{:S(2)}) collective-permute-start(bf16[80,1152]{1,0:T(8,128)(2,1)S(1)} %get-tuple-element.59), channel_id=1, source_target_pairs={{0,32},{32,64},{64,96},{96,0},{1,33},{33,65},{65,97},{97,1},{2,34}... | collective-permute-start | bytes 552968 | tf_op jit(solution)/shard_map/ppermute | solution.py:257
  123.5 9.1 %collective-permute-start.15 = (bf16[80,1152]{1,0:T(8,128)(2,1)S(1)}, bf16[80,1152]{1,0:T(8,128)(2,1)S(1)}, u32[]{:S(2)}, u32[]{:S(2)}) collective-permute-start(bf16[80,1152]{1,0:T(8,128)(2,1)S(1)} %get-tuple-element.60), channel_id=1, source_target_pairs={{0,96},{32,0},{64,32},{96,64},{1,97},{33,1},{65,33},{97,65},{2,98}... | collective-permute-start | bytes 552968 | tf_op jit(solution)/shard_map/ppermute | solution.py:257
  132.8 7.2 %collective-permute-start.18 = (bf16[80,1152]{1,0:T(8,128)(2,1)S(1)}, bf16[80,1152]{1,0:T(8,128)(2,1)S(1)}, u32[]{:S(2)}, u32[]{:S(2)}) collective-permute-start(bf16[80,1152]{1,0:T(8,128)(2,1)S(1)} %pad_maximum_fusion.3), channel_id=1, source_target_pairs={{0,24},{8,0},{16,8},{24,16},{1,25},{9,1},{17,9},{25,17},{2,26},{10... | collective-permute-start | bytes 552968 | tf_op jit(solution)/shard_map/ppermute | solution.py:257
  136.5 7.9 %collective-permute-start.17 = (bf16[80,1152]{1,0:T(8,128)(2,1)S(1)}, bf16[80,1152]{1,0:T(8,128)(2,1)S(1)}, u32[]{:S(2)}, u32[]{:S(2)}) collective-permute-start(bf16[80,1152]{1,0:T(8,128)(2,1)S(1)} %pad_maximum_fusion.3), channel_id=1, source_target_pairs={{0,8},{8,16},{16,24},{24,0},{1,9},{9,17},{17,25},{25,1},{2,10},{10... | collective-permute-start | bytes 552968 | tf_op jit(solution)/shard_map/ppermute | solution.py:257
  136.5 9.2 %collective-permute-start.16 = (bf16[80,1152]{1,0:T(8,128)(2,1)S(1)}, bf16[80,1152]{1,0:T(8,128)(2,1)S(1)}, u32[]{:S(2)}, u32[]{:S(2)}) collective-permute-start(bf16[80,1152]{1,0:T(8,128)(2,1)S(1)} %pad_maximum_fusion.3), channel_id=1, source_target_pairs={{0,16},{8,24},{16,0},{24,8},{1,17},{9,25},{17,1},{25,9},{2,18},{10... | collective-permute-start | bytes 552968 | tf_op jit(solution)/shard_map/ppermute | solution.py:257
  145.8 10.9 %collective-permute-start.21 = (bf16[72,1152]{1,0:T(8,128)(2,1)S(1)}, bf16[72,1152]{1,0:T(8,128)(2,1)S(1)}, u32[]{:S(2)}, u32[]{:S(2)}) collective-permute-start(bf16[72,1152]{1,0:T(8,128)(2,1)S(1)} %add_convert_fusion.6.refs_0_), channel_id=1, source_target_pairs={{0,96},{32,64},{64,32},{96,0},{1,97},{33,65},{65,33},{97,1},{2,98}... | collective-permute-start | bytes 497672 | tf_op jit(solution)/shard_map/ppermute | solution.py:254
  149.7 7.0 %collective-permute-start.20 = (bf16[72,1152]{1,0:T(8,128)(2,1)S(1)}, bf16[72,1152]{1,0:T(8,128)(2,1)S(1)}, u32[]{:S(2)}, u32[]{:S(2)}) collective-permute-start(bf16[72,1152]{1,0:T(8,128)(2,1)S(1)} %add_convert_fusion.6.refs_0_), channel_id=1, source_target_pairs={{0,64},{32,96},{64,0},{96,32},{1,65},{33,97},{65,1},{97,33},{2,66}... | collective-permute-start | bytes 497672 | tf_op jit(solution)/shard_map/ppermute | solution.py:254
  149.7 7.0 %collective-permute-start.19 = (bf16[72,1152]{1,0:T(8,128)(2,1)S(1)}, bf16[72,1152]{1,0:T(8,128)(2,1)S(1)}, u32[]{:S(2)}, u32[]{:S(2)}) collective-permute-start(bf16[72,1152]{1,0:T(8,128)(2,1)S(1)} %add_convert_fusion.6.refs_0_), channel_id=1, source_target_pairs={{0,32},{32,0},{64,96},{96,64},{1,33},{33,1},{65,97},{97,65},{2,34}... | collective-permute-start | bytes 497672 | tf_op jit(solution)/shard_map/ppermute | solution.py:254
  157.5 5.5 %collective-permute-start.24 = (bf16[40,1408]{1,0:T(8,128)(2,1)S(1)}, bf16[40,1408]{1,0:T(8,128)(2,1)S(1)}, u32[]{:S(2)}, u32[]{:S(2)}) collective-permute-start(bf16[40,1408]{1,0:T(8,128)(2,1)S(1)} %get-tuple-element.19.refs_0_), channel_id=1, source_target_pairs={{0,6},{2,4},{4,2},{6,0},{1,7},{3,5},{5,3},{7,1},{8,14},{10,12},{12... | collective-permute-start | bytes 337928 | tf_op jit(solution)/shard_map/ppermute | solution.py:254
  160.2 5.2 %collective-permute-start.23 = (bf16[40,1408]{1,0:T(8,128)(2,1)S(1)}, bf16[40,1408]{1,0:T(8,128)(2,1)S(1)}, u32[]{:S(2)}, u32[]{:S(2)}) collective-permute-start(bf16[40,1408]{1,0:T(8,128)(2,1)S(1)} %get-tuple-element.19.refs_0_), channel_id=1, source_target_pairs={{0,4},{2,6},{4,0},{6,2},{1,5},{3,7},{5,1},{7,3},{8,12},{10,14},{12... | collective-permute-start | bytes 337928 | tf_op jit(solution)/shard_map/ppermute | solution.py:254
  160.2 5.2 %collective-permute-start.22 = (bf16[40,1408]{1,0:T(8,128)(2,1)S(1)}, bf16[40,1408]{1,0:T(8,128)(2,1)S(1)}, u32[]{:S(2)}, u32[]{:S(2)}) collective-permute-start(bf16[40,1408]{1,0:T(8,128)(2,1)S(1)} %get-tuple-element.19.refs_0_), channel_id=1, source_target_pairs={{0,2},{2,0},{4,6},{6,4},{1,3},{3,1},{5,7},{7,5},{8,10},{10,8},{12,... | collective-permute-start | bytes 337928 | tf_op jit(solution)/shard_map/ppermute | solution.py:254
  168.6 13.1 %collective-permute-start.29 = (f32[8,1152]{1,0:T(8,128)S(1)}, f32[8,1152]{1,0:T(8,128)S(1)}, u32[]{:S(2)}, u32[]{:S(2)}) collective-permute-start(f32[8,1152]{1,0:T(8,128)S(1)} %pad_maximum_fusion.17), channel_id=1, source_target_pairs={{0,1},{1,0},{2,3},{3,2},{4,5},{5,4},{6,7},{7,6},{8,9},{9,8},{10,11... | collective-permute-start | bytes 110600 | tf_op jit(solution)/shard_map/ppermute | solution.py:251
  178.4 9.2 %collective-permute-start.27 = (bf16[32,2176]{1,0:T(8,128)(2,1)S(1)}, bf16[32,2176]{1,0:T(8,128)(2,1)S(1)}, u32[]{:S(2)}, u32[]{:S(2)}) collective-permute-start(bf16[32,2176]{1,0:T(8,128)(2,1)S(1)} %get-tuple-element.21.refs_0_), channel_id=1, source_target_pairs={{0,6},{2,4},{4,2},{6,0},{1,7},{3,5},{5,3},{7,1},{8,14},{10,12},{12... | collective-permute-start | bytes 417800 | tf_op jit(solution)/shard_map/ppermute | solution.py:254
  179.9 7.7 %collective-permute-start.26 = (bf16[32,2176]{1,0:T(8,128)(2,1)S(1)}, bf16[32,2176]{1,0:T(8,128)(2,1)S(1)}, u32[]{:S(2)}, u32[]{:S(2)}) collective-permute-start(bf16[32,2176]{1,0:T(8,128)(2,1)S(1)} %get-tuple-element.21.refs_0_), channel_id=1, source_target_pairs={{0,4},{2,6},{4,0},{6,2},{1,5},{3,7},{5,1},{7,3},{8,12},{10,14},{12... | collective-permute-start | bytes 417800 | tf_op jit(solution)/shard_map/ppermute | solution.py:254
  180.2 8.0 %collective-permute-start.25 = (bf16[32,2176]{1,0:T(8,128)(2,1)S(1)}, bf16[32,2176]{1,0:T(8,128)(2,1)S(1)}, u32[]{:S(2)}, u32[]{:S(2)}) collective-permute-start(bf16[32,2176]{1,0:T(8,128)(2,1)S(1)} %get-tuple-element.21.refs_0_), channel_id=1, source_target_pairs={{0,2},{2,0},{4,6},{6,4},{1,3},{3,1},{5,7},{7,5},{8,10},{10,8},{12,... | collective-permute-start | bytes 417800 | tf_op jit(solution)/shard_map/ppermute | solution.py:254
  190.8 6.7 %slice-start = ((s8[5308416]{0:T(1024)(128)(4,1)}), s8[4194304]{0:T(1024)(128)(4,1)S(1)}, s32[]{:S(2)}) async-start(s8[5308416]{0:T(1024)(128)(4,1)} %bitcast.139), calls=%async_computation | async-start | bytes 8388608
  190.8 2.8 %collective-permute-start.28 = (f32[32,2304]{1,0:T(8,128)S(1)}, f32[32,2304]{1,0:T(8,128)S(1)}, u32[]{:S(2)}, u32[]{:S(2)}) collective-permute-start(f32[32,2304]{1,0:T(8,128)S(1)} %pad_maximum_fusion.14), channel_id=1, source_target_pairs={{0,1},{1,0},{2,3},{3,2},{4,5},{5,4},{6,7},{7,6},{8,9},{9,8},{10,11... | collective-permute-start | bytes 884744 | tf_op jit(solution)/shard_map/ppermute | solution.py:251
  193.9 1.3 copy-start.2
  194.0 3.4 %slice-start.1 = ((s8[5308416]{0:T(1024)(128)(4,1)}), s8[1114112]{0:T(1024)(128)(4,1)S(1)}, s32[]{:S(2)}) async-start(s8[5308416]{0:T(1024)(128)(4,1)} %bitcast.139), calls=%async_computation.1 | async-start | bytes 2228224

commit v3 on v2

--- a/solution.py
+++ b/solution.py
@@ -115,6 +115,18 @@
     out_ref[rank:] = both.astype(BF)
 
 
+def sum_kernel(own_ref, own_bias_ref, *refs):
+    parts, out_ref = refs[:3], refs[3]
+    rows, width = own_ref.shape
+    main = [own_ref[...]] + [part[:rows].astype(F32) for part in parts]
+    tail = [own_bias_ref[...].astype(F32)] + [part[rows:].astype(F32) for part in parts]
+    out_ref[:rows] = paired(main).astype(BF)
+    bias = paired([t[:1] + t[1:2] for t in tail])
+    high = bias.astype(BF).astype(F32)
+    both = jnp.concatenate([high, bias - high, jnp.zeros((6, width), F32)], 0)
+    out_ref[rows:] = both.astype(BF)
+
+
 def summed_parts(parts, columns):
     load = lambda ref: ref[:, :columns].astype(F32)
     return (load(parts[0]) + load(parts[1])) + (load(parts[2]) + load(parts[3]))
@@ -295,6 +307,7 @@
             pick(part.reshape(ys, cores, rows, width), 1 - core, 1)
         )
         keep = lax.optimization_barrier(pick(part.reshape(ys, cores, rows, width), core, 1))
+        keep = keep if layer == 1 else pick(part.reshape(ys, cores, rows, width), core, 1)
         blocks = []
         for k in range(4):
             there = ypos ^ k
@@ -331,10 +344,9 @@
     for k in (1, 2, 3):
         block = loaded(pick(both, (xpos + k) % 4))
         parts.append(from_back(block, "x", k))
-    main = paired([pick(both, xpos)] + [p[:half].astype(F32) for p in parts])
-    bias = paired([from_hi_lo(p) for p in [bias_rows] + [p[half:] for p in parts]])
-    bias_rows = hi_lo(bias)
-    block = loaded(main)
+    block = in_vmem(sum_kernel, jax.ShapeDtypeStruct((half + 8, width), BF))(
+        pick(both, xpos), bias_rows, *parts
+    )
     parts = [block] + [from_back(block, "z", k) for k in (1, 2, 3)]
     main = paired([p[:half].astype(F32) for p in parts]).astype(BF)
     bias = paired([from_hi_lo(p[half:]) for p in parts])

time: 202 us -> 203 us (level)
  waiting for transfers between devices: 91.6 us -> 100 us
  starting transfers between devices: 45.5 us -> 40.8 us
    ppermute x6, waiting for transfers between devices: 14.6 us -> 20.1 us  [from_back(): return lax.ppermute(value, axis, ring(4, k))]
    squeeze x2 -> x3, local copies, waits for them, and re-layouts: 4.4 us -> 3.97 us  [pick(): return lax.dynamic_index_in_dim(stack, index, axis, keepdims=False)]
    pallas_call x3 -> x4, Pallas kernels: 6.19 us -> 6.31 us  [call(): pl.pallas_call(kernel, out_shape=outs, in_specs=[smem] * scalars + [vmem]...]
  transfers between devices with their start and end apart: 30 -> 30, of which waited for: 16 -> 15; matrix products, arithmetic and copies ran while one was open for 5% -> 5% of each run, Pallas kernels for 6% -> 6%
where the time goes in v3:
time: 203 us
  waiting for transfers between devices  100 us (49%)
  starting transfers between devices  40.8 us (20%)
  matrix products  28.6 us (14%)
  Pallas kernels  14.6 us (7%)
  other arithmetic  11.4 us (6%)
  local copies, waits for them, and re-layouts  6.29 us (3%)
    ppermute x18, waiting for transfers between devices, trade(): return lax.ppermute(value, axis, [(i, i ^ k) for i in range(4)])  77.2 us
    dot_general x2, matrix products, chip_blocks(): jnp.einsum('tr,te->re', x[layer], y[layer], preferred_element_type=F32)  21.9 us
    ppermute x18, starting transfers between devices, trade(): return lax.ppermute(value, axis, [(i, i ^ k) for i in range(4)])  20.5 us
    ppermute x6, waiting for transfers between devices, from_back(): return lax.ppermute(value, axis, ring(4, k))  20.1 us
    ppermute x6, starting transfers between devices, swap(): return lax.ppermute(value, 'core', ring(cores, 1))  11.5 us
    ppermute x6, starting transfers between devices, from_back(): return lax.ppermute(value, axis, ring(4, k))  8.68 us
    pallas_call x4, Pallas kernels, call(): pl.pallas_call(kernel, out_shape=outs, in_specs=[smem] * scalars + [vmem]...  6.31 us
    pallas_call x1, Pallas kernels, assemble(): pl.pallas_call(assemble_kernel, out_shape=jax.ShapeDtypeStruct((layers, w...  5.37 us
  transfers between devices with their start and end apart: 30, of which 15 were waited for; matrix products, arithmetic and copies ran while one was open for 5% of the time, Pallas kernels for 6%

profile of v3, /device:TPU:1, one launch (start us, length us, event | category | flops | bytes accessed | tf_op | source)
XLA Modules:
  0.0 202.9 jit_solution(2048808709856373686)
XLA Ops:
  0.7 11.7 %convolution_convert_fusion.1 = bf16[1152,1152]{1,0:T(8,128)(2,1)} fusion(bf16[2,2048,1152]{2,1,0:T(8,128)(2,1)} %param.9, bf16[2,2048,1152]{2,1,0:T(8,128)(2,1)} %param.8), kind=kOutput, calls=%fused_computation.4 | convolution fusion | flops 5437145088 | bytes 12091392 | tf_op jit(solution)/shard_map/tr,te->re/dot_general | solution.py:304
  12.3 2.6 %dynamic-slice_bitcast_fusion.2 = bf16[4,144,1152]{2,1,0:T(8,128)(2,1)} fusion(bf16[4,2,144,1152]{3,2,1,0:T(8,128)(2,1)} %bitcast.147, s32[]{:T(128)S(6)} %select_n.204), kind=kLoop, calls=%fused_computation.25 | loop fusion | bytes 2654212 | tf_op jit(solution)/shard_map/jit(dynamic_index_in_dim)/squeeze | solution.py:21
  15.0 1.4 collective-permute-start.4
  16.6 2.8 %collective-permute-done.4 = bf16[4,144,1152]{2,1,0:T(8,128)(2,1)} collective-permute-done((bf16[4,144,1152]{2,1,0:T(8,128)(2,1)}, bf16[4,144,1152]{2,1,0:T(8,128)(2,1)}, u32[]{:S(2)}, u32[]{:S(2)}) %collective-permute-start.4) | collective-permute-done | bytes 1327136 | tf_op jit(solution)/shard_map/ppermute | solution.py:263
  19.4 2.6 %fusion.17 = (bf16[144,1152]{1,0:T(8,128)(2,1)}, bf16[144,1152]{1,0:T(8,128)(2,1)}, bf16[144,1152]{1,0:T(8,128)(2,1)}) fusion(bf16[4,144,1152]{2,1,0:T(8,128)(2,1)} %collective-permute-done.4, s32[]{:T(128)S(6)} %select_n.209, bf16[4,2,144,1152]{3,2,1,0:T(8,128)(2,1)} %bitcast.148, s32[]{:T(128)S(6)} %select_n.210, s32[]{:T(128)S(6)} %select_n.203, ...), kind=kLoop, calls=%fused_computation.39 | loop fusion | flops 1990656 | bytes 2986012 | tf_op jit(solution)/shard_map/convert_element_type | solution.py:315
  21.9 10.3 %convolution_convert_fusion = bf16[1152,1152]{1,0:T(8,128)(2,1)S(1)} fusion(bf16[2,2048,1152]{2,1,0:T(8,128)(2,1)} %param.9, bf16[2,2048,1152]{2,1,0:T(8,128)(2,1)} %param.8), kind=kOutput, calls=%fused_computation.3 | convolution fusion | flops 5437145088 | bytes 12091392 | tf_op jit(solution)/shard_map/tr,te->re/dot_general | solution.py:304
  32.2 1.3 dynamic-slice_bitcast_fusion.1
  33.9 0.9 pad_maximum_fusion.2.refs_0_
  34.8 2.8 %collective-permute-start.2 = (bf16[2,152,1152]{2,1,0:T(8,128)(2,1)}, bf16[2,152,1152]{2,1,0:T(8,128)(2,1)}, u32[]{:S(2)}, u32[]{:S(2)}) collective-permute-start(bf16[2,152,1152]{2,1,0:T(8,128)(2,1)} %pad_maximum_fusion.2.refs_0_), channel_id=1, source_target_pairs={{0,6},{2,4},{4,2},{6,0},{1,7},{3,5},{5,3},{7,1},{8,14},{10,12},{12... | collective-permute-start | bytes 2101256 | tf_op jit(solution)/shard_map/ppermute | solution.py:266
  37.6 1.3 convert_reduce_fusion
  39.0 1.6 collective-permute-start.6
  40.7 1.6 collective-permute-start.5
  43.1 1.4 fusion.28
  44.5 38.4 %collective-permute-done.7 = bf16[144,1152]{1,0:T(8,128)(2,1)S(1)} collective-permute-done((bf16[144,1152]{1,0:T(8,128)(2,1)}, bf16[144,1152]{1,0:T(8,128)(2,1)S(1)}, u32[]{:S(2)}, u32[]{:S(2)}) %collective-permute-start.7) | collective-permute-done | bytes 331808 | tf_op jit(solution)/shard_map/ppermute | solution.py:266
  82.9 2.5 %collective-permute-start.11 = (bf16[144,1152]{1,0:T(8,128)(2,1)S(1)}, bf16[144,1152]{1,0:T(8,128)(2,1)S(1)}, u32[]{:S(2)}, u32[]{:S(2)}) collective-permute-start(bf16[144,1152]{1,0:T(8,128)(2,1)S(1)} %get-tuple-element.31), channel_id=1, source_target_pairs={{0,6},{2,4},{4,2},{6,0},{1,7},{3,5},{5,3},{7,1},{8,14},{10,12},{12... | collective-permute-start | bytes 995336 | tf_op jit(solution)/shard_map/ppermute | solution.py:266
  85.4 1.3 collective-permute-start.10
  86.6 1.3 fusion.16
  88.0 3.4 %collective-permute-done.9 = bf16[144,1152]{1,0:T(8,128)(2,1)S(1)} collective-permute-done((bf16[144,1152]{1,0:T(8,128)(2,1)S(1)}, bf16[144,1152]{1,0:T(8,128)(2,1)S(1)}, u32[]{:S(2)}, u32[]{:S(2)}) %collective-permute-start.9) | collective-permute-done | bytes 331808 | tf_op jit(solution)/shard_map/ppermute | solution.py:266
  91.4 0.9 collective-permute-done.11
  92.3 8.2 %collective-permute-done.10 = bf16[144,1152]{1,0:T(8,128)(2,1)S(1)} collective-permute-done((bf16[144,1152]{1,0:T(8,128)(2,1)S(1)}, bf16[144,1152]{1,0:T(8,128)(2,1)S(1)}, u32[]{:S(2)}, u32[]{:S(2)}) %collective-permute-start.10) | collective-permute-done | bytes 331808 | tf_op jit(solution)/shard_map/ppermute | solution.py:266
  100.5 1.3 fusion.24
  102.0 3.4 %collective-permute-start.12 = (bf16[152,1152]{1,0:T(8,128)(2,1)S(1)}, bf16[152,1152]{1,0:T(8,128)(2,1)S(1)}, u32[]{:S(2)}, u32[]{:S(2)}) collective-permute-start(bf16[152,1152]{1,0:T(8,128)(2,1)S(1)} %pad_maximum_fusion.3), channel_id=1, source_target_pairs={{0,1},{1,0},{2,3},{3,2},{4,5},{5,4},{6,7},{7,6},{8,9},{9,8},{10,11... | collective-permute-start | bytes 1050632 | tf_op jit(solution)/shard_map/ppermute | solution.py:263
  105.4 8.2 %collective-permute-done.refs_1_ = bf16[2,152,1152]{2,1,0:T(8,128)(2,1)} collective-permute-done((bf16[2,152,1152]{2,1,0:T(8,128)(2,1)}, bf16[2,152,1152]{2,1,0:T(8,128)(2,1)}, u32[]{:S(2)}, u32[]{:S(2)}) %collective-permute-start) | collective-permute-done | bytes 700448 | tf_op jit(solution)/shard_map/ppermute | solution.py:266
  113.6 2.9 %lineup.1.mine_ref = bf16[4,2,152,1152]{3,2,1,0:T(8,128)(2,1)} custom-call(s32[1]{0:T(128)} %bitcast.1.ypos_ref, bf16[2,152,1152]{2,1,0:T(8,128)(2,1)} %pad_maximum_fusion.2.refs_0_, bf16[2,152,1152]{2,1,0:T(8,128)(2,1)} %collective-permute-done.refs_1_, bf16[2,152,1152]{2,1,0:T(8,128)(2,1)} %collective-permute-done.1.refs_2_, ...), custom_call_target="tpu_custom_call" | custom-call | tf_op jit(solution)/shard_map/lineup/pallas_call | solution.py:177
  117.3 1.7 collective-permute-start.3
  119.5 2.4 %collective-permute-start.15 = (bf16[80,1152]{1,0:T(8,128)(2,1)S(1)}, bf16[80,1152]{1,0:T(8,128)(2,1)S(1)}, u32[]{:S(2)}, u32[]{:S(2)}) collective-permute-start(bf16[80,1152]{1,0:T(8,128)(2,1)S(1)} %get-tuple-element.54), channel_id=1, source_target_pairs={{0,96},{32,0},{64,32},{96,64},{1,97},{33,1},{65,33},{97,65},{2,98}... | collective-permute-start | bytes 552968 | tf_op jit(solution)/shard_map/ppermute | solution.py:269
  123.1 6.6 %collective-permute-done.15.refs_2_ = bf16[80,1152]{1,0:T(8,128)(2,1)S(1)} collective-permute-done((bf16[80,1152]{1,0:T(8,128)(2,1)S(1)}, bf16[80,1152]{1,0:T(8,128)(2,1)S(1)}, u32[]{:S(2)}, u32[]{:S(2)}) %collective-permute-start.15) | collective-permute-done | bytes 184352 | tf_op jit(solution)/shard_map/ppermute | solution.py:269
  129.7 4.2 %collective-permute-done.13.refs_0_ = bf16[80,1152]{1,0:T(8,128)(2,1)S(1)} collective-permute-done((bf16[80,1152]{1,0:T(8,128)(2,1)S(1)}, bf16[80,1152]{1,0:T(8,128)(2,1)S(1)}, u32[]{:S(2)}, u32[]{:S(2)}) %collective-permute-start.13) | collective-permute-done | bytes 184352 | tf_op jit(solution)/shard_map/ppermute | solution.py:269
  134.1 3.8 %collective-permute-start.18 = (bf16[80,1152]{1,0:T(8,128)(2,1)S(1)}, bf16[80,1152]{1,0:T(8,128)(2,1)S(1)}, u32[]{:S(2)}, u32[]{:S(2)}) collective-permute-start(bf16[80,1152]{1,0:T(8,128)(2,1)S(1)} %shard_map.119), channel_id=1, source_target_pairs={{0,24},{8,0},{16,8},{24,16},{1,25},{9,1},{17,9},{25,17},{2,26},{10... | collective-permute-start | bytes 552968 | tf_op jit(solution)/shard_map/ppermute | solution.py:269
  137.9 1.3 collective-permute-start.16
  139.2 2.2 %collective-permute-done.18 = bf16[80,1152]{1,0:T(8,128)(2,1)S(1)} collective-permute-done((bf16[80,1152]{1,0:T(8,128)(2,1)S(1)}, bf16[80,1152]{1,0:T(8,128)(2,1)S(1)}, u32[]{:S(2)}, u32[]{:S(2)}) %collective-permute-start.18) | collective-permute-done | bytes 184352 | tf_op jit(solution)/shard_map/ppermute | solution.py:269
  141.4 7.1 %collective-permute-done.17 = bf16[80,1152]{1,0:T(8,128)(2,1)S(1)} collective-permute-done((bf16[80,1152]{1,0:T(8,128)(2,1)S(1)}, bf16[80,1152]{1,0:T(8,128)(2,1)S(1)}, u32[]{:S(2)}, u32[]{:S(2)}) %collective-permute-start.17) | collective-permute-done | bytes 184352 | tf_op jit(solution)/shard_map/ppermute | solution.py:269
  149.3 2.7 %collective-permute-start.19 = (bf16[72,1152]{1,0:T(8,128)(2,1)S(1)}, bf16[72,1152]{1,0:T(8,128)(2,1)S(1)}, u32[]{:S(2)}, u32[]{:S(2)}) collective-permute-start(bf16[72,1152]{1,0:T(8,128)(2,1)S(1)} %add_convert_fusion.3.refs_0_), channel_id=1, source_target_pairs={{0,32},{32,0},{64,96},{96,64},{1,33},{33,1},{65,97},{97,65},{2,34}... | collective-permute-start | bytes 497672 | tf_op jit(solution)/shard_map/ppermute | solution.py:266
  152.0 7.3 %collective-permute-done.21.refs_3_ = bf16[72,1152]{1,0:T(8,128)(2,1)S(1)} collective-permute-done((bf16[72,1152]{1,0:T(8,128)(2,1)S(1)}, bf16[72,1152]{1,0:T(8,128)(2,1)S(1)}, u32[]{:S(2)}, u32[]{:S(2)}) %collective-permute-start.21) | collective-permute-done | bytes 165920 | tf_op jit(solution)/shard_map/ppermute | solution.py:266
  160.1 2.6 %collective-permute-start.24 = (bf16[40,1408]{1,0:T(8,128)(2,1)S(1)}, bf16[40,1408]{1,0:T(8,128)(2,1)S(1)}, u32[]{:S(2)}, u32[]{:S(2)}) collective-permute-start(bf16[40,1408]{1,0:T(8,128)(2,1)S(1)} %get-tuple-element.19.refs_0_), channel_id=1, source_target_pairs={{0,6},{2,4},{4,2},{6,0},{1,7},{3,5},{5,3},{7,1},{8,14},{10,12},{12... | collective-permute-start | bytes 337928 | tf_op jit(solution)/shard_map/ppermute | solution.py:266
  163.6 2.4 %collective-permute-done.24.refs_3_ = bf16[40,1408]{1,0:T(8,128)(2,1)S(1)} collective-permute-done((bf16[40,1408]{1,0:T(8,128)(2,1)S(1)}, bf16[40,1408]{1,0:T(8,128)(2,1)S(1)}, u32[]{:S(2)}, u32[]{:S(2)}) %collective-permute-start.24) | collective-permute-done | bytes 112672 | tf_op jit(solution)/shard_map/ppermute | solution.py:266
  166.0 2.0 collective-permute-done.23.refs_2_
  168.0 3.2 %shard_map.121 = (bf16[32,2176]{1,0:T(8,128)(2,1)S(1)}, f32[8,1152]{1,0:T(8,128)S(1)}) custom-call(bf16[40,1408]{1,0:T(8,128)(2,1)S(1)} %get-tuple-element.19.refs_0_, bf16[40,1408]{1,0:T(8,128)(2,1)S(1)} %collective-permute-done.22.refs_1_, bf16[40,1408]{1,0:T(8,128)(2,1)S(1)} %collective-permute-done.23.refs_2_, ...), custom_call_target="tpu_custom_call" | custom-call | tf_op jit(solution)/shard_map/pallas_call | solution.py:222
  171.2 3.1 %collective-permute-start.29 = (f32[8,1152]{1,0:T(8,128)S(1)}, f32[8,1152]{1,0:T(8,128)S(1)}, u32[]{:S(2)}, u32[]{:S(2)}) collective-permute-start(f32[8,1152]{1,0:T(8,128)S(1)} %pad_maximum_fusion.16), channel_id=1, source_target_pairs={{0,1},{1,0},{2,3},{3,2},{4,5},{5,4},{6,7},{7,6},{8,9},{9,8},{10,11... | collective-permute-start | bytes 110600 | tf_op jit(solution)/shard_map/ppermute | solution.py:263
  174.3 5.4 %assemble.1 = bf16[2,1152,1152]{2,1,0:T(8,128)(2,1)} custom-call(s32[1]{0:T(128)} %bitcast.core_ref, bf16[4,2,152,1152]{3,2,1,0:T(8,128)(2,1)} %lineup.1.mine_ref, bf16[4,2,152,1152]{3,2,1,0:T(8,128)(2,1)} %collective-permute-done.3.theirs_ref), custom_call_target="tpu_custom_call" | custom-call | tf_op jit(solution)/shard_map/assemble/pallas_call | solution.py:204
  179.7 1.5 collective-permute-start.27
  181.2 1.7 collective-permute-start.25
  183.0 5.9 %collective-permute-done.27.refs_3_ = bf16[32,2176]{1,0:T(8,128)(2,1)S(1)} collective-permute-done((bf16[32,2176]{1,0:T(8,128)(2,1)S(1)}, bf16[32,2176]{1,0:T(8,128)(2,1)S(1)}, u32[]{:S(2)}, u32[]{:S(2)}) %collective-permute-start.27) | collective-permute-done | bytes 139296 | tf_op jit(solution)/shard_map/ppermute | solution.py:266
  189.6 2.1 %shard_map.122 = (f32[32,1152]{1,0:T(8,128)S(1)}, f32[32,32]{1,0:T(8,128)S(1)}) custom-call(bf16[32,2176]{1,0:T(8,128)(2,1)S(1)} %get-tuple-element.21.refs_0_, bf16[32,2176]{1,0:T(8,128)(2,1)S(1)} %collective-permute-done.25.refs_1_, bf16[32,2176]{1,0:T(8,128)(2,1)S(1)} %collective-permute-done.26.refs_2_, bf16[32,2176]{1,0:T(8,128)(2,1)S(1)} %collective-permute-done.27.refs_3_), custom_call_target="tpu_custom_call" | custom-call | tf_op jit(solution)/shard_map/pallas_call | solution.py:222
  192.1 1.5 collective-permute-start.28
  195.5 1.1 copy-done.2
  196.6 2.2 %multiply_add_fusion = (f32[2,144,1152]{2,1,0:T(8,128)}, f32[1,2,144,1152]{3,2,1,0:T(8,128)}) fusion(f32[2,144,1152]{2,1,0:T(8,128)S(1)} %copy-done.2, f32[1,144,1152]{2,1,0:T(8,128)S(1)} %fusion.24, f32[1,144,1152]{2,1,0:T(8,128)S(1)} %bitcast.141, bf16[2,192,1152]{2,1,0:T(8,128)(2,1)S(1)} %constant_dynamic-update-slice_fusion.5, ...), kind=kOutput, calls=%fused_computation.22 | convolution fusion | flops 129060864 | bytes 6389764 | tf_op jit(solution)/shard_map/lkr,lke->lre/dot_general | solution.py:393
  198.8 4.1 %subtract_convert_fusion = bf16[2,1152,1152]{2,1,0:T(8,128)(2,1)} fusion(bf16[2,1152,1152]{2,1,0:T(8,128)(2,1)S(1)} %bitcast.138, bf16[2,192,1152]{2,1,0:T(8,128)(2,1)S(1)} %fusion.40, bf16[2,192,1152]{2,1,0:T(8,128)(2,1)S(1)} %constant_dynamic-update-slice_fusion.5), kind=kOutput, calls=%fused_computation.2 | convolution fusion | flops 1029832704 | bytes 12386304 | tf_op jit(solution)/shard_map/lkr,lke->lre/dot_general | solution.py:396
  (107 shorter events, 9.5 us)
Async XLA Ops:
  0.6 104.8 %copy-start = (f32[2,1152,32]{1,2,0:T(8,128)S(1)}, f32[2,1152,32]{1,2,0:T(8,128)}, u32[]{:S(2)}) copy-start(f32[2,1152,32]{1,2,0:T(8,128)} %param.15) | copy-start | bytes 884740
  12.3 4.0 %copy-start.5 = (f32[2,144]{1,0:T(2,128)S(1)}, f32[2,144]{1,0:T(2,128)}, u32[]{:S(2)}) copy-start(f32[2,144]{1,0:T(2,128)} %param.14) | copy-start | bytes 3460
  12.3 4.0 %copy-start.6 = (bf16[2,144]{1,0:T(2,128)(2,1)S(1)}, bf16[2,144]{1,0:T(2,128)(2,1)}, u32[]{:S(2)}) copy-start(bf16[2,144]{1,0:T(2,128)(2,1)} %param.11) | copy-start | bytes 1732
  12.3 4.1 %copy-start.1 = (f32[2,144,1152]{2,1,0:T(8,128)S(1)}, f32[2,144,1152]{2,1,0:T(8,128)}, u32[]{:S(2)}) copy-start(f32[2,144,1152]{2,1,0:T(8,128)} %param.13) | copy-start | bytes 3981316
  12.3 4.1 %copy-start.4 = (bf16[2,144,1152]{2,1,0:T(8,128)(2,1)S(1)}, bf16[2,144,1152]{2,1,0:T(8,128)(2,1)}, u32[]{:S(2)}) copy-start(bf16[2,144,1152]{2,1,0:T(8,128)(2,1)} %param.10) | copy-start | bytes 1990660
  15.0 4.4 %collective-permute-start.4 = (bf16[4,144,1152]{2,1,0:T(8,128)(2,1)}, bf16[4,144,1152]{2,1,0:T(8,128)(2,1)}, u32[]{:S(2)}, u32[]{:S(2)}) collective-permute-start(bf16[4,144,1152]{2,1,0:T(8,128)(2,1)} %dynamic-slice_bitcast_fusion.2), channel_id=1, source_target_pairs={{0,1},{1,0},{2,3},{3,2},{4,5},{5,4},{6,7},{7,6},{8,9},{9,8},{10,11... | collective-permute-start | bytes 3981320 | tf_op jit(solution)/shard_map/ppermute | solution.py:263
  21.9 15.7 %slice-start.2 = ((s8[9437184]{0:T(1024)(128)(4,1)}), s8[4194304]{0:T(1024)(128)(4,1)S(1)}, s32[]{:S(2)}) async-start(s8[9437184]{0:T(1024)(128)(4,1)} %bitcast.142), calls=%async_computation.2 | async-start | bytes 8388608
  21.9 15.7 %slice-start.3 = ((s8[9437184]{0:T(1024)(128)(4,1)}), s8[4194304]{0:T(1024)(128)(4,1)S(1)}, s32[]{:S(2)}) async-start(s8[9437184]{0:T(1024)(128)(4,1)} %bitcast.142), calls=%async_computation.3 | async-start | bytes 8388608
  21.9 15.7 %slice-start.4 = ((s8[9437184]{0:T(1024)(128)(4,1)}), s8[1048576]{0:T(1024)(128)(4,1)S(1)}, s32[]{:S(2)}) async-start(s8[9437184]{0:T(1024)(128)(4,1)} %bitcast.142), calls=%async_computation.4 | async-start | bytes 2097152
  33.5 8.8 %collective-permute-start.8 = (bf16[4,144,1152]{2,1,0:T(8,128)(2,1)}, bf16[4,144,1152]{2,1,0:T(8,128)(2,1)}, u32[]{:S(2)}, u32[]{:S(2)}) collective-permute-start(bf16[4,144,1152]{2,1,0:T(8,128)(2,1)} %get-tuple-element.34), channel_id=1, source_target_pairs={{0,1},{1,0},{2,3},{3,2},{4,5},{5,4},{6,7},{7,6},{8,9},{9,8},{10,11... | collective-permute-start | bytes 3981320 | tf_op jit(solution)/shard_map/ppermute | solution.py:263
  34.8 70.7 %collective-permute-start.2 = (bf16[2,152,1152]{2,1,0:T(8,128)(2,1)}, bf16[2,152,1152]{2,1,0:T(8,128)(2,1)}, u32[]{:S(2)}, u32[]{:S(2)}) collective-permute-start(bf16[2,152,1152]{2,1,0:T(8,128)(2,1)} %pad_maximum_fusion.2.refs_0_), channel_id=1, source_target_pairs={{0,6},{2,4},{4,2},{6,0},{1,7},{3,5},{5,3},{7,1},{8,14},{10,12},{12... | collective-permute-start | bytes 2101256 | tf_op jit(solution)/shard_map/ppermute | solution.py:266
  38.9 43.9 %collective-permute-start.7 = (bf16[144,1152]{1,0:T(8,128)(2,1)}, bf16[144,1152]{1,0:T(8,128)(2,1)S(1)}, u32[]{:S(2)}, u32[]{:S(2)}) collective-permute-start(bf16[144,1152]{1,0:T(8,128)(2,1)} %get-tuple-element.27), channel_id=1, source_target_pairs={{0,6},{2,4},{4,2},{6,0},{1,7},{3,5},{5,3},{7,1},{8,14},{10,12},{12... | collective-permute-start | bytes 995336 | tf_op jit(solution)/shard_map/ppermute | solution.py:266
  39.0 43.8 %collective-permute-start.6 = (bf16[144,1152]{1,0:T(8,128)(2,1)}, bf16[144,1152]{1,0:T(8,128)(2,1)S(1)}, u32[]{:S(2)}, u32[]{:S(2)}) collective-permute-start(bf16[144,1152]{1,0:T(8,128)(2,1)} %get-tuple-element.28), channel_id=1, source_target_pairs={{0,4},{2,6},{4,0},{6,2},{1,5},{3,7},{5,1},{7,3},{8,12},{10,14},{12... | collective-permute-start | bytes 995336 | tf_op jit(solution)/shard_map/ppermute | solution.py:266
  40.7 44.7 %collective-permute-start.5 = (bf16[144,1152]{1,0:T(8,128)(2,1)}, bf16[144,1152]{1,0:T(8,128)(2,1)S(1)}, u32[]{:S(2)}, u32[]{:S(2)}) collective-permute-start(bf16[144,1152]{1,0:T(8,128)(2,1)} %get-tuple-element.29), channel_id=1, source_target_pairs={{0,2},{2,0},{4,6},{6,4},{1,3},{3,1},{5,7},{7,5},{8,10},{10,8},{12,... | collective-permute-start | bytes 995336 | tf_op jit(solution)/shard_map/ppermute | solution.py:266
  42.3 44.3 %copy-start.3 = (f32[1,2,144,1152]{3,2,1,0:T(8,128)S(1)}, f32[1,2,144,1152]{3,2,1,0:T(8,128)}, u32[]{:S(2)}) copy-start(f32[1,2,144,1152]{3,2,1,0:T(8,128)} %param.12) | copy-start | bytes 3981316
  42.4 63.1 %collective-permute-start.1 = (bf16[2,152,1152]{2,1,0:T(8,128)(2,1)}, bf16[2,152,1152]{2,1,0:T(8,128)(2,1)}, u32[]{:S(2)}, u32[]{:S(2)}) collective-permute-start(bf16[2,152,1152]{2,1,0:T(8,128)(2,1)} %pad_maximum_fusion.2.refs_0_), channel_id=1, source_target_pairs={{0,4},{2,6},{4,0},{6,2},{1,5},{3,7},{5,1},{7,3},{8,12},{10,14},{12... | collective-permute-start | bytes 2101256 | tf_op jit(solution)/shard_map/ppermute | solution.py:266
  82.9 8.5 %collective-permute-start.9 = (bf16[144,1152]{1,0:T(8,128)(2,1)S(1)}, bf16[144,1152]{1,0:T(8,128)(2,1)S(1)}, u32[]{:S(2)}, u32[]{:S(2)}) collective-permute-start(bf16[144,1152]{1,0:T(8,128)(2,1)S(1)} %get-tuple-element.30), channel_id=1, source_target_pairs={{0,2},{2,0},{4,6},{6,4},{1,3},{3,1},{5,7},{7,5},{8,10},{10,8},{12,... | collective-permute-start | bytes 995336 | tf_op jit(solution)/shard_map/ppermute | solution.py:266
  82.9 9.4 %collective-permute-start.11 = (bf16[144,1152]{1,0:T(8,128)(2,1)S(1)}, bf16[144,1152]{1,0:T(8,128)(2,1)S(1)}, u32[]{:S(2)}, u32[]{:S(2)}) collective-permute-start(bf16[144,1152]{1,0:T(8,128)(2,1)S(1)} %get-tuple-element.31), channel_id=1, source_target_pairs={{0,6},{2,4},{4,2},{6,0},{1,7},{3,5},{5,3},{7,1},{8,14},{10,12},{12... | collective-permute-start | bytes 995336 | tf_op jit(solution)/shard_map/ppermute | solution.py:266
  85.4 15.1 %collective-permute-start.10 = (bf16[144,1152]{1,0:T(8,128)(2,1)S(1)}, bf16[144,1152]{1,0:T(8,128)(2,1)S(1)}, u32[]{:S(2)}, u32[]{:S(2)}) collective-permute-start(bf16[144,1152]{1,0:T(8,128)(2,1)S(1)} %get-tuple-element.32), channel_id=1, source_target_pairs={{0,4},{2,6},{4,0},{6,2},{1,5},{3,7},{5,1},{7,3},{8,12},{10,14},{12... | collective-permute-start | bytes 995336 | tf_op jit(solution)/shard_map/ppermute | solution.py:266
  91.4 22.3 %collective-permute-start = (bf16[2,152,1152]{2,1,0:T(8,128)(2,1)}, bf16[2,152,1152]{2,1,0:T(8,128)(2,1)}, u32[]{:S(2)}, u32[]{:S(2)}) collective-permute-start(bf16[2,152,1152]{2,1,0:T(8,128)(2,1)} %pad_maximum_fusion.2.refs_0_), channel_id=1, source_target_pairs={{0,2},{2,0},{4,6},{6,4},{1,3},{3,1},{5,7},{7,5},{8,10},{10,8},{12,... | collective-permute-start | bytes 2101256 | tf_op jit(solution)/shard_map/ppermute | solution.py:266
  102.0 17.1 %collective-permute-start.12 = (bf16[152,1152]{1,0:T(8,128)(2,1)S(1)}, bf16[152,1152]{1,0:T(8,128)(2,1)S(1)}, u32[]{:S(2)}, u32[]{:S(2)}) collective-permute-start(bf16[152,1152]{1,0:T(8,128)(2,1)S(1)} %pad_maximum_fusion.3), channel_id=1, source_target_pairs={{0,1},{1,0},{2,3},{3,2},{4,5},{5,4},{6,7},{7,6},{8,9},{9,8},{10,11... | collective-permute-start | bytes 1050632 | tf_op jit(solution)/shard_map/ppermute | solution.py:263
  117.3 57.0 %collective-permute-start.3 = (bf16[4,2,152,1152]{3,2,1,0:T(8,128)(2,1)}, bf16[4,2,152,1152]{3,2,1,0:T(8,128)(2,1)}, u32[]{:S(2)}, u32[]{:S(2)}) collective-permute-start(bf16[4,2,152,1152]{3,2,1,0:T(8,128)(2,1)} %lineup.1.mine_ref), channel_id=1, source_target_pairs={{0,1},{1,0},{2,3},{3,2},{4,5},{5,4},{6,7},{7,6},{8,9},{9,8},{10,11... | collective-permute-start | bytes 8405000 | tf_op jit(solution)/shard_map/ppermute | solution.py:263
  119.5 10.2 %collective-permute-start.15 = (bf16[80,1152]{1,0:T(8,128)(2,1)S(1)}, bf16[80,1152]{1,0:T(8,128)(2,1)S(1)}, u32[]{:S(2)}, u32[]{:S(2)}) collective-permute-start(bf16[80,1152]{1,0:T(8,128)(2,1)S(1)} %get-tuple-element.54), channel_id=1, source_target_pairs={{0,96},{32,0},{64,32},{96,64},{1,97},{33,1},{65,33},{97,65},{2,98}... | collective-permute-start | bytes 552968 | tf_op jit(solution)/shard_map/ppermute | solution.py:269
  122.0 7.8 %collective-permute-start.14 = (bf16[80,1152]{1,0:T(8,128)(2,1)S(1)}, bf16[80,1152]{1,0:T(8,128)(2,1)S(1)}, u32[]{:S(2)}, u32[]{:S(2)}) collective-permute-start(bf16[80,1152]{1,0:T(8,128)(2,1)S(1)} %get-tuple-element.55), channel_id=1, source_target_pairs={{0,64},{32,96},{64,0},{96,32},{1,65},{33,97},{65,1},{97,33},{2,66}... | collective-permute-start | bytes 552968 | tf_op jit(solution)/shard_map/ppermute | solution.py:269
  122.5 11.5 %collective-permute-start.13 = (bf16[80,1152]{1,0:T(8,128)(2,1)S(1)}, bf16[80,1152]{1,0:T(8,128)(2,1)S(1)}, u32[]{:S(2)}, u32[]{:S(2)}) collective-permute-start(bf16[80,1152]{1,0:T(8,128)(2,1)S(1)} %get-tuple-element.56), channel_id=1, source_target_pairs={{0,32},{32,64},{64,96},{96,0},{1,33},{33,65},{65,97},{97,1},{2,34}... | collective-permute-start | bytes 552968 | tf_op jit(solution)/shard_map/ppermute | solution.py:269
  134.1 7.3 %collective-permute-start.18 = (bf16[80,1152]{1,0:T(8,128)(2,1)S(1)}, bf16[80,1152]{1,0:T(8,128)(2,1)S(1)}, u32[]{:S(2)}, u32[]{:S(2)}) collective-permute-start(bf16[80,1152]{1,0:T(8,128)(2,1)S(1)} %shard_map.119), channel_id=1, source_target_pairs={{0,24},{8,0},{16,8},{24,16},{1,25},{9,1},{17,9},{25,17},{2,26},{10... | collective-permute-start | bytes 552968 | tf_op jit(solution)/shard_map/ppermute | solution.py:269
  137.9 10.6 %collective-permute-start.17 = (bf16[80,1152]{1,0:T(8,128)(2,1)S(1)}, bf16[80,1152]{1,0:T(8,128)(2,1)S(1)}, u32[]{:S(2)}, u32[]{:S(2)}) collective-permute-start(bf16[80,1152]{1,0:T(8,128)(2,1)S(1)} %shard_map.119), channel_id=1, source_target_pairs={{0,8},{8,16},{16,24},{24,0},{1,9},{9,17},{17,25},{25,1},{2,10},{10... | collective-permute-start | bytes 552968 | tf_op jit(solution)/shard_map/ppermute | solution.py:269
  137.9 10.6 %collective-permute-start.16 = (bf16[80,1152]{1,0:T(8,128)(2,1)S(1)}, bf16[80,1152]{1,0:T(8,128)(2,1)S(1)}, u32[]{:S(2)}, u32[]{:S(2)}) collective-permute-start(bf16[80,1152]{1,0:T(8,128)(2,1)S(1)} %shard_map.119), channel_id=1, source_target_pairs={{0,16},{8,24},{16,0},{24,8},{1,17},{9,25},{17,1},{25,9},{2,18},{10... | collective-permute-start | bytes 552968 | tf_op jit(solution)/shard_map/ppermute | solution.py:269
  148.6 10.6 %collective-permute-start.21 = (bf16[72,1152]{1,0:T(8,128)(2,1)S(1)}, bf16[72,1152]{1,0:T(8,128)(2,1)S(1)}, u32[]{:S(2)}, u32[]{:S(2)}) collective-permute-start(bf16[72,1152]{1,0:T(8,128)(2,1)S(1)} %add_convert_fusion.3.refs_0_), channel_id=1, source_target_pairs={{0,96},{32,64},{64,32},{96,0},{1,97},{33,65},{65,33},{97,1},{2,98}... | collective-permute-start | bytes 497672 | tf_op jit(solution)/shard_map/ppermute | solution.py:266
  148.7 10.5 %collective-permute-start.20 = (bf16[72,1152]{1,0:T(8,128)(2,1)S(1)}, bf16[72,1152]{1,0:T(8,128)(2,1)S(1)}, u32[]{:S(2)}, u32[]{:S(2)}) collective-permute-start(bf16[72,1152]{1,0:T(8,128)(2,1)S(1)} %add_convert_fusion.3.refs_0_), channel_id=1, source_target_pairs={{0,64},{32,96},{64,0},{96,32},{1,65},{33,97},{65,1},{97,33},{2,66}... | collective-permute-start | bytes 497672 | tf_op jit(solution)/shard_map/ppermute | solution.py:266
  149.3 9.9 %collective-permute-start.19 = (bf16[72,1152]{1,0:T(8,128)(2,1)S(1)}, bf16[72,1152]{1,0:T(8,128)(2,1)S(1)}, u32[]{:S(2)}, u32[]{:S(2)}) collective-permute-start(bf16[72,1152]{1,0:T(8,128)(2,1)S(1)} %add_convert_fusion.3.refs_0_), channel_id=1, source_target_pairs={{0,32},{32,0},{64,96},{96,64},{1,33},{33,1},{65,97},{97,65},{2,34}... | collective-permute-start | bytes 497672 | tf_op jit(solution)/shard_map/ppermute | solution.py:266
  160.1 5.9 %collective-permute-start.24 = (bf16[40,1408]{1,0:T(8,128)(2,1)S(1)}, bf16[40,1408]{1,0:T(8,128)(2,1)S(1)}, u32[]{:S(2)}, u32[]{:S(2)}) collective-permute-start(bf16[40,1408]{1,0:T(8,128)(2,1)S(1)} %get-tuple-element.19.refs_0_), channel_id=1, source_target_pairs={{0,6},{2,4},{4,2},{6,0},{1,7},{3,5},{5,3},{7,1},{8,14},{10,12},{12... | collective-permute-start | bytes 337928 | tf_op jit(solution)/shard_map/ppermute | solution.py:266
  162.7 5.2 %collective-permute-start.23 = (bf16[40,1408]{1,0:T(8,128)(2,1)S(1)}, bf16[40,1408]{1,0:T(8,128)(2,1)S(1)}, u32[]{:S(2)}, u32[]{:S(2)}) collective-permute-start(bf16[40,1408]{1,0:T(8,128)(2,1)S(1)} %get-tuple-element.19.refs_0_), channel_id=1, source_target_pairs={{0,4},{2,6},{4,0},{6,2},{1,5},{3,7},{5,1},{7,3},{8,12},{10,14},{12... | collective-permute-start | bytes 337928 | tf_op jit(solution)/shard_map/ppermute | solution.py:266
  162.7 5.2 %collective-permute-start.22 = (bf16[40,1408]{1,0:T(8,128)(2,1)S(1)}, bf16[40,1408]{1,0:T(8,128)(2,1)S(1)}, u32[]{:S(2)}, u32[]{:S(2)}) collective-permute-start(bf16[40,1408]{1,0:T(8,128)(2,1)S(1)} %get-tuple-element.19.refs_0_), channel_id=1, source_target_pairs={{0,2},{2,0},{4,6},{6,4},{1,3},{3,1},{5,7},{7,5},{8,10},{10,8},{12,... | collective-permute-start | bytes 337928 | tf_op jit(solution)/shard_map/ppermute | solution.py:266
  171.2 11.8 %collective-permute-start.29 = (f32[8,1152]{1,0:T(8,128)S(1)}, f32[8,1152]{1,0:T(8,128)S(1)}, u32[]{:S(2)}, u32[]{:S(2)}) collective-permute-start(f32[8,1152]{1,0:T(8,128)S(1)} %pad_maximum_fusion.16), channel_id=1, source_target_pairs={{0,1},{1,0},{2,3},{3,2},{4,5},{5,4},{6,7},{7,6},{8,9},{9,8},{10,11... | collective-permute-start | bytes 110600 | tf_op jit(solution)/shard_map/ppermute | solution.py:263
  179.7 9.2 %collective-permute-start.27 = (bf16[32,2176]{1,0:T(8,128)(2,1)S(1)}, bf16[32,2176]{1,0:T(8,128)(2,1)S(1)}, u32[]{:S(2)}, u32[]{:S(2)}) collective-permute-start(bf16[32,2176]{1,0:T(8,128)(2,1)S(1)} %get-tuple-element.21.refs_0_), channel_id=1, source_target_pairs={{0,6},{2,4},{4,2},{6,0},{1,7},{3,5},{5,3},{7,1},{8,14},{10,12},{12... | collective-permute-start | bytes 417800 | tf_op jit(solution)/shard_map/ppermute | solution.py:266
  181.2 7.7 %collective-permute-start.26 = (bf16[32,2176]{1,0:T(8,128)(2,1)S(1)}, bf16[32,2176]{1,0:T(8,128)(2,1)S(1)}, u32[]{:S(2)}, u32[]{:S(2)}) collective-permute-start(bf16[32,2176]{1,0:T(8,128)(2,1)S(1)} %get-tuple-element.21.refs_0_), channel_id=1, source_target_pairs={{0,4},{2,6},{4,0},{6,2},{1,5},{3,7},{5,1},{7,3},{8,12},{10,14},{12... | collective-permute-start | bytes 417800 | tf_op jit(solution)/shard_map/ppermute | solution.py:266
  181.2 8.2 %collective-permute-start.25 = (bf16[32,2176]{1,0:T(8,128)(2,1)S(1)}, bf16[32,2176]{1,0:T(8,128)(2,1)S(1)}, u32[]{:S(2)}, u32[]{:S(2)}) collective-permute-start(bf16[32,2176]{1,0:T(8,128)(2,1)S(1)} %get-tuple-element.21.refs_0_), channel_id=1, source_target_pairs={{0,2},{2,0},{4,6},{6,4},{1,3},{3,1},{5,7},{7,5},{8,10},{10,8},{12,... | collective-permute-start | bytes 417800 | tf_op jit(solution)/shard_map/ppermute | solution.py:266
  192.1 6.7 %slice-start = ((s8[5308416]{0:T(1024)(128)(4,1)}), s8[4194304]{0:T(1024)(128)(4,1)S(1)}, s32[]{:S(2)}) async-start(s8[5308416]{0:T(1024)(128)(4,1)} %bitcast.137), calls=%async_computation | async-start | bytes 8388608
  192.1 2.8 %collective-permute-start.28 = (f32[32,2304]{1,0:T(8,128)S(1)}, f32[32,2304]{1,0:T(8,128)S(1)}, u32[]{:S(2)}, u32[]{:S(2)}) collective-permute-start(f32[32,2304]{1,0:T(8,128)S(1)} %pad_maximum_fusion.13), channel_id=1, source_target_pairs={{0,1},{1,0},{2,3},{3,2},{4,5},{5,4},{6,7},{7,6},{8,9},{9,8},{10,11... | collective-permute-start | bytes 884744 | tf_op jit(solution)/shard_map/ppermute | solution.py:263
  195.2 1.3 copy-start.2
  195.3 3.4 %slice-start.1 = ((s8[5308416]{0:T(1024)(128)(4,1)}), s8[1114112]{0:T(1024)(128)(4,1)S(1)}, s32[]{:S(2)}) async-start(s8[5308416]{0:T(1024)(128)(4,1)} %bitcast.137), calls=%async_computation.1 | async-start | bytes 2228224

commit v4 on v2

--- a/solution.py
+++ b/solution.py
@@ -294,11 +294,10 @@
         got = swap(
             pick(part.reshape(ys, cores, rows, width), 1 - core, 1)
         )
-        keep = lax.optimization_barrier(pick(part.reshape(ys, cores, rows, width), core, 1))
         blocks = []
         for k in range(4):
             there = ypos ^ k
-            blocks.append(pick(keep, there).astype(F32) + pick(got, there).astype(F32))
+            blocks.append(pick(part, there * cores + core).astype(F32) + pick(got, there).astype(F32))
         return blocks[0], [b.astype(BF) for b in blocks[1:]]
 
     def merge(layer, own, blocks):
@@ -335,7 +334,9 @@
     bias = paired([from_hi_lo(p) for p in [bias_rows] + [p[half:] for p in parts]])
     bias_rows = hi_lo(bias)
     block = loaded(main)
-    parts = [block] + [from_back(block, "z", k) for k in (1, 2, 3)]
+    parts = [block]
+    for k in (1, 2, 3):
+        parts.append(from_back(block, "z", k))
     main = paired([p[:half].astype(F32) for p in parts]).astype(BF)
     bias = paired([from_hi_lo(p[half:]) for p in parts])
     parts = everyone(main, "x")

time: 202 us -> 201 us (level)
  local copies, waits for them, and re-layouts: 7.59 us -> 4.83 us
    squeeze x2, local copies, waits for them, and re-layouts: 4.4 us -> 1.64 us  [pick(): return lax.dynamic_index_in_dim(stack, index, axis, keepdims=False)]
  transfers between devices with their start and end apart: 30 -> 30, of which waited for: 16 -> 16; matrix products, arithmetic and copies ran while one was open for 5% -> 6% of each run, Pallas kernels for 6% -> 6%
where the time goes in v4:
time: 201 us; the launch traced here: 200 us
  waiting for transfers between devices  90.7 us (45%)
  starting transfers between devices  46 us (23%)
  matrix products  28.6 us (14%)
  Pallas kernels  14.5 us (7%)
  other arithmetic  14.3 us (7%)
  local copies, waits for them, and re-layouts  4.83 us (2%)
    ppermute x18, waiting for transfers between devices, trade(): return lax.ppermute(value, axis, [(i, i ^ k) for i in range(4)])  74.6 us
    dot_general x2, matrix products, chip_blocks(): jnp.einsum('tr,te->re', x[layer], y[layer], preferred_element_type=F32)  21.9 us
    ppermute x18, starting transfers between devices, trade(): return lax.ppermute(value, axis, [(i, i ^ k) for i in range(4)])  21.8 us
    ppermute x6, waiting for transfers between devices, from_back(): return lax.ppermute(value, axis, ring(4, k))  14.6 us
    ppermute x6, starting transfers between devices, swap(): return lax.ppermute(value, 'core', ring(cores, 1))  13.8 us
    ppermute x6, starting transfers between devices, from_back(): return lax.ppermute(value, axis, ring(4, k))  10.4 us
    pallas_call x3, Pallas kernels, call(): pl.pallas_call(kernel, out_shape=outs, in_specs=[smem] * scalars + [vmem]...  6.19 us
    pallas_call x1, Pallas kernels, assemble(): pl.pallas_call(assemble_kernel, out_shape=jax.ShapeDtypeStruct((layers, w...  5.37 us
  transfers between devices with their start and end apart: 30, of which 16 were waited for; matrix products, arithmetic and copies ran while one was open for 6% of the time, Pallas kernels for 6%

profile of v4, /device:TPU:1, one launch (start us, length us, event | category | flops | bytes accessed | tf_op | source)
XLA Modules:
  0.0 200.1 jit_solution(14371906982330087531)
XLA Ops:
  0.7 11.6 %convolution_convert_fusion.1 = bf16[1152,1152]{1,0:T(8,128)(2,1)} fusion(bf16[2,2048,1152]{2,1,0:T(8,128)(2,1)} %param.9, bf16[2,2048,1152]{2,1,0:T(8,128)(2,1)} %param.8), kind=kOutput, calls=%fused_computation.4 | convolution fusion | flops 5437145088 | bytes 12091392 | tf_op jit(solution)/shard_map/tr,te->re/dot_general | solution.py:292
  12.3 1.5 dynamic-slice_bitcast_fusion.1
  13.8 1.6 collective-permute-start.4
  15.5 1.2 subtract_convert_fusion.1
  16.8 1.5 collective-permute-done.4
  18.3 2.6 %fusion.26 = (bf16[144,1152]{1,0:T(8,128)(2,1)}, bf16[144,1152]{1,0:T(8,128)(2,1)}, bf16[144,1152]{1,0:T(8,128)(2,1)S(1)}) fusion(bf16[4,144,1152]{2,1,0:T(8,128)(2,1)} %collective-permute-done.4, s32[]{:T(128)S(6)} %select_n.205, bf16[8,144,1152]{2,1,0:T(8,128)(2,1)} %bitcast.143, s32[]{:T(128)S(6)} %select_n.204, s32[]{:T(128)S(6)} %select_n.203, ...), kind=kLoop, calls=%fused_computation.60 | loop fusion | flops 1990656 | bytes 2986008 | tf_op jit(solution)/shard_map/convert_element_type | solution.py:301
  20.9 10.3 %convolution_convert_fusion = bf16[1152,1152]{1,0:T(8,128)(2,1)S(1)} fusion(bf16[2,2048,1152]{2,1,0:T(8,128)(2,1)} %param.9, bf16[2,2048,1152]{2,1,0:T(8,128)(2,1)} %param.8), kind=kOutput, calls=%fused_computation.3 | convolution fusion | flops 5437145088 | bytes 12091392 | tf_op jit(solution)/shard_map/tr,te->re/dot_general | solution.py:292
  32.6 2.8 %collective-permute-start.2 = (bf16[2,152,1152]{2,1,0:T(8,128)(2,1)S(1)}, bf16[2,152,1152]{2,1,0:T(8,128)(2,1)S(1)}, u32[]{:S(2)}, u32[]{:S(2)}) collective-permute-start(bf16[2,152,1152]{2,1,0:T(8,128)(2,1)S(1)} %pad_maximum_fusion.2.refs_0_), channel_id=1, source_target_pairs={{0,6},{2,4},{4,2},{6,0},{1,7},{3,5},{5,3},{7,1},{8,14},{10,12},{12... | collective-permute-start | bytes 2101256 | tf_op jit(solution)/shard_map/ppermute | solution.py:254
  35.5 1.3 convert_reduce_fusion
  36.9 1.6 collective-permute-start.6
  38.5 1.6 collective-permute-start.5
  40.9 1.8 fusion.27
  42.7 37.7 %collective-permute-done.7 = bf16[144,1152]{1,0:T(8,128)(2,1)} collective-permute-done((bf16[144,1152]{1,0:T(8,128)(2,1)}, bf16[144,1152]{1,0:T(8,128)(2,1)}, u32[]{:S(2)}, u32[]{:S(2)}) %collective-permute-start.7) | collective-permute-done | bytes 331808 | tf_op jit(solution)/shard_map/ppermute | solution.py:254
  80.4 2.5 %collective-permute-start.11 = (bf16[144,1152]{1,0:T(8,128)(2,1)S(1)}, bf16[144,1152]{1,0:T(8,128)(2,1)S(1)}, u32[]{:S(2)}, u32[]{:S(2)}) collective-permute-start(bf16[144,1152]{1,0:T(8,128)(2,1)S(1)} %get-tuple-element.30), channel_id=1, source_target_pairs={{0,6},{2,4},{4,2},{6,0},{1,7},{3,5},{5,3},{7,1},{8,14},{10,12},{12... | collective-permute-start | bytes 995336 | tf_op jit(solution)/shard_map/ppermute | solution.py:254
  82.9 1.3 collective-permute-start.10
  84.2 1.6 fusion.16
  85.8 2.9 %collective-permute-done.9 = bf16[144,1152]{1,0:T(8,128)(2,1)S(1)} collective-permute-done((bf16[144,1152]{1,0:T(8,128)(2,1)S(1)}, bf16[144,1152]{1,0:T(8,128)(2,1)S(1)}, u32[]{:S(2)}, u32[]{:S(2)}) %collective-permute-start.9) | collective-permute-done | bytes 331808 | tf_op jit(solution)/shard_map/ppermute | solution.py:254
  89.6 8.2 %collective-permute-done.10 = bf16[144,1152]{1,0:T(8,128)(2,1)S(1)} collective-permute-done((bf16[144,1152]{1,0:T(8,128)(2,1)S(1)}, bf16[144,1152]{1,0:T(8,128)(2,1)S(1)}, u32[]{:S(2)}, u32[]{:S(2)}) %collective-permute-start.10) | collective-permute-done | bytes 331808 | tf_op jit(solution)/shard_map/ppermute | solution.py:254
  97.9 1.4 fusion.17
  99.4 3.8 %collective-permute-start.12 = (bf16[152,1152]{1,0:T(8,128)(2,1)S(1)}, bf16[152,1152]{1,0:T(8,128)(2,1)}, u32[]{:S(2)}, u32[]{:S(2)}) collective-permute-start(bf16[152,1152]{1,0:T(8,128)(2,1)S(1)} %pad_maximum_fusion.7), channel_id=1, source_target_pairs={{0,1},{1,0},{2,3},{3,2},{4,5},{5,4},{6,7},{7,6},{8,9},{9,8},{10,11... | collective-permute-start | bytes 1050632 | tf_op jit(solution)/shard_map/ppermute | solution.py:251
  103.3 7.7 %collective-permute-done.refs_1_ = bf16[2,152,1152]{2,1,0:T(8,128)(2,1)} collective-permute-done((bf16[2,152,1152]{2,1,0:T(8,128)(2,1)S(1)}, bf16[2,152,1152]{2,1,0:T(8,128)(2,1)}, u32[]{:S(2)}, u32[]{:S(2)}) %collective-permute-start) | collective-permute-done | bytes 700448 | tf_op jit(solution)/shard_map/ppermute | solution.py:254
  111.0 3.0 %lineup.1.mine_ref = bf16[4,2,152,1152]{3,2,1,0:T(8,128)(2,1)} custom-call(s32[1]{0:T(128)} %bitcast.1.ypos_ref, bf16[2,152,1152]{2,1,0:T(8,128)(2,1)} %copy-done.3, bf16[2,152,1152]{2,1,0:T(8,128)(2,1)} %collective-permute-done.refs_1_, bf16[2,152,1152]{2,1,0:T(8,128)(2,1)} %collective-permute-done.1.refs_2_, bf16[2,152,1152]{2,1,0:T(8,128)(2,1)} %copy-done.6), custom_call_target="tpu_custom_call" | custom-call | tf_op jit(solution)/shard_map/lineup/pallas_call | solution.py:165
  114.7 1.9 collective-permute-start.3
  117.5 1.1 fusion.10
  118.9 2.7 %collective-permute-start.13 = (bf16[80,1152]{1,0:T(8,128)(2,1)S(1)}, bf16[80,1152]{1,0:T(8,128)(2,1)S(1)}, u32[]{:S(2)}, u32[]{:S(2)}) collective-permute-start(bf16[80,1152]{1,0:T(8,128)(2,1)S(1)} %get-tuple-element.54), channel_id=1, source_target_pairs={{0,64},{32,96},{64,0},{96,32},{1,65},{33,97},{65,1},{97,33},{2,66}... | collective-permute-start | bytes 552968 | tf_op jit(solution)/shard_map/ppermute | solution.py:257
  121.9 2.4 %collective-permute-start.15 = (bf16[80,1152]{1,0:T(8,128)(2,1)S(1)}, bf16[80,1152]{1,0:T(8,128)(2,1)S(1)}, u32[]{:S(2)}, u32[]{:S(2)}) collective-permute-start(bf16[80,1152]{1,0:T(8,128)(2,1)S(1)} %get-tuple-element.56), channel_id=1, source_target_pairs={{0,96},{32,0},{64,32},{96,64},{1,97},{33,1},{65,33},{97,65},{2,98}... | collective-permute-start | bytes 552968 | tf_op jit(solution)/shard_map/ppermute | solution.py:257
  124.3 2.4 %collective-permute-done.13 = bf16[80,1152]{1,0:T(8,128)(2,1)S(1)} collective-permute-done((bf16[80,1152]{1,0:T(8,128)(2,1)S(1)}, bf16[80,1152]{1,0:T(8,128)(2,1)S(1)}, u32[]{:S(2)}, u32[]{:S(2)}) %collective-permute-start.13) | collective-permute-done | bytes 184352 | tf_op jit(solution)/shard_map/ppermute | solution.py:257
  126.6 4.3 %collective-permute-done.14 = bf16[80,1152]{1,0:T(8,128)(2,1)S(1)} collective-permute-done((bf16[80,1152]{1,0:T(8,128)(2,1)S(1)}, bf16[80,1152]{1,0:T(8,128)(2,1)S(1)}, u32[]{:S(2)}, u32[]{:S(2)}) %collective-permute-start.14) | collective-permute-done | bytes 184352 | tf_op jit(solution)/shard_map/ppermute | solution.py:257
  131.2 3.7 %collective-permute-start.18 = (bf16[80,1152]{1,0:T(8,128)(2,1)S(1)}, bf16[80,1152]{1,0:T(8,128)(2,1)S(1)}, u32[]{:S(2)}, u32[]{:S(2)}) collective-permute-start(bf16[80,1152]{1,0:T(8,128)(2,1)S(1)} %pad_maximum_fusion.3), channel_id=1, source_target_pairs={{0,24},{8,0},{16,8},{24,16},{1,25},{9,1},{17,9},{25,17},{2,26},{10... | collective-permute-start | bytes 552968 | tf_op jit(solution)/shard_map/ppermute | solution.py:257
  134.9 1.3 collective-permute-start.16
  136.2 2.1 %collective-permute-done.18 = bf16[80,1152]{1,0:T(8,128)(2,1)S(1)} collective-permute-done((bf16[80,1152]{1,0:T(8,128)(2,1)S(1)}, bf16[80,1152]{1,0:T(8,128)(2,1)S(1)}, u32[]{:S(2)}, u32[]{:S(2)}) %collective-permute-start.18) | collective-permute-done | bytes 184352 | tf_op jit(solution)/shard_map/ppermute | solution.py:257
  138.3 4.4 %collective-permute-done.17 = bf16[80,1152]{1,0:T(8,128)(2,1)S(1)} collective-permute-done((bf16[80,1152]{1,0:T(8,128)(2,1)S(1)}, bf16[80,1152]{1,0:T(8,128)(2,1)S(1)}, u32[]{:S(2)}, u32[]{:S(2)}) %collective-permute-start.17) | collective-permute-done | bytes 184352 | tf_op jit(solution)/shard_map/ppermute | solution.py:257
  142.8 1.3 collective-permute-done.16
  144.2 3.9 %collective-permute-start.21 = (bf16[72,1152]{1,0:T(8,128)(2,1)S(1)}, bf16[72,1152]{1,0:T(8,128)(2,1)S(1)}, u32[]{:S(2)}, u32[]{:S(2)}) collective-permute-start(bf16[72,1152]{1,0:T(8,128)(2,1)S(1)} %add_convert_fusion.6.refs_0_), channel_id=1, source_target_pairs={{0,96},{32,64},{64,32},{96,0},{1,97},{33,65},{65,33},{97,1},{2,98}... | collective-permute-start | bytes 497672 | tf_op jit(solution)/shard_map/ppermute | solution.py:254
  148.8 6.3 %collective-permute-done.21.refs_3_ = bf16[72,1152]{1,0:T(8,128)(2,1)S(1)} collective-permute-done((bf16[72,1152]{1,0:T(8,128)(2,1)S(1)}, bf16[72,1152]{1,0:T(8,128)(2,1)S(1)}, u32[]{:S(2)}, u32[]{:S(2)}) %collective-permute-start.21) | collective-permute-done | bytes 165920 | tf_op jit(solution)/shard_map/ppermute | solution.py:254
  156.0 2.6 %collective-permute-start.24 = (bf16[40,1408]{1,0:T(8,128)(2,1)S(1)}, bf16[40,1408]{1,0:T(8,128)(2,1)S(1)}, u32[]{:S(2)}, u32[]{:S(2)}) collective-permute-start(bf16[40,1408]{1,0:T(8,128)(2,1)S(1)} %get-tuple-element.19.refs_0_), channel_id=1, source_target_pairs={{0,6},{2,4},{4,2},{6,0},{1,7},{3,5},{5,3},{7,1},{8,14},{10,12},{12... | collective-permute-start | bytes 337928 | tf_op jit(solution)/shard_map/ppermute | solution.py:254
  159.4 2.1 %collective-permute-done.24.refs_3_ = bf16[40,1408]{1,0:T(8,128)(2,1)S(1)} collective-permute-done((bf16[40,1408]{1,0:T(8,128)(2,1)S(1)}, bf16[40,1408]{1,0:T(8,128)(2,1)S(1)}, u32[]{:S(2)}, u32[]{:S(2)}) %collective-permute-start.24) | collective-permute-done | bytes 112672 | tf_op jit(solution)/shard_map/ppermute | solution.py:254
  161.5 2.3 %collective-permute-done.23.refs_2_ = bf16[40,1408]{1,0:T(8,128)(2,1)S(1)} collective-permute-done((bf16[40,1408]{1,0:T(8,128)(2,1)S(1)}, bf16[40,1408]{1,0:T(8,128)(2,1)S(1)}, u32[]{:S(2)}, u32[]{:S(2)}) %collective-permute-start.23) | collective-permute-done | bytes 112672 | tf_op jit(solution)/shard_map/ppermute | solution.py:254
  163.8 3.2 %shard_map.120 = (bf16[32,2176]{1,0:T(8,128)(2,1)S(1)}, f32[8,1152]{1,0:T(8,128)S(1)}) custom-call(bf16[40,1408]{1,0:T(8,128)(2,1)S(1)} %get-tuple-element.19.refs_0_, bf16[40,1408]{1,0:T(8,128)(2,1)S(1)} %collective-permute-done.22.refs_1_, bf16[40,1408]{1,0:T(8,128)(2,1)S(1)} %collective-permute-done.23.refs_2_, ...), custom_call_target="tpu_custom_call" | custom-call | tf_op jit(solution)/shard_map/pallas_call | solution.py:210
  167.0 4.5 %collective-permute-start.29 = (f32[8,1152]{1,0:T(8,128)S(1)}, f32[8,1152]{1,0:T(8,128)S(1)}, u32[]{:S(2)}, u32[]{:S(2)}) collective-permute-start(f32[8,1152]{1,0:T(8,128)S(1)} %pad_maximum_fusion.17), channel_id=1, source_target_pairs={{0,1},{1,0},{2,3},{3,2},{4,5},{5,4},{6,7},{7,6},{8,9},{9,8},{10,11... | collective-permute-start | bytes 110600 | tf_op jit(solution)/shard_map/ppermute | solution.py:251
  171.5 5.4 %assemble.1 = bf16[2,1152,1152]{2,1,0:T(8,128)(2,1)} custom-call(s32[1]{0:T(128)} %bitcast.core_ref, bf16[4,2,152,1152]{3,2,1,0:T(8,128)(2,1)} %lineup.1.mine_ref, bf16[4,2,152,1152]{3,2,1,0:T(8,128)(2,1)} %collective-permute-done.3.theirs_ref), custom_call_target="tpu_custom_call" | custom-call | tf_op jit(solution)/shard_map/assemble/pallas_call | solution.py:192
  176.8 1.5 collective-permute-start.27
  178.7 1.4 collective-permute-start.25
  180.1 5.9 %collective-permute-done.27.refs_3_ = bf16[32,2176]{1,0:T(8,128)(2,1)S(1)} collective-permute-done((bf16[32,2176]{1,0:T(8,128)(2,1)S(1)}, bf16[32,2176]{1,0:T(8,128)(2,1)S(1)}, u32[]{:S(2)}, u32[]{:S(2)}) %collective-permute-start.27) | collective-permute-done | bytes 139296 | tf_op jit(solution)/shard_map/ppermute | solution.py:254
  186.8 2.1 %shard_map.121 = (f32[32,1152]{1,0:T(8,128)S(1)}, f32[32,32]{1,0:T(8,128)S(1)}) custom-call(bf16[32,2176]{1,0:T(8,128)(2,1)S(1)} %get-tuple-element.21.refs_0_, bf16[32,2176]{1,0:T(8,128)(2,1)S(1)} %collective-permute-done.25.refs_1_, bf16[32,2176]{1,0:T(8,128)(2,1)S(1)} %collective-permute-done.26.refs_2_, bf16[32,2176]{1,0:T(8,128)(2,1)S(1)} %collective-permute-done.27.refs_3_), custom_call_target="tpu_custom_call" | custom-call | tf_op jit(solution)/shard_map/pallas_call | solution.py:210
  189.3 1.5 collective-permute-start.28
  193.7 2.2 %multiply_add_fusion = (f32[2,144,1152]{2,1,0:T(8,128)}, f32[1,2,144,1152]{3,2,1,0:T(8,128)}) fusion(f32[2,144,1152]{2,1,0:T(8,128)S(1)} %copy-done.2, f32[1,144,1152]{2,1,0:T(8,128)S(1)} %fusion.17, f32[1,144,1152]{2,1,0:T(8,128)S(1)} %bitcast.137, bf16[2,192,1152]{2,1,0:T(8,128)(2,1)S(1)} %constant_dynamic-update-slice_fusion.5, ...), kind=kOutput, calls=%fused_computation.22 | convolution fusion | flops 129060864 | bytes 6389764 | tf_op jit(solution)/shard_map/lkr,lke->lre/dot_general | solution.py:382
  195.9 4.2 %subtract_convert_fusion = bf16[2,1152,1152]{2,1,0:T(8,128)(2,1)} fusion(bf16[2,1152,1152]{2,1,0:T(8,128)(2,1)S(1)} %bitcast.134, bf16[2,192,1152]{2,1,0:T(8,128)(2,1)S(1)} %fusion.41, bf16[2,192,1152]{2,1,0:T(8,128)(2,1)S(1)} %constant_dynamic-update-slice_fusion.5), kind=kOutput, calls=%fused_computation.2 | convolution fusion | flops 1029832704 | bytes 12386304 | tf_op jit(solution)/shard_map/lkr,lke->lre/dot_general | solution.py:385
  (114 shorter events, 12.5 us)
Async XLA Ops:
  0.6 102.6 %copy-start = (f32[2,1152,32]{1,2,0:T(8,128)S(1)}, f32[2,1152,32]{1,2,0:T(8,128)}, u32[]{:S(2)}) copy-start(f32[2,1152,32]{1,2,0:T(8,128)} %param.15) | copy-start | bytes 884740
  12.3 3.2 %copy-start.7 = (f32[2,144]{1,0:T(2,128)S(1)}, f32[2,144]{1,0:T(2,128)}, u32[]{:S(2)}) copy-start(f32[2,144]{1,0:T(2,128)} %param.14) | copy-start | bytes 3460
  12.3 3.2 %copy-start.9 = (bf16[2,144]{1,0:T(2,128)(2,1)S(1)}, bf16[2,144]{1,0:T(2,128)(2,1)}, u32[]{:S(2)}) copy-start(bf16[2,144]{1,0:T(2,128)(2,1)} %param.11) | copy-start | bytes 1732
  12.3 3.2 %copy-start.1 = (f32[2,144,1152]{2,1,0:T(8,128)S(1)}, f32[2,144,1152]{2,1,0:T(8,128)}, u32[]{:S(2)}) copy-start(f32[2,144,1152]{2,1,0:T(8,128)} %param.13) | copy-start | bytes 3981316
  13.8 4.5 %collective-permute-start.4 = (bf16[4,144,1152]{2,1,0:T(8,128)(2,1)S(1)}, bf16[4,144,1152]{2,1,0:T(8,128)(2,1)}, u32[]{:S(2)}, u32[]{:S(2)}) collective-permute-start(bf16[4,144,1152]{2,1,0:T(8,128)(2,1)S(1)} %dynamic-slice_bitcast_fusion.1), channel_id=1, source_target_pairs={{0,1},{1,0},{2,3},{3,2},{4,5},{5,4},{6,7},{7,6},{8,9},{9,8},{10,11... | collective-permute-start | bytes 3981320 | tf_op jit(solution)/shard_map/ppermute | solution.py:251
  20.9 14.6 %slice-start.2 = ((s8[9437184]{0:T(1024)(128)(4,1)}), s8[4194304]{0:T(1024)(128)(4,1)S(1)}, s32[]{:S(2)}) async-start(s8[9437184]{0:T(1024)(128)(4,1)} %bitcast.138), calls=%async_computation.2 | async-start | bytes 8388608
  20.9 14.6 %slice-start.3 = ((s8[9437184]{0:T(1024)(128)(4,1)}), s8[4194304]{0:T(1024)(128)(4,1)S(1)}, s32[]{:S(2)}) async-start(s8[9437184]{0:T(1024)(128)(4,1)} %bitcast.138), calls=%async_computation.3 | async-start | bytes 8388608
  20.9 14.6 %slice-start.4 = ((s8[9437184]{0:T(1024)(128)(4,1)}), s8[1048576]{0:T(1024)(128)(4,1)S(1)}, s32[]{:S(2)}) async-start(s8[9437184]{0:T(1024)(128)(4,1)} %bitcast.138), calls=%async_computation.4 | async-start | bytes 2097152
  31.1 1.5 copy-start.4
  31.3 8.9 %collective-permute-start.8 = (bf16[4,144,1152]{2,1,0:T(8,128)(2,1)S(1)}, bf16[4,144,1152]{2,1,0:T(8,128)(2,1)}, u32[]{:S(2)}, u32[]{:S(2)}) collective-permute-start(bf16[4,144,1152]{2,1,0:T(8,128)(2,1)S(1)} %dynamic-slice_bitcast_fusion), channel_id=1, source_target_pairs={{0,1},{1,0},{2,3},{3,2},{4,5},{5,4},{6,7},{7,6},{8,9},{9,8},{10,11... | collective-permute-start | bytes 3981320 | tf_op jit(solution)/shard_map/ppermute | solution.py:251
  32.6 56.1 %copy-start.3 = (bf16[2,152,1152]{2,1,0:T(8,128)(2,1)}, bf16[2,152,1152]{2,1,0:T(8,128)(2,1)S(1)}, u32[]{:S(2)}) copy-start(bf16[2,152,1152]{2,1,0:T(8,128)(2,1)S(1)} %pad_maximum_fusion.2.refs_0_) | copy-start | bytes 2101252
  32.6 70.6 %collective-permute-start.2 = (bf16[2,152,1152]{2,1,0:T(8,128)(2,1)S(1)}, bf16[2,152,1152]{2,1,0:T(8,128)(2,1)S(1)}, u32[]{:S(2)}, u32[]{:S(2)}) collective-permute-start(bf16[2,152,1152]{2,1,0:T(8,128)(2,1)S(1)} %pad_maximum_fusion.2.refs_0_), channel_id=1, source_target_pairs={{0,6},{2,4},{4,2},{6,0},{1,7},{3,5},{5,3},{7,1},{8,14},{10,12},{12... | collective-permute-start | bytes 2101256 | tf_op jit(solution)/shard_map/ppermute | solution.py:254
  36.8 43.6 %collective-permute-start.7 = (bf16[144,1152]{1,0:T(8,128)(2,1)}, bf16[144,1152]{1,0:T(8,128)(2,1)}, u32[]{:S(2)}, u32[]{:S(2)}) collective-permute-start(bf16[144,1152]{1,0:T(8,128)(2,1)} %get-tuple-element.32), channel_id=1, source_target_pairs={{0,6},{2,4},{4,2},{6,0},{1,7},{3,5},{5,3},{7,1},{8,14},{10,12},{12... | collective-permute-start | bytes 995336 | tf_op jit(solution)/shard_map/ppermute | solution.py:254
  36.9 43.5 %collective-permute-start.6 = (bf16[144,1152]{1,0:T(8,128)(2,1)}, bf16[144,1152]{1,0:T(8,128)(2,1)}, u32[]{:S(2)}, u32[]{:S(2)}) collective-permute-start(bf16[144,1152]{1,0:T(8,128)(2,1)} %get-tuple-element.33), channel_id=1, source_target_pairs={{0,4},{2,6},{4,0},{6,2},{1,5},{3,7},{5,1},{7,3},{8,12},{10,14},{12... | collective-permute-start | bytes 995336 | tf_op jit(solution)/shard_map/ppermute | solution.py:254
  38.5 44.4 %collective-permute-start.5 = (bf16[144,1152]{1,0:T(8,128)(2,1)S(1)}, bf16[144,1152]{1,0:T(8,128)(2,1)}, u32[]{:S(2)}, u32[]{:S(2)}) collective-permute-start(bf16[144,1152]{1,0:T(8,128)(2,1)S(1)} %get-tuple-element.34), channel_id=1, source_target_pairs={{0,2},{2,0},{4,6},{6,4},{1,3},{3,1},{5,7},{7,5},{8,10},{10,8},{12,... | collective-permute-start | bytes 995336 | tf_op jit(solution)/shard_map/ppermute | solution.py:254
  40.2 63.1 %collective-permute-start.1 = (bf16[2,152,1152]{2,1,0:T(8,128)(2,1)S(1)}, bf16[2,152,1152]{2,1,0:T(8,128)(2,1)}, u32[]{:S(2)}, u32[]{:S(2)}) collective-permute-start(bf16[2,152,1152]{2,1,0:T(8,128)(2,1)S(1)} %pad_maximum_fusion.2.refs_0_), channel_id=1, source_target_pairs={{0,4},{2,6},{4,0},{6,2},{1,5},{3,7},{5,1},{7,3},{8,12},{10,14},{12... | collective-permute-start | bytes 2101256 | tf_op jit(solution)/shard_map/ppermute | solution.py:254
  40.9 43.3 %copy-start.5 = (f32[1,2,144,1152]{3,2,1,0:T(8,128)S(1)}, f32[1,2,144,1152]{3,2,1,0:T(8,128)}, u32[]{:S(2)}) copy-start(f32[1,2,144,1152]{3,2,1,0:T(8,128)} %param.12) | copy-start | bytes 3981316
  80.4 8.3 %collective-permute-start.9 = (bf16[144,1152]{1,0:T(8,128)(2,1)S(1)}, bf16[144,1152]{1,0:T(8,128)(2,1)S(1)}, u32[]{:S(2)}, u32[]{:S(2)}) collective-permute-start(bf16[144,1152]{1,0:T(8,128)(2,1)S(1)} %get-tuple-element.29), channel_id=1, source_target_pairs={{0,2},{2,0},{4,6},{6,4},{1,3},{3,1},{5,7},{7,5},{8,10},{10,8},{12,... | collective-permute-start | bytes 995336 | tf_op jit(solution)/shard_map/ppermute | solution.py:254
  80.4 9.2 %collective-permute-start.11 = (bf16[144,1152]{1,0:T(8,128)(2,1)S(1)}, bf16[144,1152]{1,0:T(8,128)(2,1)S(1)}, u32[]{:S(2)}, u32[]{:S(2)}) collective-permute-start(bf16[144,1152]{1,0:T(8,128)(2,1)S(1)} %get-tuple-element.30), channel_id=1, source_target_pairs={{0,6},{2,4},{4,2},{6,0},{1,7},{3,5},{5,3},{7,1},{8,14},{10,12},{12... | collective-permute-start | bytes 995336 | tf_op jit(solution)/shard_map/ppermute | solution.py:254
  82.9 14.9 %collective-permute-start.10 = (bf16[144,1152]{1,0:T(8,128)(2,1)S(1)}, bf16[144,1152]{1,0:T(8,128)(2,1)S(1)}, u32[]{:S(2)}, u32[]{:S(2)}) collective-permute-start(bf16[144,1152]{1,0:T(8,128)(2,1)S(1)} %get-tuple-element.31), channel_id=1, source_target_pairs={{0,4},{2,6},{4,0},{6,2},{1,5},{3,7},{5,1},{7,3},{8,12},{10,14},{12... | collective-permute-start | bytes 995336 | tf_op jit(solution)/shard_map/ppermute | solution.py:254
  88.7 22.3 %collective-permute-start = (bf16[2,152,1152]{2,1,0:T(8,128)(2,1)S(1)}, bf16[2,152,1152]{2,1,0:T(8,128)(2,1)}, u32[]{:S(2)}, u32[]{:S(2)}) collective-permute-start(bf16[2,152,1152]{2,1,0:T(8,128)(2,1)S(1)} %pad_maximum_fusion.2.refs_0_), channel_id=1, source_target_pairs={{0,2},{2,0},{4,6},{6,4},{1,3},{3,1},{5,7},{7,5},{8,10},{10,8},{12,... | collective-permute-start | bytes 2101256 | tf_op jit(solution)/shard_map/ppermute | solution.py:254
  99.4 17.2 %collective-permute-start.12 = (bf16[152,1152]{1,0:T(8,128)(2,1)S(1)}, bf16[152,1152]{1,0:T(8,128)(2,1)}, u32[]{:S(2)}, u32[]{:S(2)}) collective-permute-start(bf16[152,1152]{1,0:T(8,128)(2,1)S(1)} %pad_maximum_fusion.7), channel_id=1, source_target_pairs={{0,1},{1,0},{2,3},{3,2},{4,5},{5,4},{6,7},{7,6},{8,9},{9,8},{10,11... | collective-permute-start | bytes 1050632 | tf_op jit(solution)/shard_map/ppermute | solution.py:251
  103.3 7.7 %copy-start.6 = (bf16[2,152,1152]{2,1,0:T(8,128)(2,1)}, bf16[2,152,1152]{2,1,0:T(8,128)(2,1)S(1)}, u32[]{:S(2)}) copy-start(bf16[2,152,1152]{2,1,0:T(8,128)(2,1)S(1)} %collective-permute-done.2.refs_3_) | copy-start | bytes 2101252
  114.7 56.7 %collective-permute-start.3 = (bf16[4,2,152,1152]{3,2,1,0:T(8,128)(2,1)}, bf16[4,2,152,1152]{3,2,1,0:T(8,128)(2,1)}, u32[]{:S(2)}, u32[]{:S(2)}) collective-permute-start(bf16[4,2,152,1152]{3,2,1,0:T(8,128)(2,1)} %lineup.1.mine_ref), channel_id=1, source_target_pairs={{0,1},{1,0},{2,3},{3,2},{4,5},{5,4},{6,7},{7,6},{8,9},{9,8},{10,11... | collective-permute-start | bytes 8405000 | tf_op jit(solution)/shard_map/ppermute | solution.py:251
  118.9 7.8 %collective-permute-start.13 = (bf16[80,1152]{1,0:T(8,128)(2,1)S(1)}, bf16[80,1152]{1,0:T(8,128)(2,1)S(1)}, u32[]{:S(2)}, u32[]{:S(2)}) collective-permute-start(bf16[80,1152]{1,0:T(8,128)(2,1)S(1)} %get-tuple-element.54), channel_id=1, source_target_pairs={{0,64},{32,96},{64,0},{96,32},{1,65},{33,97},{65,1},{97,33},{2,66}... | collective-permute-start | bytes 552968 | tf_op jit(solution)/shard_map/ppermute | solution.py:257
  121.6 9.4 %collective-permute-start.14 = (bf16[80,1152]{1,0:T(8,128)(2,1)S(1)}, bf16[80,1152]{1,0:T(8,128)(2,1)S(1)}, u32[]{:S(2)}, u32[]{:S(2)}) collective-permute-start(bf16[80,1152]{1,0:T(8,128)(2,1)S(1)} %get-tuple-element.55), channel_id=1, source_target_pairs={{0,32},{32,64},{64,96},{96,0},{1,33},{33,65},{65,97},{97,1},{2,34}... | collective-permute-start | bytes 552968 | tf_op jit(solution)/shard_map/ppermute | solution.py:257
  121.9 9.1 %collective-permute-start.15 = (bf16[80,1152]{1,0:T(8,128)(2,1)S(1)}, bf16[80,1152]{1,0:T(8,128)(2,1)S(1)}, u32[]{:S(2)}, u32[]{:S(2)}) collective-permute-start(bf16[80,1152]{1,0:T(8,128)(2,1)S(1)} %get-tuple-element.56), channel_id=1, source_target_pairs={{0,96},{32,0},{64,32},{96,64},{1,97},{33,1},{65,33},{97,65},{2,98}... | collective-permute-start | bytes 552968 | tf_op jit(solution)/shard_map/ppermute | solution.py:257
  131.2 7.2 %collective-permute-start.18 = (bf16[80,1152]{1,0:T(8,128)(2,1)S(1)}, bf16[80,1152]{1,0:T(8,128)(2,1)S(1)}, u32[]{:S(2)}, u32[]{:S(2)}) collective-permute-start(bf16[80,1152]{1,0:T(8,128)(2,1)S(1)} %pad_maximum_fusion.3), channel_id=1, source_target_pairs={{0,24},{8,0},{16,8},{24,16},{1,25},{9,1},{17,9},{25,17},{2,26},{10... | collective-permute-start | bytes 552968 | tf_op jit(solution)/shard_map/ppermute | solution.py:257
  134.9 7.9 %collective-permute-start.17 = (bf16[80,1152]{1,0:T(8,128)(2,1)S(1)}, bf16[80,1152]{1,0:T(8,128)(2,1)S(1)}, u32[]{:S(2)}, u32[]{:S(2)}) collective-permute-start(bf16[80,1152]{1,0:T(8,128)(2,1)S(1)} %pad_maximum_fusion.3), channel_id=1, source_target_pairs={{0,8},{8,16},{16,24},{24,0},{1,9},{9,17},{17,25},{25,1},{2,10},{10... | collective-permute-start | bytes 552968 | tf_op jit(solution)/shard_map/ppermute | solution.py:257
  134.9 9.2 %collective-permute-start.16 = (bf16[80,1152]{1,0:T(8,128)(2,1)S(1)}, bf16[80,1152]{1,0:T(8,128)(2,1)S(1)}, u32[]{:S(2)}, u32[]{:S(2)}) collective-permute-start(bf16[80,1152]{1,0:T(8,128)(2,1)S(1)} %pad_maximum_fusion.3), channel_id=1, source_target_pairs={{0,16},{8,24},{16,0},{24,8},{1,17},{9,25},{17,1},{25,9},{2,18},{10... | collective-permute-start | bytes 552968 | tf_op jit(solution)/shard_map/ppermute | solution.py:257
  144.2 10.9 %collective-permute-start.21 = (bf16[72,1152]{1,0:T(8,128)(2,1)S(1)}, bf16[72,1152]{1,0:T(8,128)(2,1)S(1)}, u32[]{:S(2)}, u32[]{:S(2)}) collective-permute-start(bf16[72,1152]{1,0:T(8,128)(2,1)S(1)} %add_convert_fusion.6.refs_0_), channel_id=1, source_target_pairs={{0,96},{32,64},{64,32},{96,0},{1,97},{33,65},{65,33},{97,1},{2,98}... | collective-permute-start | bytes 497672 | tf_op jit(solution)/shard_map/ppermute | solution.py:254
  148.1 7.0 %collective-permute-start.20 = (bf16[72,1152]{1,0:T(8,128)(2,1)S(1)}, bf16[72,1152]{1,0:T(8,128)(2,1)S(1)}, u32[]{:S(2)}, u32[]{:S(2)}) collective-permute-start(bf16[72,1152]{1,0:T(8,128)(2,1)S(1)} %add_convert_fusion.6.refs_0_), channel_id=1, source_target_pairs={{0,64},{32,96},{64,0},{96,32},{1,65},{33,97},{65,1},{97,33},{2,66}... | collective-permute-start | bytes 497672 | tf_op jit(solution)/shard_map/ppermute | solution.py:254
  148.1 7.0 %collective-permute-start.19 = (bf16[72,1152]{1,0:T(8,128)(2,1)S(1)}, bf16[72,1152]{1,0:T(8,128)(2,1)S(1)}, u32[]{:S(2)}, u32[]{:S(2)}) collective-permute-start(bf16[72,1152]{1,0:T(8,128)(2,1)S(1)} %add_convert_fusion.6.refs_0_), channel_id=1, source_target_pairs={{0,32},{32,0},{64,96},{96,64},{1,33},{33,1},{65,97},{97,65},{2,34}... | collective-permute-start | bytes 497672 | tf_op jit(solution)/shard_map/ppermute | solution.py:254
  156.0 5.6 %collective-permute-start.24 = (bf16[40,1408]{1,0:T(8,128)(2,1)S(1)}, bf16[40,1408]{1,0:T(8,128)(2,1)S(1)}, u32[]{:S(2)}, u32[]{:S(2)}) collective-permute-start(bf16[40,1408]{1,0:T(8,128)(2,1)S(1)} %get-tuple-element.19.refs_0_), channel_id=1, source_target_pairs={{0,6},{2,4},{4,2},{6,0},{1,7},{3,5},{5,3},{7,1},{8,14},{10,12},{12... | collective-permute-start | bytes 337928 | tf_op jit(solution)/shard_map/ppermute | solution.py:254
  158.6 5.2 %collective-permute-start.23 = (bf16[40,1408]{1,0:T(8,128)(2,1)S(1)}, bf16[40,1408]{1,0:T(8,128)(2,1)S(1)}, u32[]{:S(2)}, u32[]{:S(2)}) collective-permute-start(bf16[40,1408]{1,0:T(8,128)(2,1)S(1)} %get-tuple-element.19.refs_0_), channel_id=1, source_target_pairs={{0,4},{2,6},{4,0},{6,2},{1,5},{3,7},{5,1},{7,3},{8,12},{10,14},{12... | collective-permute-start | bytes 337928 | tf_op jit(solution)/shard_map/ppermute | solution.py:254
  158.6 5.2 %collective-permute-start.22 = (bf16[40,1408]{1,0:T(8,128)(2,1)S(1)}, bf16[40,1408]{1,0:T(8,128)(2,1)S(1)}, u32[]{:S(2)}, u32[]{:S(2)}) collective-permute-start(bf16[40,1408]{1,0:T(8,128)(2,1)S(1)} %get-tuple-element.19.refs_0_), channel_id=1, source_target_pairs={{0,2},{2,0},{4,6},{6,4},{1,3},{3,1},{5,7},{7,5},{8,10},{10,8},{12,... | collective-permute-start | bytes 337928 | tf_op jit(solution)/shard_map/ppermute | solution.py:254
  167.0 13.1 %collective-permute-start.29 = (f32[8,1152]{1,0:T(8,128)S(1)}, f32[8,1152]{1,0:T(8,128)S(1)}, u32[]{:S(2)}, u32[]{:S(2)}) collective-permute-start(f32[8,1152]{1,0:T(8,128)S(1)} %pad_maximum_fusion.17), channel_id=1, source_target_pairs={{0,1},{1,0},{2,3},{3,2},{4,5},{5,4},{6,7},{7,6},{8,9},{9,8},{10,11... | collective-permute-start | bytes 110600 | tf_op jit(solution)/shard_map/ppermute | solution.py:251
  176.8 14.6 %copy-start.8 = (f32[2,144]{1,0:T(2,128)S(1)}, f32[2,144]{1,0:T(2,128)}, u32[]{:S(2)}) copy-start(f32[2,144]{1,0:T(2,128)} %param.14) | copy-start | bytes 3460
  176.8 9.2 %collective-permute-start.27 = (bf16[32,2176]{1,0:T(8,128)(2,1)S(1)}, bf16[32,2176]{1,0:T(8,128)(2,1)S(1)}, u32[]{:S(2)}, u32[]{:S(2)}) collective-permute-start(bf16[32,2176]{1,0:T(8,128)(2,1)S(1)} %get-tuple-element.21.refs_0_), channel_id=1, source_target_pairs={{0,6},{2,4},{4,2},{6,0},{1,7},{3,5},{5,3},{7,1},{8,14},{10,12},{12... | collective-permute-start | bytes 417800 | tf_op jit(solution)/shard_map/ppermute | solution.py:254
  178.3 7.7 %collective-permute-start.26 = (bf16[32,2176]{1,0:T(8,128)(2,1)S(1)}, bf16[32,2176]{1,0:T(8,128)(2,1)S(1)}, u32[]{:S(2)}, u32[]{:S(2)}) collective-permute-start(bf16[32,2176]{1,0:T(8,128)(2,1)S(1)} %get-tuple-element.21.refs_0_), channel_id=1, source_target_pairs={{0,4},{2,6},{4,0},{6,2},{1,5},{3,7},{5,1},{7,3},{8,12},{10,14},{12... | collective-permute-start | bytes 417800 | tf_op jit(solution)/shard_map/ppermute | solution.py:254
  178.7 7.9 %collective-permute-start.25 = (bf16[32,2176]{1,0:T(8,128)(2,1)S(1)}, bf16[32,2176]{1,0:T(8,128)(2,1)S(1)}, u32[]{:S(2)}, u32[]{:S(2)}) collective-permute-start(bf16[32,2176]{1,0:T(8,128)(2,1)S(1)} %get-tuple-element.21.refs_0_), channel_id=1, source_target_pairs={{0,2},{2,0},{4,6},{6,4},{1,3},{3,1},{5,7},{7,5},{8,10},{10,8},{12,... | collective-permute-start | bytes 417800 | tf_op jit(solution)/shard_map/ppermute | solution.py:254
  189.2 6.7 %slice-start = ((s8[5308416]{0:T(1024)(128)(4,1)}), s8[4194304]{0:T(1024)(128)(4,1)S(1)}, s32[]{:S(2)}) async-start(s8[5308416]{0:T(1024)(128)(4,1)} %bitcast.133), calls=%async_computation | async-start | bytes 8388608
  189.3 2.8 %collective-permute-start.28 = (f32[32,2304]{1,0:T(8,128)S(1)}, f32[32,2304]{1,0:T(8,128)S(1)}, u32[]{:S(2)}, u32[]{:S(2)}) collective-permute-start(f32[32,2304]{1,0:T(8,128)S(1)} %pad_maximum_fusion.14), channel_id=1, source_target_pairs={{0,1},{1,0},{2,3},{3,2},{4,5},{5,4},{6,7},{7,6},{8,9},{9,8},{10,11... | collective-permute-start | bytes 884744 | tf_op jit(solution)/shard_map/ppermute | solution.py:251
  192.4 1.3 copy-start.2
  192.5 3.4 %slice-start.1 = ((s8[5308416]{0:T(1024)(128)(4,1)}), s8[1114112]{0:T(1024)(128)(4,1)S(1)}, s32[]{:S(2)}) async-start(s8[5308416]{0:T(1024)(128)(4,1)} %bitcast.133), calls=%async_computation.1 | async-start | bytes 2228224
